TPU v7x, 512 devices: a whole 4x8x8 slice. The times are simulated.
512 devices in a mesh: zg: 8 (over x, core), xy: 64 (over y, z).
Axes of the slice: x: 4, y: 8, z: 8, core: 2. Of those that a mesh axis runs over, the one named last changes fastest.
Arguments:
- source: float32 [64, 2048, 128], P('zg', 'xy'), may hold values from -4 to 4
- conductivity: float32 [64, 2048, 128], P('zg', 'xy'), may hold values from 0.5 to 4
- fluid: int32 [64, 2048, 128], P('zg', 'xy'), may hold values from 0 to 1, as said below
- pressure: float32 [64, 2048, 128], P('zg', 'xy'), may hold values from -6 to 6
Outputs:
- relaxed: float32 [64, 2048, 128], P('zg', 'xy')
- coarse: float32 [32, 1024, 64], P('zg', 'xy')
Inputs may be any that keep to these rules, and one draw needn't show every extreme that they name: `fluid`: the solid cells of a column, if any, are its lowest ones.
All inputs are finite; a program needn't handle non-finite values.
Results may differ from a plain program's by a relative error of at most 0.000049.
Values sent between devices are 32-bit elements; how exact they have to be, the bound alone decides.
No kernel may reach another device: no remote copies, remote signals or barrier semaphores. Data moves between devices by JAX's collectives and lax.ppermute only.
A program may use at most 64 MiB of HBM per device.

v0:
```python
import jax
import jax.numpy as jnp
from jax import lax
from jax.sharding import Mesh
from jax.sharding import PartitionSpec as P

ZG = ("zg_0", "zg_1")


vertical_ratio = 100.0
absorption = 0.05


def shifted(block, axis, distance):
    devices = range(lax.axis_size(axis))
    route = [(i - distance, i) for i in devices if i - distance in devices]
    return lax.ppermute(block, axis, route)


def in_order(pieces, dim):
    pieces = jnp.moveaxis(pieces, 0, dim)
    dims = pieces.shape
    return pieces.reshape(*dims[:dim], dims[dim] * dims[dim + 1], *dims[dim + 2 :])


def stacked_from(array, axes, sequence):
    pieces = array[None]
    for k in sequence:
        pieces = lax.all_gather(pieces, axes[k], axis=0, tiled=True)
    current = [lax.axis_size(axes[k]) for k in reversed(sequence)]
    pieces = pieces.reshape(*current, *array.shape)
    turned = sorted(range(len(sequence)), key=lambda place: sequence[len(sequence) - 1 - place])
    return pieces.transpose(*turned, *range(len(sequence), pieces.ndim)).reshape(-1, *array.shape)


def gathered_by_axis(array, axes, sequence, dim):
    return in_order(stacked_from(array, axes, sequence), dim)


def extended(cells, sides, width):
    for axis, dim in sides:
        count = lax.axis_size(axis)
        ends = count - 1
        head = lax.slice_in_dim(cells, 0, width, axis=dim)
        tail = lax.slice_in_dim(cells, cells.shape[dim] - width, cells.shape[dim], axis=dim)
        cells = jnp.concatenate(
            [
                lax.ppermute(tail, axis, [(i, (i + 1) % count) for i in range(ends)]),
                cells,
                lax.ppermute(head, axis, [((i + 1) % count, i) for i in range(ends)]),
            ],
            axis=dim,
        )
    return cells


def thomas(lower_coef, diagonal, upper_coef, right_side):

    def forward(carried, level_row):
        ratio_prev, value_prev = carried
        sub_coef, mid_coef, sup_coef, src_term = level_row
        pivots = mid_coef - sub_coef * ratio_prev
        ratio_now = sup_coef / pivots
        value_now = (src_term - sub_coef[None] * value_prev) / pivots[None]
        return ((ratio_now, value_now), (ratio_now, value_now))

    initial = (jnp.zeros_like(diagonal[0]), jnp.zeros_like(right_side[0]))
    unused, (ratios, values) = lax.scan(
        forward, initial, (lower_coef, diagonal, upper_coef, right_side)
    )

    def backward(carried, level_row):
        ratio_now, value_now = level_row
        result = value_now - ratio_now[None] * carried
        return (result, result)

    unused_end, solved = lax.scan(
        backward, jnp.zeros_like(right_side[0]), (ratios, values), reverse=True
    )
    return solved


def faces(weighted, padded):
    face_below = vertical_ratio * jnp.sqrt(weighted * padded[:-2, 1:-1, 1:-1])
    face_above = vertical_ratio * jnp.sqrt(weighted * padded[2:, 1:-1, 1:-1])
    face_west = jnp.sqrt(weighted * padded[1:-1, :-2, 1:-1])
    face_east = jnp.sqrt(weighted * padded[1:-1, 2:, 1:-1])
    face_south = jnp.sqrt(weighted * padded[1:-1, 1:-1, :-2])
    face_north = jnp.sqrt(weighted * padded[1:-1, 1:-1, 2:])
    return (face_below, face_above, face_west, face_east, face_south, face_north)


def horizontal(coefs, padded):
    return (
        coefs[2] * padded[:, :-2, 1:-1]
        + coefs[3] * padded[:, 2:, 1:-1]
        + coefs[4] * padded[:, 1:-1, :-2]
        + coefs[5] * padded[:, 1:-1, 2:]
    )


def restrict_axis(values, dimension):
    length = values.shape[dimension] - 2
    pieces = [
        lax.slice_in_dim(values, offset, offset + length - 1, 2, dimension) for offset in range(4)
    ]
    return 0.125 * (pieces[0] + 3.0 * pieces[1] + 3.0 * pieces[2] + pieces[3])


def restrict(padded):
    for dimension in range(3):
        padded = restrict_axis(padded, dimension)
    return padded


def pad_side(values):
    return jnp.pad(values, ((0, 0), (0, 0), (1, 1)))


def select_colour(values, colour):
    levels, across, along = values.shape
    blocks = values.reshape(levels, across // 2, 2, along // 2, 2)
    return jnp.concatenate([blocks[:, :, 0, :, colour], blocks[:, :, 1, :, 1 - colour]], axis=-1)


def insert_colour(values, compact, colour):
    levels, across, along = values.shape
    half_len = along // 2
    even_new = compact[..., :half_len]
    odd_new = compact[..., half_len:]
    blocks = values.reshape(levels, across // 2, 2, along // 2, 2)
    if colour == 0:
        row_even = jnp.stack([even_new, blocks[:, :, 0, :, 1]], axis=-1)
        row_odd = jnp.stack([blocks[:, :, 1, :, 0], odd_new], axis=-1)
    else:
        row_even = jnp.stack([blocks[:, :, 0, :, 0], even_new], axis=-1)
        row_odd = jnp.stack([odd_new, blocks[:, :, 1, :, 1]], axis=-1)
    return jnp.stack([row_even, row_odd], axis=2).reshape(levels, across, along)


def line_solve(lower_coef, diagonal, upper_coef, right_side):
    interior = lower_coef.shape[0] - 1
    zero_rows = jnp.zeros_like(right_side[: interior - 1])
    from_below = jnp.concatenate([-lower_coef[:1], zero_rows], axis=0)
    from_above = jnp.concatenate([zero_rows, -upper_coef[interior - 1 : interior]], axis=0)
    stacked = jnp.stack([right_side[:interior], from_below, from_above], axis=1)
    solved = thomas(lower_coef[:interior], diagonal[:interior], upper_coef[:interior], stacked)
    particular = solved[:, 0]
    lower_part = solved[:, 1]
    upper_part = solved[:, 2]
    lowest = jnp.stack([particular[0], lower_part[0], upper_part[0]])
    next_low = shifted(lowest, ZG, -1)
    sub_sep = lower_coef[interior]
    sup_sep = upper_coef[interior]
    red_lower = sub_sep * lower_part[interior - 1]
    red_diag = diagonal[interior] + sub_sep * upper_part[interior - 1] + sup_sep * next_low[1]
    red_upper = sup_sep * next_low[2]
    red_right = right_side[interior] - sub_sep * particular[interior - 1] - sup_sep * next_low[0]
    rows_all = gathered_by_axis(
        jnp.stack([red_lower, red_diag, red_upper, red_right])[None], ("zg_0", "zg_1"), (0, 1), 0
    )
    groups = rows_all.shape[0]
    ratio_prev = jnp.zeros_like(red_diag)
    value_prev = jnp.zeros_like(red_diag)
    ratio_list = []
    value_list = []
    for member in range(groups):
        pivots = rows_all[member, 1] - rows_all[member, 0] * ratio_prev
        ratio_prev = rows_all[member, 2] / pivots
        value_prev = (rows_all[member, 3] - rows_all[member, 0] * value_prev) / pivots
        ratio_list.append(ratio_prev)
        value_list.append(value_prev)
    follow = jnp.zeros_like(red_diag)
    sep_list = [None] * groups
    for member in range(groups - 1, -1, -1):
        follow = value_list[member] - ratio_list[member] * follow
        sep_list[member] = follow
    separators = jnp.stack(sep_list)
    position = lax.axis_index(ZG)
    sep_here = lax.dynamic_index_in_dim(separators, position, 0, keepdims=False)
    below_pick = lax.dynamic_index_in_dim(
        separators, jnp.maximum(position - 1, 0), 0, keepdims=False
    )
    sep_below = jnp.where(position > 0, below_pick, jnp.zeros_like(below_pick))
    inner = particular + sep_below[None] * lower_part + sep_here[None] * upper_part
    return jnp.concatenate([inner, sep_here[None]], axis=0)


def shards(source, conductivity, fluid, pressure):
    fluid_real = fluid.astype(jnp.float32)
    weighted = conductivity * fluid_real
    rimmed = extended(weighted, ((ZG, 0), ("xy", 1)), 1)
    coefs = faces(weighted, pad_side(rimmed))
    diagonal = fluid_real * (
        absorption + coefs[0] + coefs[1] + coefs[2] + coefs[3] + coefs[4] + coefs[5]
    ) + (1.0 - fluid_real)
    forcing = fluid_real * source
    lower_coef = -coefs[0]
    upper_coef = -coefs[1]
    for colour in (0, 1):
        beside = extended(pressure, (("xy", 1),), 1)
        right_side = forcing + horizontal(coefs, pad_side(beside))
        solved = line_solve(
            select_colour(lower_coef, colour),
            select_colour(diagonal, colour),
            select_colour(upper_coef, colour),
            select_colour(right_side, colour),
        )
        pressure = insert_colour(pressure, solved, colour)
    full = pad_side(extended(pressure, ((ZG, 0), ("xy", 1)), 1))
    applied = diagonal * pressure - (
        horizontal(coefs, full[1:-1])
        + coefs[0] * full[:-2, 1:-1, 1:-1]
        + coefs[1] * full[2:, 1:-1, 1:-1]
    )
    residual = forcing - applied
    rimmed_res = extended(residual, ((ZG, 0), ("xy", 1)), 1)
    coarse = restrict(pad_side(rimmed_res))
    return (pressure, coarse)


def solution(mesh):
    finer = Mesh(mesh.devices.reshape(4, 2, mesh.shape["xy"]), ("zg_0", "zg_1", "xy"))
    in_specs = (P(ZG, "xy", None), P(ZG, "xy", None), P(ZG, "xy", None), P(ZG, "xy", None))
    out_specs = (P(ZG, "xy", None), P(ZG, "xy", None))
    return jax.shard_map(
        shards, mesh=finer, in_specs=in_specs, out_specs=out_specs, check_vma=False
    )
```

profile of v0, /device:TPU:33, one launch (start us, length us, event | category | flops | bytes accessed | tf_op | source)
XLA Modules:
  0.0 186.2 jit_solution(15149730447677153103)
XLA Ops:
  1.4 4.0 %collective-permute-start.4 = (f32[8,1,128]{2,1,0:T(1,128)S(1)}, f32[8,1,128]{2,1,0:T(1,128)S(1)}, u32[]{:S(2)}, u32[]{:S(2)}) collective-permute-start(f32[8,1,128]{2,1,0:T(1,128)S(1)} %get-tuple-element.629), channel_id=1, source_target_pairs={{0,1},{1,2},{2,3},{3,4},{4,5},{5,6},{6,7},{7,8},{8,9},{9,10},{10,1... | collective-permute-start | bytes 12296 | tf_op jit(solution)/shard_map/ppermute | solution.py:48
  5.4 8.5 %collective-permute-start.5 = (f32[8,1,128]{2,1,0:T(1,128)S(1)}, f32[8,1,128]{2,1,0:T(1,128)S(1)}, u32[]{:S(2)}, u32[]{:S(2)}) collective-permute-start(f32[8,1,128]{2,1,0:T(1,128)S(1)} %get-tuple-element.630), channel_id=1, source_target_pairs={{1,0},{2,1},{3,2},{4,3},{5,4},{6,5},{7,6},{8,7},{9,8},{10,9},{11,1... | collective-permute-start | bytes 12296 | tf_op jit(solution)/shard_map/ppermute | solution.py:50
  14.9 4.0 %collective-permute-start.1 = (f32[1,32,128]{2,1,0:T(8,128)S(1)}, f32[1,32,128]{2,1,0:T(8,128)S(1)}, u32[]{:S(2)}, u32[]{:S(2)}) collective-permute-start(f32[1,32,128]{2,1,0:T(8,128)S(1)} %get-tuple-element.627), channel_id=1, source_target_pairs={{0,64},{64,128},{128,192},{192,256},{256,320},{320,384},{384,448},... | collective-permute-start | bytes 49160 | tf_op jit(solution)/shard_map/ppermute | solution.py:48
  18.9 1.9 %collective-permute-start = (f32[1,32,128]{2,1,0:T(8,128)S(1)}, f32[1,32,128]{2,1,0:T(8,128)S(1)}, u32[]{:S(2)}, u32[]{:S(2)}) collective-permute-start(f32[1,32,128]{2,1,0:T(8,128)S(1)} %get-tuple-element.628), channel_id=1, source_target_pairs={{64,0},{128,64},{192,128},{256,192},{320,256},{384,320},{448,384},... | collective-permute-start | bytes 49160 | tf_op jit(solution)/shard_map/ppermute | solution.py:50
  26.7 3.6 %collective-permute-start.3 = (f32[10,1,128]{2,1,0:T(1,128)}, f32[10,1,128]{2,1,0:T(1,128)}, u32[]{:S(2)}, u32[]{:S(2)}) collective-permute-start(f32[10,1,128]{2,1,0:T(1,128)} %get-tuple-element.619), channel_id=1, source_target_pairs={{1,0},{2,1},{3,2},{4,3},{5,4},{6,5},{7,6},{8,7},{9,8},{10,9},{11,1... | collective-permute-start | bytes 15368 | tf_op jit(solution)/shard_map/ppermute | solution.py:50
  30.3 2.1 %collective-permute-start.2 = (f32[10,1,128]{2,1,0:T(1,128)}, f32[10,1,128]{2,1,0:T(1,128)}, u32[]{:S(2)}, u32[]{:S(2)}) collective-permute-start(f32[10,1,128]{2,1,0:T(1,128)} %get-tuple-element.620), channel_id=1, source_target_pairs={{0,1},{1,2},{2,3},{3,4},{4,5},{5,6},{6,7},{7,8},{8,9},{9,10},{10,1... | collective-permute-start | bytes 15368 | tf_op jit(solution)/shard_map/ppermute | solution.py:48
  33.1 3.3 %fusion.177 = (f32[8,16,1,64,1]{0,4,3,2,1:T(1,128)}, f32[8,16,1,64,1]{0,4,3,2,1:T(1,128)}, f32[8,16,1,64,1]{0,4,3,2,1:T(1,128)S(1)}, f32[8,16,1,64,1]{0,4,3,2,1:T(1,128)S(1)}) fusion(f32[8,16,2,64,2]{0,4,3,2,1:T(2,128)S(1)} %bitcast.700), kind=kLoop, calls=%fused_computation.414 | loop fusion | bytes 262144 | tf_op jit(solution)/shard_map/slice | solution.py:123
  45.5 3.2 %fusion.175 = (f32[8,16,1,64,1]{0,4,3,2,1:T(1,128)}, f32[8,16,1,64,1]{0,4,3,2,1:T(1,128)S(1)}, f32[8,16,1,64,1]{0,4,3,2,1:T(1,128)}, f32[8,16,1,64,1]{0,4,3,2,1:T(1,128)}) fusion(f32[8,16,2,64,2]{0,4,3,2,1:T(2,128)S(1)} %bitcast.701), kind=kLoop, calls=%fused_computation.412 | loop fusion | bytes 262144 | tf_op jit(solution)/shard_map/slice | solution.py:123
  57.1 1.9 %fusion.178 = (f32[8,16,1,64,1]{0,4,3,2,1:T(1,128)}, f32[8,16,1,64,1]{0,4,3,2,1:T(1,128)S(1)}) fusion(f32[8,16,2,64,2]{0,4,3,2,1:T(2,128)S(1)} %bitcast.705), kind=kLoop, calls=%fused_computation.415 | loop fusion | bytes 131072 | tf_op jit(solution)/shard_map/slice | solution.py:123
  63.2 3.2 %fusion.176 = (f32[8,16,1,64,1]{0,4,3,2,1:T(1,128)}, f32[8,16,1,64,1]{0,4,3,2,1:T(1,128)S(1)}, f32[8,16,1,64,1]{0,4,3,2,1:T(1,128)}, f32[8,16,1,64,1]{0,4,3,2,1:T(1,128)}) fusion(f32[8,16,2,64,2]{0,4,3,2,1:T(2,128)S(1)} %bitcast.702), kind=kLoop, calls=%fused_computation.413 | loop fusion | bytes 262144 | tf_op jit(solution)/shard_map/slice | solution.py:123
  71.0 5.4 %while.68 = (s32[]{:T(128)}, f32[16,128]{1,0:T(8,128)S(1)}, f32[3,16,128]{2,1,0:T(8,128)S(1)}, f32[7,16,128]{2,1,0:T(8,128)S(1)}, f32[7,3,16,128]{3,2,1,0:T(8,12...) while((s32[]{:T(128)}, f32[16,128]{1,0:T(8,128)S(1)}, ...), condition=%wide.region_1.2_spmd.clone, body=%wide.region_0.1_spmd.clone.sunk | while | flops 32771 | bytes 180360 | solution.py:68
  77.3 1.9 %collective-permute-start.6 = (f32[3,16,128]{2,1,0:T(8,128)S(1)}, f32[3,16,128]{2,1,0:T(8,128)S(1)}, u32[]{:S(2)}, u32[]{:S(2)}) collective-permute-start(f32[3,16,128]{2,1,0:T(8,128)S(1)} %pad_maximum_fusion.28), channel_id=1, source_target_pairs={{64,0},{128,64},{192,128},{256,192},{320,256},{384,320},{448,384},... | collective-permute-start | bytes 73736 | tf_op jit(solution)/shard_map/ppermute | solution.py:17
  80.6 2.1 %collective-permute-done.6 = f32[3,16,128]{2,1,0:T(8,128)S(1)} collective-permute-done((f32[3,16,128]{2,1,0:T(8,128)S(1)}, f32[3,16,128]{2,1,0:T(8,128)S(1)}, u32[]{:S(2)}, u32[]{:S(2)}) %collective-permute-start.6) | collective-permute-done | bytes 24608 | tf_op jit(solution)/shard_map/ppermute | solution.py:17
  82.9 9.3 %all-gather = f32[16,16,128]{2,1,0:T(8,128)S(1)} all-gather(f32[4,16,128]{2,1,0:T(8,128)S(1)} %pad_maximum_fusion.26), channel_id=2, replica_groups=mesh['zg_0'=4,'zg_1'=2,'xy'=64] {'zg_0'}, dimensions={0}, use_global_device_ids=true | all-gather | bytes 163840 | tf_op jit(solution)/shard_map/all_gather | solution.py:29
  92.2 3.6 %all_gather.13 = f32[8,1,4,16,128]{4,3,2,1,0:T(8,128)S(1)} all-gather(f32[4,1,4,16,128]{4,3,2,1,0:T(8,128)S(1)} %bitcast.738), channel_id=1, replica_groups=mesh['zg_0'=4,'zg_1'=2,'xy'=64] {'zg_1'}, dimensions={0}, use_global_device_ids=true | all-gather | bytes 393216 | tf_op jit(solution)/shard_map/all_gather | solution.py:29
  98.6 1.9 %collective-permute-start.7 = (f32[8,1,128]{2,1,0:T(1,128)S(1)}, f32[8,1,128]{2,1,0:T(1,128)S(1)}, u32[]{:S(2)}, u32[]{:S(2)}) collective-permute-start(f32[8,1,128]{2,1,0:T(1,128)S(1)} %get-tuple-element.625), channel_id=1, source_target_pairs={{0,1},{1,2},{2,3},{3,4},{4,5},{5,6},{6,7},{7,8},{8,9},{9,10},{10,1... | collective-permute-start | bytes 12296 | tf_op jit(solution)/shard_map/ppermute | solution.py:48
  100.5 7.2 %collective-permute-start.8 = (f32[8,1,128]{2,1,0:T(1,128)S(1)}, f32[8,1,128]{2,1,0:T(1,128)S(1)}, u32[]{:S(2)}, u32[]{:S(2)}) collective-permute-start(f32[8,1,128]{2,1,0:T(1,128)S(1)} %get-tuple-element.626), channel_id=1, source_target_pairs={{1,0},{2,1},{3,2},{4,3},{5,4},{6,5},{7,6},{8,7},{9,8},{10,9},{11,1... | collective-permute-start | bytes 12296 | tf_op jit(solution)/shard_map/ppermute | solution.py:50
  110.1 1.9 %fusion.173 = (f32[8,16,1,64,1]{0,4,3,2,1:T(1,128)}, f32[8,16,1,64,1]{0,4,3,2,1:T(1,128)S(1)}) fusion(f32[8,16,2,64,2]{0,4,3,2,1:T(2,128)S(1)} %bitcast.706), kind=kLoop, calls=%fused_computation.410 | loop fusion | bytes 131072 | tf_op jit(solution)/shard_map/slice | solution.py:123
  114.5 9.8 %while.70 = (s32[]{:T(128)}, f32[16,128]{1,0:T(8,128)}, f32[3,16,128]{2,1,0:T(8,128)S(1)}, f32[7,16,128]{2,1,0:T(8,128)S(1)}, f32[7,3,16,128]{3,2,1,0:T(8,128)S(...) while((s32[]{:T(128)}, f32[16,128]{1,0:T(8,128)}, ...), condition=%wide.region_5.6_spmd.clone, body=%wide.region_4.5_spmd.clone.sunk | while | flops 32771 | bytes 180360 | solution.py:68
  124.7 3.0 %collective-permute-start.9 = (f32[3,16,128]{2,1,0:T(8,128)S(1)}, f32[3,16,128]{2,1,0:T(8,128)S(1)}, u32[]{:S(2)}, u32[]{:S(2)}) collective-permute-start(f32[3,16,128]{2,1,0:T(8,128)S(1)} %pad_maximum_fusion.29), channel_id=1, source_target_pairs={{64,0},{128,64},{192,128},{256,192},{320,256},{384,320},{448,384},... | collective-permute-start | bytes 73736 | tf_op jit(solution)/shard_map/ppermute | solution.py:17
  127.8 2.2 %collective-permute-done.9 = f32[3,16,128]{2,1,0:T(8,128)S(1)} collective-permute-done((f32[3,16,128]{2,1,0:T(8,128)S(1)}, f32[3,16,128]{2,1,0:T(8,128)S(1)}, u32[]{:S(2)}, u32[]{:S(2)}) %collective-permute-start.9) | collective-permute-done | bytes 24608 | tf_op jit(solution)/shard_map/ppermute | solution.py:17
  130.2 9.1 %all-gather.1 = f32[16,16,128]{2,1,0:T(8,128)S(1)} all-gather(f32[4,16,128]{2,1,0:T(8,128)S(1)} %pad_maximum_fusion.27), channel_id=3, replica_groups=mesh['zg_0'=4,'zg_1'=2,'xy'=64] {'zg_0'}, dimensions={0}, use_global_device_ids=true | all-gather | bytes 163840 | tf_op jit(solution)/shard_map/all_gather | solution.py:29
  139.3 3.4 %all_gather.15 = f32[8,1,4,16,128]{4,3,2,1,0:T(8,128)S(1)} all-gather(f32[4,1,4,16,128]{4,3,2,1,0:T(8,128)S(1)} %bitcast.739), channel_id=1, replica_groups=mesh['zg_0'=4,'zg_1'=2,'xy'=64] {'zg_1'}, dimensions={0}, use_global_device_ids=true | all-gather | bytes 393216 | tf_op jit(solution)/shard_map/all_gather | solution.py:29
  144.0 3.4 %collective-permute-start.10 = (f32[1,32,128]{2,1,0:T(8,128)S(1)}, f32[1,32,128]{2,1,0:T(8,128)S(1)}, u32[]{:S(2)}, u32[]{:S(2)}) collective-permute-start(f32[1,32,128]{2,1,0:T(8,128)S(1)} %slice.792), channel_id=1, source_target_pairs={{0,64},{64,128},{128,192},{192,256},{256,320},{320,384},{384,448},... | collective-permute-start | bytes 49160 | tf_op jit(solution)/shard_map/ppermute | solution.py:48
  148.3 1.9 %collective-permute-start.11 = (f32[1,32,128]{2,1,0:T(8,128)S(1)}, f32[1,32,128]{2,1,0:T(8,128)S(1)}, u32[]{:S(2)}, u32[]{:S(2)}) collective-permute-start(f32[1,32,128]{2,1,0:T(8,128)S(1)} %slice.794), channel_id=1, source_target_pairs={{64,0},{128,64},{192,128},{256,192},{320,256},{384,320},{448,384},... | collective-permute-start | bytes 49160 | tf_op jit(solution)/shard_map/ppermute | solution.py:50
  153.4 1.9 %collective-permute-start.12 = (f32[10,1,128]{2,1,0:T(1,128)S(1)}, f32[10,1,128]{2,1,0:T(1,128)S(1)}, u32[]{:S(2)}, u32[]{:S(2)}) collective-permute-start(f32[10,1,128]{2,1,0:T(1,128)S(1)} %get-tuple-element.617), channel_id=1, source_target_pairs={{0,1},{1,2},{2,3},{3,4},{4,5},{5,6},{6,7},{7,8},{8,9},{9,10},{10,1... | collective-permute-start | bytes 15368 | tf_op jit(solution)/shard_map/ppermute | solution.py:48
  155.3 7.2 %collective-permute-start.13 = (f32[10,1,128]{2,1,0:T(1,128)S(1)}, f32[10,1,128]{2,1,0:T(1,128)S(1)}, u32[]{:S(2)}, u32[]{:S(2)}) collective-permute-start(f32[10,1,128]{2,1,0:T(1,128)S(1)} %get-tuple-element.618), channel_id=1, source_target_pairs={{1,0},{2,1},{3,2},{4,3},{5,4},{6,5},{7,6},{8,7},{9,8},{10,9},{11,1... | collective-permute-start | bytes 15368 | tf_op jit(solution)/shard_map/ppermute | solution.py:50
  164.5 3.1 %collective-permute-start.14 = (f32[1,32,128]{2,1,0:T(8,128)S(1)}, f32[1,32,128]{2,1,0:T(8,128)S(1)}, u32[]{:S(2)}, u32[]{:S(2)}) collective-permute-start(f32[1,32,128]{2,1,0:T(8,128)S(1)} %get-tuple-element.623), channel_id=1, source_target_pairs={{0,64},{64,128},{128,192},{192,256},{256,320},{320,384},{384,448},... | collective-permute-start | bytes 49160 | tf_op jit(solution)/shard_map/ppermute | solution.py:48
  167.6 1.9 %collective-permute-start.15 = (f32[1,32,128]{2,1,0:T(8,128)S(1)}, f32[1,32,128]{2,1,0:T(8,128)S(1)}, u32[]{:S(2)}, u32[]{:S(2)}) collective-permute-start(f32[1,32,128]{2,1,0:T(8,128)S(1)} %get-tuple-element.624), channel_id=1, source_target_pairs={{64,0},{128,64},{192,128},{256,192},{320,256},{384,320},{448,384},... | collective-permute-start | bytes 49160 | tf_op jit(solution)/shard_map/ppermute | solution.py:50
  169.6 3.1 %collective-permute-done.15 = f32[1,32,128]{2,1,0:T(8,128)S(1)} collective-permute-done((f32[1,32,128]{2,1,0:T(8,128)S(1)}, f32[1,32,128]{2,1,0:T(8,128)S(1)}, u32[]{:S(2)}, u32[]{:S(2)}) %collective-permute-start.15) | collective-permute-done | bytes 16416 | tf_op jit(solution)/shard_map/ppermute | solution.py:50
  172.7 1.9 %collective-permute-start.16 = (f32[10,1,128]{2,1,0:T(1,128)S(1)}, f32[10,1,128]{2,1,0:T(1,128)S(1)}, u32[]{:S(2)}, u32[]{:S(2)}) collective-permute-start(f32[10,1,128]{2,1,0:T(1,128)S(1)} %get-tuple-element.615), channel_id=1, source_target_pairs={{0,1},{1,2},{2,3},{3,4},{4,5},{5,6},{6,7},{7,8},{8,9},{9,10},{10,1... | collective-permute-start | bytes 15368 | tf_op jit(solution)/shard_map/ppermute | solution.py:48
  174.6 7.2 %collective-permute-start.17 = (f32[10,1,128]{2,1,0:T(1,128)S(1)}, f32[10,1,128]{2,1,0:T(1,128)S(1)}, u32[]{:S(2)}, u32[]{:S(2)}) collective-permute-start(f32[10,1,128]{2,1,0:T(1,128)S(1)} %get-tuple-element.616), channel_id=1, source_target_pairs={{1,0},{2,1},{3,2},{4,3},{5,4},{6,5},{7,6},{8,7},{9,8},{10,9},{11,1... | collective-permute-start | bytes 15368 | tf_op jit(solution)/shard_map/ppermute | solution.py:50
  (292 shorter events, 71.3 us)
Async XLA Ops:
  1.4 23.7 %collective-permute-start.4 = (f32[8,1,128]{2,1,0:T(1,128)S(1)}, f32[8,1,128]{2,1,0:T(1,128)S(1)}, u32[]{:S(2)}, u32[]{:S(2)}) collective-permute-start(f32[8,1,128]{2,1,0:T(1,128)S(1)} %get-tuple-element.629), channel_id=1, source_target_pairs={{0,1},{1,2},{2,3},{3,4},{4,5},{5,6},{6,7},{7,8},{8,9},{9,10},{10,1... | collective-permute-start | bytes 12296 | tf_op jit(solution)/shard_map/ppermute | solution.py:48
  5.4 19.7 %collective-permute-start.5 = (f32[8,1,128]{2,1,0:T(1,128)S(1)}, f32[8,1,128]{2,1,0:T(1,128)S(1)}, u32[]{:S(2)}, u32[]{:S(2)}) collective-permute-start(f32[8,1,128]{2,1,0:T(1,128)S(1)} %get-tuple-element.630), channel_id=1, source_target_pairs={{1,0},{2,1},{3,2},{4,3},{5,4},{6,5},{7,6},{8,7},{9,8},{10,9},{11,1... | collective-permute-start | bytes 12296 | tf_op jit(solution)/shard_map/ppermute | solution.py:50
  14.9 11.1 %collective-permute-start.1 = (f32[1,32,128]{2,1,0:T(8,128)S(1)}, f32[1,32,128]{2,1,0:T(8,128)S(1)}, u32[]{:S(2)}, u32[]{:S(2)}) collective-permute-start(f32[1,32,128]{2,1,0:T(8,128)S(1)} %get-tuple-element.627), channel_id=1, source_target_pairs={{0,64},{64,128},{128,192},{192,256},{256,320},{320,384},{384,448},... | collective-permute-start | bytes 49160 | tf_op jit(solution)/shard_map/ppermute | solution.py:48
  18.9 7.2 %collective-permute-start = (f32[1,32,128]{2,1,0:T(8,128)S(1)}, f32[1,32,128]{2,1,0:T(8,128)S(1)}, u32[]{:S(2)}, u32[]{:S(2)}) collective-permute-start(f32[1,32,128]{2,1,0:T(8,128)S(1)} %get-tuple-element.628), channel_id=1, source_target_pairs={{64,0},{128,64},{192,128},{256,192},{320,256},{384,320},{448,384},... | collective-permute-start | bytes 49160 | tf_op jit(solution)/shard_map/ppermute | solution.py:50
  26.7 14.0 %collective-permute-start.3 = (f32[10,1,128]{2,1,0:T(1,128)}, f32[10,1,128]{2,1,0:T(1,128)}, u32[]{:S(2)}, u32[]{:S(2)}) collective-permute-start(f32[10,1,128]{2,1,0:T(1,128)} %get-tuple-element.619), channel_id=1, source_target_pairs={{1,0},{2,1},{3,2},{4,3},{5,4},{6,5},{7,6},{8,7},{9,8},{10,9},{11,1... | collective-permute-start | bytes 15368 | tf_op jit(solution)/shard_map/ppermute | solution.py:50
  30.3 10.4 %collective-permute-start.2 = (f32[10,1,128]{2,1,0:T(1,128)}, f32[10,1,128]{2,1,0:T(1,128)}, u32[]{:S(2)}, u32[]{:S(2)}) collective-permute-start(f32[10,1,128]{2,1,0:T(1,128)} %get-tuple-element.620), channel_id=1, source_target_pairs={{0,1},{1,2},{2,3},{3,4},{4,5},{5,6},{6,7},{7,8},{8,9},{9,10},{10,1... | collective-permute-start | bytes 15368 | tf_op jit(solution)/shard_map/ppermute | solution.py:48
  71.0 11.9 %copy-start.29 = (f32[8,16,64]{2,1,0:T(8,128)S(1)}, f32[8,16,64]{2,1,0:T(8,128)}, u32[]{:S(2)}) copy-start(f32[8,16,64]{2,1,0:T(8,128)} %copy.437) | copy-start | bytes 98308
  71.0 11.9 %copy-start.30 = (f32[8,16,64]{2,1,0:T(8,128)S(1)}, f32[8,16,64]{2,1,0:T(8,128)}, u32[]{:S(2)}) copy-start(f32[8,16,64]{2,1,0:T(8,128)} %copy.436) | copy-start | bytes 98308
  76.9 19.2 %copy-start.32 = (f32[8,16,64,1]{2,1,3,0:T(8,128)S(1)}, f32[8,16,64,1]{2,1,3,0:T(8,128)}, u32[]{:S(2)}) copy-start(f32[8,16,64,1]{2,1,3,0:T(8,128)} %copy.455) | copy-start | bytes 98308
  77.1 19.7 %copy-start.25 = (f32[8,16,64]{2,1,0:T(8,128)}, f32[8,16,64]{2,1,0:T(8,128)S(1)}, u32[]{:S(2)}) copy-start(f32[8,16,64]{2,1,0:T(8,128)S(1)} %copy.452) | copy-start | bytes 98308
  77.1 19.7 %copy-start.31 = (f32[8,16,64,1]{2,1,3,0:T(8,128)S(1)}, f32[8,16,64,1]{2,1,3,0:T(8,128)}, u32[]{:S(2)}) copy-start(f32[8,16,64,1]{2,1,3,0:T(8,128)} %copy.448) | copy-start | bytes 98308
  77.3 19.5 %copy-start.27 = (f32[8,16,64]{2,1,0:T(8,128)}, f32[8,16,64]{2,1,0:T(8,128)S(1)}, u32[]{:S(2)}) copy-start(f32[8,16,64]{2,1,0:T(8,128)S(1)} %copy.451) | copy-start | bytes 98308
  77.3 5.4 %collective-permute-start.6 = (f32[3,16,128]{2,1,0:T(8,128)S(1)}, f32[3,16,128]{2,1,0:T(8,128)S(1)}, u32[]{:S(2)}, u32[]{:S(2)}) collective-permute-start(f32[3,16,128]{2,1,0:T(8,128)S(1)} %pad_maximum_fusion.28), channel_id=1, source_target_pairs={{64,0},{128,64},{192,128},{256,192},{320,256},{384,320},{448,384},... | collective-permute-start | bytes 73736 | tf_op jit(solution)/shard_map/ppermute | solution.py:17
  98.6 9.8 %collective-permute-start.7 = (f32[8,1,128]{2,1,0:T(1,128)S(1)}, f32[8,1,128]{2,1,0:T(1,128)S(1)}, u32[]{:S(2)}, u32[]{:S(2)}) collective-permute-start(f32[8,1,128]{2,1,0:T(1,128)S(1)} %get-tuple-element.625), channel_id=1, source_target_pairs={{0,1},{1,2},{2,3},{3,4},{4,5},{5,6},{6,7},{7,8},{8,9},{9,10},{10,1... | collective-permute-start | bytes 12296 | tf_op jit(solution)/shard_map/ppermute | solution.py:48
  100.5 7.8 %collective-permute-start.8 = (f32[8,1,128]{2,1,0:T(1,128)S(1)}, f32[8,1,128]{2,1,0:T(1,128)S(1)}, u32[]{:S(2)}, u32[]{:S(2)}) collective-permute-start(f32[8,1,128]{2,1,0:T(1,128)S(1)} %get-tuple-element.626), channel_id=1, source_target_pairs={{1,0},{2,1},{3,2},{4,3},{5,4},{6,5},{7,6},{8,7},{9,8},{10,9},{11,1... | collective-permute-start | bytes 12296 | tf_op jit(solution)/shard_map/ppermute | solution.py:50
  112.0 12.3 %copy-start.20 = (f32[3,16,128]{2,1,0:T(8,128)S(1)}, f32[3,16,128]{2,1,0:T(8,128)}, u32[]{:S(2)}) copy-start(f32[3,16,128]{2,1,0:T(8,128)} %custom-call.5) | copy-start | bytes 73732
  112.0 15.8 %copy-start.11 = (f32[8,16,64]{2,1,0:T(8,128)S(1)}, f32[8,16,64]{2,1,0:T(8,128)}, u32[]{:S(2)}) copy-start(f32[8,16,64]{2,1,0:T(8,128)} %copy-done.10) | copy-start | bytes 98308
  112.0 15.8 %copy-start.13 = (f32[8,16,64]{2,1,0:T(8,128)S(1)}, f32[8,16,64]{2,1,0:T(8,128)}, u32[]{:S(2)}) copy-start(f32[8,16,64]{2,1,0:T(8,128)} %copy-done.12) | copy-start | bytes 98308
  112.0 18.1 %copy-start.26 = (f32[8,16,64]{2,1,0:T(8,128)S(1)}, f32[8,16,64]{2,1,0:T(8,128)}, u32[]{:S(2)}) copy-start(f32[8,16,64]{2,1,0:T(8,128)} %copy-done.25) | copy-start | bytes 98308
  112.0 18.1 %copy-start.28 = (f32[8,16,64]{2,1,0:T(8,128)S(1)}, f32[8,16,64]{2,1,0:T(8,128)}, u32[]{:S(2)}) copy-start(f32[8,16,64]{2,1,0:T(8,128)} %copy-done.27) | copy-start | bytes 98308
  124.2 18.8 %copy-start.34 = (f32[8,16,64,1]{2,1,3,0:T(8,128)S(1)}, f32[8,16,64,1]{2,1,3,0:T(8,128)}, u32[]{:S(2)}) copy-start(f32[8,16,64,1]{2,1,3,0:T(8,128)} %slice_bitcast_fusion.1) | copy-start | bytes 98308
  124.3 18.8 %copy-start.33 = (f32[8,16,64,1]{2,1,3,0:T(8,128)S(1)}, f32[8,16,64,1]{2,1,3,0:T(8,128)}, u32[]{:S(2)}) copy-start(f32[8,16,64,1]{2,1,3,0:T(8,128)} %slice_bitcast_fusion) | copy-start | bytes 98308
  124.7 5.3 %collective-permute-start.9 = (f32[3,16,128]{2,1,0:T(8,128)S(1)}, f32[3,16,128]{2,1,0:T(8,128)S(1)}, u32[]{:S(2)}, u32[]{:S(2)}) collective-permute-start(f32[3,16,128]{2,1,0:T(8,128)S(1)} %pad_maximum_fusion.29), channel_id=1, source_target_pairs={{64,0},{128,64},{192,128},{256,192},{320,256},{384,320},{448,384},... | collective-permute-start | bytes 73736 | tf_op jit(solution)/shard_map/ppermute | solution.py:17
  144.0 8.0 %collective-permute-start.10 = (f32[1,32,128]{2,1,0:T(8,128)S(1)}, f32[1,32,128]{2,1,0:T(8,128)S(1)}, u32[]{:S(2)}, u32[]{:S(2)}) collective-permute-start(f32[1,32,128]{2,1,0:T(8,128)S(1)} %slice.792), channel_id=1, source_target_pairs={{0,64},{64,128},{128,192},{192,256},{256,320},{320,384},{384,448},... | collective-permute-start | bytes 49160 | tf_op jit(solution)/shard_map/ppermute | solution.py:48
  148.3 5.1 %collective-permute-start.11 = (f32[1,32,128]{2,1,0:T(8,128)S(1)}, f32[1,32,128]{2,1,0:T(8,128)S(1)}, u32[]{:S(2)}, u32[]{:S(2)}) collective-permute-start(f32[1,32,128]{2,1,0:T(8,128)S(1)} %slice.794), channel_id=1, source_target_pairs={{64,0},{128,64},{192,128},{256,192},{320,256},{384,320},{448,384},... | collective-permute-start | bytes 49160 | tf_op jit(solution)/shard_map/ppermute | solution.py:50
  151.9 31.1 %copy-start.1 = (f32[8,32,128]{2,1,0:T(8,128)}, f32[8,32,128]{2,1,0:T(8,128)S(1)}, u32[]{:S(2)}) copy-start(f32[8,32,128]{2,1,0:T(8,128)S(1)} %copy.485) | copy-start | bytes 393220
  153.4 9.2 %collective-permute-start.12 = (f32[10,1,128]{2,1,0:T(1,128)S(1)}, f32[10,1,128]{2,1,0:T(1,128)S(1)}, u32[]{:S(2)}, u32[]{:S(2)}) collective-permute-start(f32[10,1,128]{2,1,0:T(1,128)S(1)} %get-tuple-element.617), channel_id=1, source_target_pairs={{0,1},{1,2},{2,3},{3,4},{4,5},{5,6},{6,7},{7,8},{8,9},{9,10},{10,1... | collective-permute-start | bytes 15368 | tf_op jit(solution)/shard_map/ppermute | solution.py:48
  155.3 8.0 %collective-permute-start.13 = (f32[10,1,128]{2,1,0:T(1,128)S(1)}, f32[10,1,128]{2,1,0:T(1,128)S(1)}, u32[]{:S(2)}, u32[]{:S(2)}) collective-permute-start(f32[10,1,128]{2,1,0:T(1,128)S(1)} %get-tuple-element.618), channel_id=1, source_target_pairs={{1,0},{2,1},{3,2},{4,3},{5,4},{6,5},{7,6},{8,7},{9,8},{10,9},{11,1... | collective-permute-start | bytes 15368 | tf_op jit(solution)/shard_map/ppermute | solution.py:50
  164.5 5.1 %collective-permute-start.14 = (f32[1,32,128]{2,1,0:T(8,128)S(1)}, f32[1,32,128]{2,1,0:T(8,128)S(1)}, u32[]{:S(2)}, u32[]{:S(2)}) collective-permute-start(f32[1,32,128]{2,1,0:T(8,128)S(1)} %get-tuple-element.623), channel_id=1, source_target_pairs={{0,64},{64,128},{128,192},{192,256},{256,320},{320,384},{384,448},... | collective-permute-start | bytes 49160 | tf_op jit(solution)/shard_map/ppermute | solution.py:48
  167.6 5.1 %collective-permute-start.15 = (f32[1,32,128]{2,1,0:T(8,128)S(1)}, f32[1,32,128]{2,1,0:T(8,128)S(1)}, u32[]{:S(2)}, u32[]{:S(2)}) collective-permute-start(f32[1,32,128]{2,1,0:T(8,128)S(1)} %get-tuple-element.624), channel_id=1, source_target_pairs={{64,0},{128,64},{192,128},{256,192},{320,256},{384,320},{448,384},... | collective-permute-start | bytes 49160 | tf_op jit(solution)/shard_map/ppermute | solution.py:50
  172.7 9.2 %collective-permute-start.16 = (f32[10,1,128]{2,1,0:T(1,128)S(1)}, f32[10,1,128]{2,1,0:T(1,128)S(1)}, u32[]{:S(2)}, u32[]{:S(2)}) collective-permute-start(f32[10,1,128]{2,1,0:T(1,128)S(1)} %get-tuple-element.615), channel_id=1, source_target_pairs={{0,1},{1,2},{2,3},{3,4},{4,5},{5,6},{6,7},{7,8},{8,9},{9,10},{10,1... | collective-permute-start | bytes 15368 | tf_op jit(solution)/shard_map/ppermute | solution.py:48
  174.6 8.0 %collective-permute-start.17 = (f32[10,1,128]{2,1,0:T(1,128)S(1)}, f32[10,1,128]{2,1,0:T(1,128)S(1)}, u32[]{:S(2)}, u32[]{:S(2)}) collective-permute-start(f32[10,1,128]{2,1,0:T(1,128)S(1)} %get-tuple-element.616), channel_id=1, source_target_pairs={{1,0},{2,1},{3,2},{4,3},{5,4},{6,5},{7,6},{8,7},{9,8},{10,9},{11,1... | collective-permute-start | bytes 15368 | tf_op jit(solution)/shard_map/ppermute | solution.py:50
  (28 other events, 165.4 us)
where the time goes:
time: 189 us; the launch traced here: 186 us
  starting transfers between devices  66.8 us (35%)
  local copies, waits for them, and re-layouts  48 us (25%)
  other arithmetic  33.2 us (18%)
  blocking collectives  25.3 us (13%)
  waiting for transfers between devices  10.3 us (5%)
    ppermute x8, starting transfers between devices, extended(): lax.ppermute(head, axis, [((i + 1) % count, i) for i in range(ends)])  39.5 us
    all_gather x4, blocking collectives, stacked_from(): pieces = lax.all_gather(pieces, axes[k], axis=0, tiled=True)  25.3 us
    ppermute x8, starting transfers between devices, extended(): lax.ppermute(tail, axis, [(i, (i + 1) % count) for i in range(ends)])  22.4 us
    dynamic_update_slice x42, other arithmetic, thomas(): lax.scan(forward, initial, (lower_coef, diagonal, upper_coef, right_side))  15.1 us
    slice x5, local copies, waits for them, and re-layouts, select_colour(): blocks[:, :, 1, :, 1 - colour]  13.5 us
    squeeze x8, local copies, waits for them, and re-layouts, select_colour(): blocks[:, :, 1, :, 1 - colour]  8.53 us
    ppermute x8, waiting for transfers between devices, extended(): lax.ppermute(head, axis, [((i + 1) % count, i) for i in range(ends)])  5.96 us
    squeeze x8, local copies, waits for them, and re-layouts, select_colour(): blocks[:, :, 0, :, colour]  5.38 us
  transfers between devices with their start and end apart: 18, of which 6 were waited for; matrix products, arithmetic and copies ran while one was open for 10% of the time, Pallas kernels for 0%

commit v1 on v0

v1 whole, which is shorter than its diff:
```python
import jax
import jax.numpy as jnp
from jax import lax
from jax.experimental import pallas as pl
from jax.experimental.pallas import tpu as pltpu
from jax.sharding import Mesh
from jax.sharding import PartitionSpec as P

INTERPRET = False
vertical_ratio = 100.0
absorption = 0.05

LEV = 16
WIN = 24
LAN = 128
F32 = jnp.float32


def east_of(v):
    return pltpu.roll(v, WIN - 1, 0)


def west_of(v):
    return pltpu.roll(v, 1, 0)


def north_of(v):
    return pltpu.roll(v, LAN - 1, 1)


def south_of(v):
    return pltpu.roll(v, 1, 1)


def iotas():
    row = lax.broadcasted_iota(jnp.int32, (WIN, LAN), 0)
    lane = lax.broadcasted_iota(jnp.int32, (WIN, LAN), 1)
    red = ((row + lane) & 1) == 0
    return row, lane, red


def side_faces(w, last_lane):
    east = jnp.sqrt(w * east_of(w))
    north = jnp.where(last_lane, 0.0, jnp.sqrt(w * north_of(w)))
    return east, north


def horizontal(east, north, p):
    return (
        west_of(east * p)
        + east * east_of(p)
        + south_of(north * p)
        + north * north_of(p)
    )


def weigh_kernel(source, cond, fluid, pressure, out):
    real = fluid[...].astype(F32)
    out[0] = cond[...] * real
    out[1] = real * source[...]
    out[2] = pressure[...]


def edge_kernel(both, out):
    core = lax.axis_index("zk")
    start = pl.multiple_of(core * 24, 8)
    for f in range(3):
        for l in range(LEV):
            out[f, l] = both[l // 8, f, l % 8, pl.ds(start, 8), :]


def first_kernel(both, halo, send, ef, nf, vf, dg, fr, pr, rc, mm, gr, br, bg):
    core = lax.axis_index("zk")
    row, lane, red = iotas()
    last_lane = lane == LAN - 1
    row8 = lax.broadcasted_iota(jnp.int32, (8, LAN), 0)
    from_near = (row8 < 4) == (core == 0)
    own_at = pl.multiple_of(core * 16, 8)
    near_at = pl.multiple_of(16 - 8 * core, 8)

    def window(f, l):
        own = both[l // 8, f, l % 8, pl.ds(own_at, 16), :]
        near = both[l // 8, f, l % 8, pl.ds(near_at, 8), :]
        return jnp.concatenate([own, jnp.where(from_near, near, halo[f, l])], axis=0)

    w = None
    below = None
    for l in range(LEV):
        w_prev, w = w, window(0, l)
        east, north = side_faces(w, last_lane)
        ef[l] = east
        nf[l] = north
        west, south = west_of(east), south_of(north)
        if l > 0:
            below = vertical_ratio * jnp.sqrt(w * w_prev)
            vf[l] = below
        else:
            vf[l] = jnp.zeros_like(w)
            w0 = w
        fluid = jnp.where(w > 0.0, 1.0, 0.0)
        dg[l] = fluid * (absorption + (west + east + south + north)) + (1.0 - fluid)
        f = window(1, l)
        p = window(2, l)
        fr[l] = f
        pr[l] = p
    w15 = w
    bot = None
    for l in range(LEV):
        d = dg[l] + vf[l]
        if l < LEV - 1:
            d = d + vf[l + 1]
        dg[l] = d
        p = pr[l]
        b = fr[l] + horizontal(ef[l], nf[l], p)
        if l == 0:
            top_d, top_b = d, b
            continue
        v = vf[l]
        if l == 1:
            dd, bb, g = d, b, v
        else:
            dd = d - mult * v
            bb = b + mult * bb
            g = mult * g
        if l < LEV - 1:
            rcp = 1.0 / dd
            mult = vf[l + 1] * rcp
            grl = g * rcp
            rc[l] = rcp
            mm[l] = mult
            gr[l] = grl
            br[l] = bb
            top_d = top_d - g * grl
            top_b = top_b + grl * bb
    beta = gr[LEV - 2]
    gamma = mm[LEV - 2]
    bg[0] = jnp.where(red, south_of(gamma), beta)
    for l in range(LEV - 3, 0, -1):
        beta = gr[l] + mm[l] * beta
        gamma = mm[l] * gamma
    bg[1] = jnp.where(red, south_of(gamma), beta)
    packed = jnp.where(red, top_b, south_of(bb))
    for peer in range(4):
        send[peer, 0] = top_d
        send[peer, 1] = g
        send[peer, 2] = dd
        send[peer, 3] = w0
        send[peer, 4] = w15
        send[peer, 5] = packed
    bg[2] = window(0, LEV - 2)
    bg[3] = window(0, 1)


def chain_solve(rj, mj, cj, right):
    acc = [right[0]]
    for j in range(1, 8):
        acc.append(right[j] + mj[j] * acc[j - 1])
    out = [None] * 8
    out[7] = acc[7] * rj[7]
    for j in range(6, -1, -1):
        out[j] = (acc[j] + cj[j + 1] * out[j + 1]) * rj[j]
    return out


def second_kernel(got, ef, nf, vf, fr, pr, rc, mm, gr, br, bg, send, p1, bb_out, chain, u_red):
    chip = lax.axis_index("zc")
    row, lane, red = iotas()
    pivot = None
    rj, mj, cj, right = [], [], [], []
    face = None
    for j in range(8):
        group, last = j // 2, j % 2
        if last == 0:
            up = got[group, 0]
            link = face if group > 0 else None
            if group > 0:
                up = up + face
            packed = got[group, 5]
            right.append(packed)
        else:
            up = got[group, 2]
            link = got[group, 1]
            if group < 3:
                face = vertical_ratio * jnp.sqrt(got[group, 4] * got[group + 1, 3])
                up = up + face
            right.append(north_of(packed))
        if link is None:
            mj.append(None)
            cj.append(None)
            pivot = up
        else:
            m = link * rj[-1]
            mj.append(m)
            cj.append(link)
            pivot = up - m * link
        rj.append(1.0 / pivot)
        chain[0, j] = rj[j]
        if j > 0:
            chain[1, j] = mj[j]
            chain[2, j] = cj[j]
        else:
            chain[1, j] = jnp.zeros((WIN, LAN), F32)
            chain[2, j] = jnp.zeros((WIN, LAN), F32)
    sol = chain_solve(rj, mj, cj, right)
    for j in range(8):
        u_red[j] = sol[j]
    low = u_red[2 * chip]
    high = u_red[2 * chip + 1]
    p1[0] = jnp.where(red, low, pr[0])
    p1[LEV - 1] = jnp.where(red, high, pr[LEV - 1])
    cur = high
    for l in range(LEV - 2, 0, -1):
        cur = br[l] * rc[l] + gr[l] * low + mm[l] * cur
        p1[l] = jnp.where(red, cur, pr[l])
    for l in range(LEV):
        b = fr[l] + horizontal(ef[l], nf[l], p1[l])
        if l == 0:
            top_b = b
            continue
        if l == 1:
            bb = b
        else:
            bb = b + mm[l - 1] * bb
        if l < LEV - 1:
            bb_out[l] = bb
            top_b = top_b + gr[l] * bb
    bb_out[0] = jnp.zeros((WIN, LAN), F32)
    bb_out[LEV - 1] = jnp.zeros((WIN, LAN), F32)
    alpha14 = bb_out[LEV - 2] * rc[LEV - 2]
    alpha = alpha14
    for l in range(LEV - 3, 0, -1):
        alpha = bb_out[l] * rc[l] + mm[l] * alpha
    packed = jnp.where(red, south_of(bb), top_b)
    up_mix = jnp.where(red, p1[LEV - 2], alpha14)
    down_mix = jnp.where(red, p1[1], alpha)
    for peer in range(4):
        send[peer, 0] = packed

        @pl.when(chip < peer)
        def _():
            send[peer, 1] = up_mix
            send[peer, 2] = bg[0]
            send[peer, 3] = bg[2]
            send[peer, 4] = fr[LEV - 1]

        @pl.when(chip >= peer)
        def _():
            send[peer, 1] = down_mix
            send[peer, 2] = bg[1]
            send[peer, 3] = bg[3]
            send[peer, 4] = fr[0]


def third_kernel(got3, got2, ef, nf, vf, dg, fr, rc, mm, gr, bb_in, p1, chain, u_red, weights, out, u_all, full, res):
    chip = lax.axis_index("zc")
    row, lane, red = iotas()
    last_lane = lane == LAN - 1
    rj = [chain[0, j] for j in range(8)]
    mj = [chain[1, j] for j in range(8)]
    cj = [chain[2, j] for j in range(8)]
    right = []
    for group in range(4):
        packed = got3[group, 0]
        right += [packed, north_of(packed)]
    sol = chain_solve(rj, mj, cj, right)
    for j in range(8):
        u_all[j] = jnp.where(red, u_red[j], sol[j])
    low = u_all[2 * chip]
    high = u_all[2 * chip + 1]
    full[2] = low
    full[LEV + 1] = high
    cur = high
    for l in range(LEV - 2, 0, -1):
        cur = bb_in[l] * rc[l] + gr[l] * low + mm[l] * cur
        full[l + 2] = jnp.where(red, p1[l], cur)
    for l in range(LEV):
        out[l] = full[l + 2, 0:16, :]

    for side in (0, 1):
        near_chip = jnp.maximum(chip - 1, 0) if side == 0 else jnp.minimum(chip + 1, 3)
        there = chip > 0 if side == 0 else chip < 3
        mix = got3[near_chip, 1]
        pack = got3[near_chip, 2]
        w_far = got3[near_chip, 3]
        f_near = got3[near_chip, 4]
        w_near = got2[near_chip, 4 if side == 0 else 3]
        w_own = got2[chip, 3 if side == 0 else 4]
        p_low = u_all[2 * near_chip]
        p_high = u_all[2 * near_chip + 1]
        p_far = jnp.where(red, mix, mix + pack * p_low + north_of(pack) * p_high)
        p_near = p_high if side == 0 else p_low
        p_own = low if side == 0 else high
        w_near = jnp.where(there, w_near, 0.0)
        face_own = vertical_ratio * jnp.sqrt(w_near * w_own)
        face_far = vertical_ratio * jnp.sqrt(w_near * w_far)
        east, north = side_faces(w_near, last_lane)
        fluid = jnp.where(w_near > 0.0, 1.0, 0.0)
        diag = fluid * (
            absorption + (west_of(east) + east + south_of(north) + north) + face_own + face_far
        ) + (1.0 - fluid)
        applied = diag * p_near - (horizontal(east, north, p_near) + face_own * p_own + face_far * p_far)
        beyond = jnp.where(there, f_near - applied, 0.0)
        if side == 0:
            res[0] = beyond
            face_low = face_own
            p_below = p_near
        else:
            res[LEV + 1] = beyond
            face_high = face_own
            p_above = p_near
    for l in range(LEV):
        p = full[l + 2]
        d = dg[l]
        if l == 0:
            d = d + face_low
            vert = face_low * p_below + vf[1] * full[3]
        elif l == LEV - 1:
            d = d + face_high
            vert = vf[l] * full[l + 1] + face_high * p_above
        else:
            vert = vf[l] * full[l + 1] + vf[l + 1] * full[l + 3]
        applied = d * p - (horizontal(ef[l], nf[l], p) + vert)
        res[l + 1] = fr[l] - applied
    for big in range(LEV // 2):
        z = 2 * big
        s = 0.125 * (res[z] + 3.0 * res[z + 1] + 3.0 * res[z + 2] + res[z + 3])
        e = east_of(s)
        s = 0.125 * (west_of(s) + 3.0 * s + 3.0 * e + east_of(e))
        res[z] = jnp.dot(s, weights[...], precision=lax.Precision.HIGHEST, preferred_element_type=F32)
        out[LEV + big] = jnp.concatenate(
            [res[z, pl.ds(0, 8, stride=2), :], jnp.zeros((8, LAN), F32)], axis=0
        )


def last_kernel(both, relaxed, coarse):
    core = lax.axis_index("zk")
    for j in range(2):
        for l in range(8):
            relaxed[l, 16 * j : 16 * j + 16, :] = both[j, core * 8 + l]
        for big in range(4):
            coarse[big, 8 * j : 8 * j + 8, :] = both[j, LEV + core * 4 + big, 0:8, 0:64]


def call(kernel, name, shapes, scratch=(), space=pltpu.VMEM):
    vm = pl.BlockSpec(memory_space=pltpu.VMEM)

    def run(*args):
        return pl.pallas_call(
            kernel,
            out_shape=[jax.ShapeDtypeStruct(s, F32) for s in shapes],
            in_specs=[vm] * len(args),
            out_specs=[vm] * len(shapes),
            scratch_shapes=[pltpu.VMEM(s, F32) for s in scratch],
            name=name,
            interpret=INTERPRET,
        )(*args)

    return run


def restriction_matrix():
    fine = lax.broadcasted_iota(jnp.int32, (LAN, LAN), 0)
    big = lax.broadcasted_iota(jnp.int32, (LAN, LAN), 1)
    off = fine - 2 * big + 1
    inner = (off == 1) | (off == 2)
    outer = (off == 0) | (off == 3)
    return jnp.where(inner, 0.375, jnp.where(outer, 0.125, 0.0)).astype(F32)


def shards(source, conductivity, fluid, pressure):
    cell = (WIN, LAN)
    field = (LEV, WIN, LAN)
    (mine,) = call(weigh_kernel, "weigh", [(3, 8, 32, LAN)])(source, conductivity, fluid, pressure)
    both = lax.all_gather(mine, "zk", axis=0, tiled=False)
    (edge,) = call(edge_kernel, "edge", [(3, LEV, 8, LAN)])(both)
    count = lax.axis_size("xy")
    pairs = [(q, count + q - 1) for q in range(1, count)]
    pairs += [(b, a) for a, b in pairs]
    halo = lax.ppermute(edge, ("zk", "xy"), pairs)
    send2, ef, nf, vf, dg, fr, pr, rc, mm, gr, br, bg = call(
        first_kernel, "first", [(4, 6) + cell] + [field] * 10 + [(4,) + cell]
    )(both, halo)
    got2 = lax.all_to_all(send2, "zc", 0, 0, tiled=False)
    send3, p1, bb, chain, u_red = call(
        second_kernel, "second", [(4, 5) + cell, field, field, (3, 8) + cell, (8,) + cell]
    )(got2, ef, nf, vf, fr, pr, rc, mm, gr, br, bg)
    got3 = lax.all_to_all(send3, "zc", 0, 0, tiled=False)
    (done,) = call(
        third_kernel,
        "third",
        [(LEV + LEV // 2, 16, LAN)],
        [(8,) + cell, (LEV + 4,) + cell, (LEV + 2,) + cell],
    )(got3, got2, ef, nf, vf, dg, fr, rc, mm, gr, bb, p1, chain, u_red, restriction_matrix())
    ends = lax.all_gather(done, "zk", axis=0, tiled=False)
    relaxed, coarse = call(last_kernel, "last", [(8, 32, LAN), (4, 16, LAN // 2)])(ends)
    return relaxed, coarse


def solution(mesh):
    finer = Mesh(mesh.devices.reshape(4, 2, mesh.shape["xy"]), ("zc", "zk", "xy"))
    spec = P(("zc", "zk"), "xy", None)
    return jax.shard_map(shards, mesh=finer, in_specs=(spec,) * 4, out_specs=(spec,) * 2, check_vma=False)
```

time: 189 us -> 65.5 us (0.35)
  the two profiles are of different devices: /device:TPU:33 before, /device:TPU:57 now
where the time goes in v1:
time: 65.5 us; the launch traced here: 64.7 us
  blocking collectives  21.3 us (33%)
  Pallas kernels  14.5 us (22%)
  waiting for transfers between devices  14 us (21%)
  starting transfers between devices  11.4 us (17%)
  local copies, waits for them, and re-layouts  2.08 us (3%)
  between operations  0.66 us (1%)
    all_gather x1, blocking collectives, shards(): ends = lax.all_gather(done, 'zk', axis=0, tiled=False)  14.7 us
    pallas_call x6, Pallas kernels, run(): pl.pallas_call(kernel, out_shape=[jax.ShapeDtypeStruct(s, F32) for s in s...  14.5 us
    all_gather x1, blocking collectives, shards(): both = lax.all_gather(mine, 'zk', axis=0, tiled=False)  6.69 us
    all_to_all x1, waiting for transfers between devices, shards(): got2 = lax.all_to_all(send2, 'zc', 0, 0, tiled=False)  5.7 us
    all_to_all x1, waiting for transfers between devices, shards(): got3 = lax.all_to_all(send3, 'zc', 0, 0, tiled=False)  4.76 us
    all_to_all x1, starting transfers between devices, shards(): got2 = lax.all_to_all(send2, 'zc', 0, 0, tiled=False)  4.02 us
    ppermute x1, starting transfers between devices, shards(): halo = lax.ppermute(edge, ('zk', 'xy'), pairs)  4.01 us
    ppermute x1, waiting for transfers between devices, shards(): halo = lax.ppermute(edge, ('zk', 'xy'), pairs)  3.55 us
  transfers between devices with their start and end apart: 3, of which 3 were waited for; matrix products, arithmetic and copies ran while one was open for 1% of the time, Pallas kernels for 0%

profile of v1, /device:TPU:57, one launch (start us, length us, event | category | flops | bytes accessed | tf_op | source)
XLA Modules:
  0.0 64.7 jit_solution(13628192044890980032)
XLA Ops:
  0.6 1.9 %weigh.1 = f32[3,8,32,128]{3,2,1,0:T(8,128)} custom-call(f32[8,32,128]{2,1,0:T(8,128)} %source.1, f32[8,32,128]{2,1,0:T(8,128)} %cond.1, s32[8,32,128]{2,1,0:T(8,128)} %fluid.1, f32[8,32,128]{2,1,0:T(8,128)} %pressure.1), custom_call_target="tpu_custom_call" | custom-call | tf_op jit(solution)/shard_map/weigh/pallas_call | solution.py:348
  2.5 6.7 %all-gather = f32[6,8,32,128]{3,2,1,0:T(8,128)} all-gather(f32[3,8,32,128]{3,2,1,0:T(8,128)} %weigh.1), channel_id=2, replica_groups=mesh['zc'=4,'zk'=2,'xy'=64] {'zk'}, dimensions={0}, use_global_device_ids=true | all-gather | bytes 1179648 | tf_op jit(solution)/shard_map/all_gather | solution.py:374
  9.2 1.8 %edge.1 = f32[3,16,8,128]{3,2,1,0:T(8,128)} custom-call(f32[2,3,8,32,128]{4,3,2,1,0:T(8,128)} %bitcast.2), custom_call_target="tpu_custom_call" | custom-call | tf_op jit(solution)/shard_map/edge/pallas_call | solution.py:348
  11.0 4.0 %collective-permute-start = (f32[3,16,8,128]{3,2,1,0:T(8,128)}, f32[3,16,8,128]{3,2,1,0:T(8,128)S(1)}, u32[]{:S(2)}, u32[]{:S(2)}) collective-permute-start(f32[3,16,8,128]{3,2,1,0:T(8,128)} %edge.1), channel_id=1, source_target_pairs={{1,64},{2,65},{3,66},{4,67},{5,68},{6,69},{7,70},{8,71},{9,72},{10... | collective-permute-start | bytes 589832 | tf_op jit(solution)/shard_map/ppermute | solution.py:379
  15.1 3.5 %collective-permute-done.halo = f32[3,16,8,128]{3,2,1,0:T(8,128)S(1)} collective-permute-done((f32[3,16,8,128]{3,2,1,0:T(8,128)}, f32[3,16,8,128]{3,2,1,0:T(8,128)S(1)}, u32[]{:S(2)}, u32[]{:S(2)}) %collective-permute-start) | collective-permute-done | bytes 196640 | tf_op jit(solution)/shard_map/ppermute | solution.py:379
  18.6 0.0 copy-start.2
  18.6 0.7 %copy-done.2 = f32[3,16,8,128]{3,2,1,0:T(8,128)} copy-done((f32[3,16,8,128]{3,2,1,0:T(8,128)}, f32[3,16,8,128]{3,2,1,0:T(8,128)S(1)}, u32[]{:S(2)}) %copy-start.2) | copy-done | bytes 196632
  19.3 2.9 %first.1 = (f32[4,6,24,128]{3,2,1,0:T(8,128)}, f32[16,24,128]{2,1,0:T(8,128)}, f32[16,24,128]{2,1,0:T(8,128)}, f32[16,24,128]{2,1,0:T(8,128)}, f32[16,24,128]{2,...) custom-call(f32[2,3,8,32,128]{4,3,2,1,0:T(8,128)} %bitcast.3, ...), custom_call_target="tpu_custom_call" | custom-call | tf_op jit(solution)/shard_map/first/pallas_call | solution.py:348
  22.2 4.0 %all-to-all-start = ((f32[4,6,24,128]{3,2,1,0:T(8,128)}), f32[4,6,24,128]{3,2,1,0:T(8,128)S(1)}, u32[]{:S(2)}, u32[]{:S(2)}) async-start(f32[4,6,24,128]{3,2,1,0:T(8,128)} %get-tuple-element.19), calls=%async_computation | async-start | bytes 589824 | tf_op jit(solution)/shard_map/all_to_all | solution.py:383
  26.2 5.7 %all-to-all-done.got.got2 = f32[4,6,24,128]{3,2,1,0:T(8,128)S(1)} async-done(((f32[4,6,24,128]{3,2,1,0:T(8,128)}), f32[4,6,24,128]{3,2,1,0:T(8,128)S(1)}, u32[]{:S(2)}, u32[]{:S(2)}) %all-to-all-start) | async-done | bytes 294944 | tf_op jit(solution)/shard_map/all_to_all | solution.py:383
  31.9 0.0 copy-start
  31.9 0.7 %copy-done = f32[4,6,24,128]{3,2,1,0:T(8,128)} copy-done((f32[4,6,24,128]{3,2,1,0:T(8,128)}, f32[4,6,24,128]{3,2,1,0:T(8,128)S(1)}, u32[]{:S(2)}) %copy-start) | copy-done | bytes 294936
  32.6 3.0 %second.1 = (f32[4,5,24,128]{3,2,1,0:T(8,128)}, f32[16,24,128]{2,1,0:T(8,128)}, f32[16,24,128]{2,1,0:T(8,128)}, f32[3,8,24,128]{3,2,1,0:T(8,128)}, f32[8,24,128]{2,1,0:T(8,128)}) custom-call(f32[4,6,24,128]{3,2,1,0:T(8,128)} %copy-done, f32[16,24,128]{2,1,0:T(8,128)} %get-tuple-element.20.ef, f32[16,24,128]{2,1,0:T(8,128)} %get-tuple-element.21.nf, ...), custom_call_target="tpu_custom_call" | custom-call | tf_op jit(solution)/shard_map/second/pallas_call | solution.py:348
  35.6 3.4 %all-to-all-start.1 = ((f32[4,5,24,128]{3,2,1,0:T(8,128)}), f32[4,5,24,128]{3,2,1,0:T(8,128)S(1)}, u32[]{:S(2)}, u32[]{:S(2)}) async-start(f32[4,5,24,128]{3,2,1,0:T(8,128)} %get-tuple-element.30), calls=%async_computation.1 | async-start | bytes 491520 | tf_op jit(solution)/shard_map/all_to_all | solution.py:387
  39.0 0.6 %select_select_fusion.weights = f32[128,128]{1,0:T(8,128)} fusion(s32[128]{0:T(128)S(1)} %iota_multiply_fusion), kind=kLoop, calls=%fused_computation | loop fusion | flops 163840 | bytes 66048 | tf_op jit(solution)/shard_map/jit(_where)/select_n | solution.py:367
  39.6 4.8 %all-to-all-done.1.got3 = f32[4,5,24,128]{3,2,1,0:T(8,128)S(1)} async-done(((f32[4,5,24,128]{3,2,1,0:T(8,128)}), f32[4,5,24,128]{3,2,1,0:T(8,128)S(1)}, u32[]{:S(2)}, u32[]{:S(2)}) %all-to-all-start.1) | async-done | bytes 245792 | tf_op jit(solution)/shard_map/all_to_all | solution.py:387
  44.4 0.0 copy-start.1
  44.4 0.7 %copy-done.1 = f32[4,5,24,128]{3,2,1,0:T(8,128)} copy-done((f32[4,5,24,128]{3,2,1,0:T(8,128)}, f32[4,5,24,128]{3,2,1,0:T(8,128)S(1)}, u32[]{:S(2)}) %copy-start.1) | copy-done | bytes 245784
  45.1 3.3 %third.1 = f32[24,16,128]{2,1,0:T(8,128)} custom-call(f32[4,5,24,128]{3,2,1,0:T(8,128)} %copy-done.1, f32[4,6,24,128]{3,2,1,0:T(8,128)} %copy-done, f32[16,24,128]{2,1,0:T(8,128)} %get-tuple-element.20.ef, f32[16,24,128]{2,1,0:T(8,128)} %get-tuple-element.21.nf, f32[16,24,128]{2,1,0:T(8,128)} %get-tuple-element.22.vf, f32[16,24,128]{2,1,0:T(8,128)} %get-tuple-element.31.dg, ...), custom_call_target="tpu_custom_call" | custom-call | tf_op jit(solution)/shard_map/third/pallas_call | solution.py:348
  48.4 14.7 %all-gather.1 = f32[48,16,128]{2,1,0:T(8,128)} all-gather(f32[24,16,128]{2,1,0:T(8,128)} %third.1), channel_id=3, replica_groups=mesh['zc'=4,'zk'=2,'xy'=64] {'zk'}, dimensions={0}, use_global_device_ids=true | all-gather | bytes 589824 | tf_op jit(solution)/shard_map/all_gather | solution.py:394
  63.0 1.7 %last.1 = (f32[8,32,128]{2,1,0:T(8,128)}, f32[4,16,64]{2,1,0:T(8,128)}) custom-call(f32[2,24,16,128]{3,2,1,0:T(8,128)} %bitcast.4), custom_call_target="tpu_custom_call" | custom-call | tf_op jit(solution)/shard_map/last/pallas_call | solution.py:348
  (1 shorter events, 0.0 us)
Async XLA Ops:
  11.0 7.6 %collective-permute-start = (f32[3,16,8,128]{3,2,1,0:T(8,128)}, f32[3,16,8,128]{3,2,1,0:T(8,128)S(1)}, u32[]{:S(2)}, u32[]{:S(2)}) collective-permute-start(f32[3,16,8,128]{3,2,1,0:T(8,128)} %edge.1), channel_id=1, source_target_pairs={{1,64},{2,65},{3,66},{4,67},{5,68},{6,69},{7,70},{8,71},{9,72},{10... | collective-permute-start | bytes 589832 | tf_op jit(solution)/shard_map/ppermute | solution.py:379
  18.6 0.7 %copy-start.2 = (f32[3,16,8,128]{3,2,1,0:T(8,128)}, f32[3,16,8,128]{3,2,1,0:T(8,128)S(1)}, u32[]{:S(2)}) copy-start(f32[3,16,8,128]{3,2,1,0:T(8,128)S(1)} %collective-permute-done.halo) | copy-start | bytes 589828
  22.2 9.7 %all-to-all-start = ((f32[4,6,24,128]{3,2,1,0:T(8,128)}), f32[4,6,24,128]{3,2,1,0:T(8,128)S(1)}, u32[]{:S(2)}, u32[]{:S(2)}) async-start(f32[4,6,24,128]{3,2,1,0:T(8,128)} %get-tuple-element.19), calls=%async_computation | async-start | bytes 589824 | tf_op jit(solution)/shard_map/all_to_all | solution.py:383
  31.9 0.7 %copy-start = (f32[4,6,24,128]{3,2,1,0:T(8,128)}, f32[4,6,24,128]{3,2,1,0:T(8,128)S(1)}, u32[]{:S(2)}) copy-start(f32[4,6,24,128]{3,2,1,0:T(8,128)S(1)} %all-to-all-done.got.got2) | copy-start | bytes 884740
  35.6 8.8 %all-to-all-start.1 = ((f32[4,5,24,128]{3,2,1,0:T(8,128)}), f32[4,5,24,128]{3,2,1,0:T(8,128)S(1)}, u32[]{:S(2)}, u32[]{:S(2)}) async-start(f32[4,5,24,128]{3,2,1,0:T(8,128)} %get-tuple-element.30), calls=%async_computation.1 | async-start | bytes 491520 | tf_op jit(solution)/shard_map/all_to_all | solution.py:387
  44.4 0.7 %copy-start.1 = (f32[4,5,24,128]{3,2,1,0:T(8,128)}, f32[4,5,24,128]{3,2,1,0:T(8,128)S(1)}, u32[]{:S(2)}) copy-start(f32[4,5,24,128]{3,2,1,0:T(8,128)S(1)} %all-to-all-done.1.got3) | copy-start | bytes 737284

commit v2 on v1

--- a/solution.py
+++ b/solution.py
@@ -7,6 +7,7 @@
 from jax.sharding import PartitionSpec as P
 
 INTERPRET = False
+SCOPED = 4 << 20
 vertical_ratio = 100.0
 absorption = 0.05
 
@@ -341,17 +342,21 @@
             coarse[big, 8 * j : 8 * j + 8, :] = both[j, LEV + core * 4 + big, 0:8, 0:64]
 
 
-def call(kernel, name, shapes, scratch=(), space=pltpu.VMEM):
+def call(kernel, name, shapes, scratch=(), ends=""):
     vm = pl.BlockSpec(memory_space=pltpu.VMEM)
 
     def run(*args):
+        if ends != "first" and not INTERPRET:
+            args = [pltpu.with_memory_space_constraint(a, pltpu.VMEM) for a in args]
+        plain = ends == "last" or INTERPRET
         return pl.pallas_call(
             kernel,
-            out_shape=[jax.ShapeDtypeStruct(s, F32) for s in shapes],
+            out_shape=[jax.ShapeDtypeStruct(s, F32) if plain else pltpu.VMEM(s, F32) for s in shapes],
             in_specs=[vm] * len(args),
             out_specs=[vm] * len(shapes),
             scratch_shapes=[pltpu.VMEM(s, F32) for s in scratch],
             name=name,
+            compiler_params=pltpu.CompilerParams(vmem_limit_bytes=SCOPED),
             interpret=INTERPRET,
         )(*args)
 
@@ -370,7 +375,7 @@
 def shards(source, conductivity, fluid, pressure):
     cell = (WIN, LAN)
     field = (LEV, WIN, LAN)
-    (mine,) = call(weigh_kernel, "weigh", [(3, 8, 32, LAN)])(source, conductivity, fluid, pressure)
+    (mine,) = call(weigh_kernel, "weigh", [(3, 8, 32, LAN)], ends="first")(source, conductivity, fluid, pressure)
     both = lax.all_gather(mine, "zk", axis=0, tiled=False)
     (edge,) = call(edge_kernel, "edge", [(3, LEV, 8, LAN)])(both)
     count = lax.axis_size("xy")
@@ -392,7 +397,7 @@
         [(8,) + cell, (LEV + 4,) + cell, (LEV + 2,) + cell],
     )(got3, got2, ef, nf, vf, dg, fr, rc, mm, gr, bb, p1, chain, u_red, restriction_matrix())
     ends = lax.all_gather(done, "zk", axis=0, tiled=False)
-    relaxed, coarse = call(last_kernel, "last", [(8, 32, LAN), (4, 16, LAN // 2)])(ends)
+    relaxed, coarse = call(last_kernel, "last", [(8, 32, LAN), (4, 16, LAN // 2)], ends="last")(ends)
     return relaxed, coarse
 
 

time: 65.5 us -> 49.2 us (0.75)
  Pallas kernels: 14.5 us -> 3.93 us
  blocking collectives: 21.3 us -> 14.5 us
  local copies, waits for them, and re-layouts: 2.08 us -> 3.61 us
    pallas_call x6, Pallas kernels: 14.5 us -> 3.93 us  [run(): pl.pallas_call(kernel, out_shape=[jax.ShapeDtypeStruct(s, F32) if plain e...]
    all_gather x1, blocking collectives: 6.69 us -> 2.67 us  [shards(): both = lax.all_gather(mine, 'zk', axis=0, tiled=False)]
    all_gather x1, blocking collectives: 14.7 us -> 11.9 us  [shards(): ends = lax.all_gather(done, 'zk', axis=0, tiled=False)]
    unnamed x6 -> x8, local copies, waits for them, and re-layouts: 2.08 us -> 3.61 us
  transfers between devices with their start and end apart: 3 -> 3, of which waited for: 3 -> 3; matrix products, arithmetic and copies ran while one was open for 1% -> 0% of each run, Pallas kernels for 0% -> 0%
where the time goes in v2:
time: 49.2 us; the launch traced here: 48.9 us
  blocking collectives  14.5 us (29%)
  waiting for transfers between devices  14.4 us (29%)
  starting transfers between devices  11.7 us (24%)
  Pallas kernels  3.93 us (8%)
  local copies, waits for them, and re-layouts  3.61 us (7%)
  between operations  0.68 us (1%)
    all_gather x1, blocking collectives, shards(): ends = lax.all_gather(done, 'zk', axis=0, tiled=False)  11.9 us
    all_to_all x1, waiting for transfers between devices, shards(): got2 = lax.all_to_all(send2, 'zc', 0, 0, tiled=False)  5.7 us
    all_to_all x1, waiting for transfers between devices, shards(): got3 = lax.all_to_all(send3, 'zc', 0, 0, tiled=False)  5.37 us
    ppermute x1, starting transfers between devices, shards(): halo = lax.ppermute(edge, ('zk', 'xy'), pairs)  4.26 us
    all_to_all x1, starting transfers between devices, shards(): got2 = lax.all_to_all(send2, 'zc', 0, 0, tiled=False)  4.01 us
    pallas_call x6, Pallas kernels, run(): pl.pallas_call(kernel, out_shape=[jax.ShapeDtypeStruct(s, F32) if plain e...  3.93 us
    unnamed x8, local copies, waits for them, and re-layouts  3.61 us
    all_to_all x1, starting transfers between devices, shards(): got3 = lax.all_to_all(send3, 'zc', 0, 0, tiled=False)  3.39 us
  transfers between devices with their start and end apart: 3, of which 3 were waited for; matrix products, arithmetic and copies ran while one was open for 0% of the time, Pallas kernels for 0%

profile of v2, /device:TPU:57, one launch (start us, length us, event | category | flops | bytes accessed | tf_op | source)
XLA Modules:
  0.0 48.9 jit_solution(18251046290594145399)
XLA Ops:
  0.6 0.0 copy-start
  0.6 0.9 %copy-done = f32[8,32,128]{2,1,0:T(8,128)S(1)} copy-done((f32[8,32,128]{2,1,0:T(8,128)S(1)}, f32[8,32,128]{2,1,0:T(8,128)}, u32[]{:S(2)}) %copy-start) | copy-done | bytes 131096
  1.5 0.0 copy-start.1
  1.5 0.9 %copy-done.1 = f32[8,32,128]{2,1,0:T(8,128)S(1)} copy-done((f32[8,32,128]{2,1,0:T(8,128)S(1)}, f32[8,32,128]{2,1,0:T(8,128)}, u32[]{:S(2)}) %copy-start.1) | copy-done | bytes 131096
  2.4 0.0 copy-start.2
  2.4 0.9 %copy-done.2 = s32[8,32,128]{2,1,0:T(8,128)S(1)} copy-done((s32[8,32,128]{2,1,0:T(8,128)S(1)}, s32[8,32,128]{2,1,0:T(8,128)}, u32[]{:S(2)}) %copy-start.2) | copy-done | bytes 131096
  3.3 0.0 copy-start.3
  3.3 0.9 %copy-done.3 = f32[8,32,128]{2,1,0:T(8,128)S(1)} copy-done((f32[8,32,128]{2,1,0:T(8,128)S(1)}, f32[8,32,128]{2,1,0:T(8,128)}, u32[]{:S(2)}) %copy-start.3) | copy-done | bytes 131096
  4.3 2.7 %all-gather = f32[6,8,32,128]{3,2,1,0:T(8,128)S(1)} all-gather(f32[3,8,32,128]{3,2,1,0:T(8,128)S(1)} %weigh.1), channel_id=2, replica_groups=mesh['zc'=4,'zk'=2,'xy'=64] {'zk'}, dimensions={0}, use_global_device_ids=true | all-gather | bytes 1179648 | tf_op jit(solution)/shard_map/all_gather | solution.py:379
  7.0 4.3 %collective-permute-start = (f32[3,16,8,128]{3,2,1,0:T(8,128)S(1)}, f32[3,16,8,128]{3,2,1,0:T(8,128)S(1)}, u32[]{:S(2)}, u32[]{:S(2)}) collective-permute-start(f32[3,16,8,128]{3,2,1,0:T(8,128)S(1)} %edge.1), channel_id=1, source_target_pairs={{1,64},{2,65},{3,66},{4,67},{5,68},{6,69},{7,70},{8,71},{9,72},{10... | collective-permute-start | bytes 589832 | tf_op jit(solution)/shard_map/ppermute | solution.py:384
  11.3 3.3 %collective-permute-done.halo = f32[3,16,8,128]{3,2,1,0:T(8,128)S(1)} collective-permute-done((f32[3,16,8,128]{3,2,1,0:T(8,128)S(1)}, f32[3,16,8,128]{3,2,1,0:T(8,128)S(1)}, u32[]{:S(2)}, u32[]{:S(2)}) %collective-permute-start) | collective-permute-done | bytes 196640 | tf_op jit(solution)/shard_map/ppermute | solution.py:384
  14.6 1.3 %first.1 = (f32[4,6,24,128]{3,2,1,0:T(8,128)}, f32[16,24,128]{2,1,0:T(8,128)S(1)}, f32[16,24,128]{2,1,0:T(8,128)S(1)}, f32[16,24,128]{2,1,0:T(8,128)S(1)}, f32[1...) custom-call(f32[2,3,8,32,128]{4,3,2,1,0:T(8,128)S(1)} %bitcast.3, ...), custom_call_target="tpu_custom_call" | custom-call | tf_op jit(solution)/shard_map/first/pallas_call | solution.py:352
  15.9 4.0 %all-to-all-start = ((f32[4,6,24,128]{3,2,1,0:T(8,128)}), f32[4,6,24,128]{3,2,1,0:T(8,128)S(1)}, u32[]{:S(2)}, u32[]{:S(2)}) async-start(f32[4,6,24,128]{3,2,1,0:T(8,128)} %get-tuple-element.19), calls=%async_computation | async-start | bytes 589824 | tf_op jit(solution)/shard_map/all_to_all | solution.py:388
  19.9 5.7 %all-to-all-done.got.got2 = f32[4,6,24,128]{3,2,1,0:T(8,128)S(1)} async-done(((f32[4,6,24,128]{3,2,1,0:T(8,128)}), f32[4,6,24,128]{3,2,1,0:T(8,128)S(1)}, u32[]{:S(2)}, u32[]{:S(2)}) %all-to-all-start) | async-done | bytes 294944 | tf_op jit(solution)/shard_map/all_to_all | solution.py:388
  25.6 1.1 %second.1 = (f32[4,5,24,128]{3,2,1,0:T(8,128)}, f32[16,24,128]{2,1,0:T(8,128)S(1)}, f32[16,24,128]{2,1,0:T(8,128)S(1)}, f32[3,8,24,128]{3,2,1,0:T(8,128)S(1)}, f32[8,24,128]{2,1,0:T(8,128)S(1)}) custom-call(f32[4,6,24,128]{3,2,1,0:T(8,128)S(1)} %all-to-all-done.got.got2, f32[16,24,128]{2,1,0:T(8,128)S(1)} %get-tuple-element.20.ef, ...), custom_call_target="tpu_custom_call" | custom-call | tf_op jit(solution)/shard_map/second/pallas_call | solution.py:352
  26.7 3.4 %all-to-all-start.1 = ((f32[4,5,24,128]{3,2,1,0:T(8,128)}), f32[4,5,24,128]{3,2,1,0:T(8,128)S(1)}, u32[]{:S(2)}, u32[]{:S(2)}) async-start(f32[4,5,24,128]{3,2,1,0:T(8,128)} %get-tuple-element.30), calls=%async_computation.1 | async-start | bytes 491520 | tf_op jit(solution)/shard_map/all_to_all | solution.py:392
  30.2 5.4 %all-to-all-done.1.got3 = f32[4,5,24,128]{3,2,1,0:T(8,128)S(1)} async-done(((f32[4,5,24,128]{3,2,1,0:T(8,128)}), f32[4,5,24,128]{3,2,1,0:T(8,128)S(1)}, u32[]{:S(2)}, u32[]{:S(2)}) %all-to-all-start.1) | async-done | bytes 245792 | tf_op jit(solution)/shard_map/all_to_all | solution.py:392
  35.5 0.8 %third.1 = f32[24,16,128]{2,1,0:T(8,128)S(1)} custom-call(f32[4,5,24,128]{3,2,1,0:T(8,128)S(1)} %all-to-all-done.1.got3, f32[4,6,24,128]{3,2,1,0:T(8,128)S(1)} %all-to-all-done.got.got2, f32[16,24,128]{2,1,0:T(8,128)S(1)} %get-tuple-element.20.ef, f32[16,24,128]{2,1,0:T(8,128)S(1)} %get-tuple-element.21.nf, f32[16,24,128]{2,1,0:T(8,128)S(1)} %get-tuple-element.22.vf, ...), custom_call_target="tpu_custom_call" | custom-call | tf_op jit(solution)/shard_map/third/pallas_call | solution.py:352
  36.3 11.9 %all-gather.1 = f32[48,16,128]{2,1,0:T(8,128)S(1)} all-gather(f32[24,16,128]{2,1,0:T(8,128)S(1)} %third.1), channel_id=3, replica_groups=mesh['zc'=4,'zk'=2,'xy'=64] {'zk'}, dimensions={0}, use_global_device_ids=true | all-gather | bytes 589824 | tf_op jit(solution)/shard_map/all_gather | solution.py:399
  48.2 0.7 %last.1 = (f32[8,32,128]{2,1,0:T(8,128)}, f32[4,16,64]{2,1,0:T(8,128)}) custom-call(f32[2,24,16,128]{3,2,1,0:T(8,128)S(1)} %bitcast.4), custom_call_target="tpu_custom_call" | custom-call | tf_op jit(solution)/shard_map/last/pallas_call | solution.py:352
  (4 shorter events, 0.1 us)
Async XLA Ops:
  0.6 0.9 %copy-start = (f32[8,32,128]{2,1,0:T(8,128)S(1)}, f32[8,32,128]{2,1,0:T(8,128)}, u32[]{:S(2)}) copy-start(f32[8,32,128]{2,1,0:T(8,128)} %source.1) | copy-start | bytes 393220
  1.5 0.9 %copy-start.1 = (f32[8,32,128]{2,1,0:T(8,128)S(1)}, f32[8,32,128]{2,1,0:T(8,128)}, u32[]{:S(2)}) copy-start(f32[8,32,128]{2,1,0:T(8,128)} %cond.1) | copy-start | bytes 393220
  2.4 0.9 %copy-start.2 = (s32[8,32,128]{2,1,0:T(8,128)S(1)}, s32[8,32,128]{2,1,0:T(8,128)}, u32[]{:S(2)}) copy-start(s32[8,32,128]{2,1,0:T(8,128)} %fluid.1) | copy-start | bytes 393220
  3.3 0.9 %copy-start.3 = (f32[8,32,128]{2,1,0:T(8,128)S(1)}, f32[8,32,128]{2,1,0:T(8,128)}, u32[]{:S(2)}) copy-start(f32[8,32,128]{2,1,0:T(8,128)} %pressure.1) | copy-start | bytes 393220
  7.0 7.6 %collective-permute-start = (f32[3,16,8,128]{3,2,1,0:T(8,128)S(1)}, f32[3,16,8,128]{3,2,1,0:T(8,128)S(1)}, u32[]{:S(2)}, u32[]{:S(2)}) collective-permute-start(f32[3,16,8,128]{3,2,1,0:T(8,128)S(1)} %edge.1), channel_id=1, source_target_pairs={{1,64},{2,65},{3,66},{4,67},{5,68},{6,69},{7,70},{8,71},{9,72},{10... | collective-permute-start | bytes 589832 | tf_op jit(solution)/shard_map/ppermute | solution.py:384
  15.9 9.7 %all-to-all-start = ((f32[4,6,24,128]{3,2,1,0:T(8,128)}), f32[4,6,24,128]{3,2,1,0:T(8,128)S(1)}, u32[]{:S(2)}, u32[]{:S(2)}) async-start(f32[4,6,24,128]{3,2,1,0:T(8,128)} %get-tuple-element.19), calls=%async_computation | async-start | bytes 589824 | tf_op jit(solution)/shard_map/all_to_all | solution.py:388
  26.7 8.8 %all-to-all-start.1 = ((f32[4,5,24,128]{3,2,1,0:T(8,128)}), f32[4,5,24,128]{3,2,1,0:T(8,128)S(1)}, u32[]{:S(2)}, u32[]{:S(2)}) async-start(f32[4,5,24,128]{3,2,1,0:T(8,128)} %get-tuple-element.30), calls=%async_computation.1 | async-start | bytes 491520 | tf_op jit(solution)/shard_map/all_to_all | solution.py:392

commit v3 on v1

--- a/solution.py
+++ b/solution.py
@@ -7,10 +7,12 @@
 from jax.sharding import PartitionSpec as P
 
 INTERPRET = False
+SCOPED = 4 << 20
 vertical_ratio = 100.0
 absorption = 0.05
 
 LEV = 16
+HALF = 8
 WIN = 24
 LAN = 128
 F32 = jnp.float32
@@ -54,22 +56,34 @@
     )
 
 
-def weigh_kernel(source, cond, fluid, pressure, out):
-    real = fluid[...].astype(F32)
-    out[0] = cond[...] * real
-    out[1] = real * source[...]
-    out[2] = pressure[...]
-
-
-def edge_kernel(both, out):
+def weigh_kernel(source, cond, fluid, pressure, out, cross, along, source_v, cond_v, fluid_v, sems):
     core = lax.axis_index("zk")
-    start = pl.multiple_of(core * 24, 8)
-    for f in range(3):
-        for l in range(LEV):
-            out[f, l] = both[l // 8, f, l % 8, pl.ds(start, 8), :]
-
-
-def first_kernel(both, halo, send, ef, nf, vf, dg, fr, pr, rc, mm, gr, br, bg):
+    copies = [
+        pltpu.make_async_copy(cond, cond_v, sems.at[0]),
+        pltpu.make_async_copy(fluid, fluid_v, sems.at[1]),
+        pltpu.make_async_copy(source, source_v, sems.at[2]),
+        pltpu.make_async_copy(pressure, out.at[2], sems.at[3]),
+    ]
+    for copy in copies:
+        copy.start()
+    for copy in copies:
+        copy.wait()
+    for l in range(HALF):
+        real = fluid_v[l].astype(F32)
+        out[0, l] = cond_v[l] * real
+        out[1, l] = real * source_v[l]
+    row8 = lax.broadcasted_iota(jnp.int32, (8, LAN), 0)
+    for ref, high in ((cross, core), (along, 1 - core)):
+        start = pl.multiple_of(high * 24, 8)
+        keep = (row8 < 4) == (high == 0)
+        for f in range(3):
+            for l in range(4):
+                one = out[f, l, pl.ds(start, 8), :]
+                two = out[f, l + 4, pl.ds(start, 8), :]
+                ref[f, l] = jnp.where(keep, one, pltpu.roll(two, 4, 0))
+
+
+def first_kernel(both, cross, along, send, ef, nf, vf, dg, fr, pr, rc, mm, gr, br, bg):
     core = lax.axis_index("zk")
     row, lane, red = iotas()
     last_lane = lane == LAN - 1
@@ -81,7 +95,11 @@
     def window(f, l):
         own = both[l // 8, f, l % 8, pl.ds(own_at, 16), :]
         near = both[l // 8, f, l % 8, pl.ds(near_at, 8), :]
-        return jnp.concatenate([own, jnp.where(from_near, near, halo[f, l])], axis=0)
+        straight = core == l // 8
+        far = jnp.where(straight, along[f, l % 4], cross[f, l % 4])
+        if l % 8 >= 4:
+            far = pltpu.roll(far, 4, 0)
+        return jnp.concatenate([own, jnp.where(from_near, near, far)], axis=0)
 
     w = None
     below = None
@@ -134,11 +152,13 @@
             top_b = top_b + grl * bb
     beta = gr[LEV - 2]
     gamma = mm[LEV - 2]
-    bg[0] = jnp.where(red, south_of(gamma), beta)
+    far = vf[LEV - 1]
+    bg[0] = jnp.where(red, south_of(far * gamma), far * beta)
     for l in range(LEV - 3, 0, -1):
         beta = gr[l] + mm[l] * beta
         gamma = mm[l] * gamma
-    bg[1] = jnp.where(red, south_of(gamma), beta)
+    far = vf[1]
+    bg[1] = jnp.where(red, south_of(far * gamma), far * beta)
     packed = jnp.where(red, top_b, south_of(bb))
     for peer in range(4):
         send[peer, 0] = top_d
@@ -147,8 +167,6 @@
         send[peer, 3] = w0
         send[peer, 4] = w15
         send[peer, 5] = packed
-    bg[2] = window(0, LEV - 2)
-    bg[3] = window(0, 1)
 
 
 def chain_solve(rj, mj, cj, right):
@@ -231,8 +249,8 @@
     for l in range(LEV - 3, 0, -1):
         alpha = bb_out[l] * rc[l] + mm[l] * alpha
     packed = jnp.where(red, south_of(bb), top_b)
-    up_mix = jnp.where(red, p1[LEV - 2], alpha14)
-    down_mix = jnp.where(red, p1[1], alpha)
+    up_mix = fr[LEV - 1] + vf[LEV - 1] * jnp.where(red, p1[LEV - 2], alpha14)
+    down_mix = fr[0] + vf[1] * jnp.where(red, p1[1], alpha)
     for peer in range(4):
         send[peer, 0] = packed
 
@@ -240,18 +258,16 @@
         def _():
             send[peer, 1] = up_mix
             send[peer, 2] = bg[0]
-            send[peer, 3] = bg[2]
-            send[peer, 4] = fr[LEV - 1]
+            send[peer, 3] = vf[LEV - 1]
 
         @pl.when(chip >= peer)
         def _():
             send[peer, 1] = down_mix
             send[peer, 2] = bg[1]
-            send[peer, 3] = bg[3]
-            send[peer, 4] = fr[0]
-
-
-def third_kernel(got3, got2, ef, nf, vf, dg, fr, rc, mm, gr, bb_in, p1, chain, u_red, weights, out, u_all, full, res):
+            send[peer, 3] = vf[1]
+
+
+def third_kernel(got3, got2, ef, nf, vf, dg, fr, rc, mm, gr, bb_in, p1, chain, u_red, out, u_all, full, res):
     chip = lax.axis_index("zc")
     row, lane, red = iotas()
     last_lane = lane == LAN - 1
@@ -281,25 +297,23 @@
         there = chip > 0 if side == 0 else chip < 3
         mix = got3[near_chip, 1]
         pack = got3[near_chip, 2]
-        w_far = got3[near_chip, 3]
-        f_near = got3[near_chip, 4]
+        face_far = got3[near_chip, 3]
         w_near = got2[near_chip, 4 if side == 0 else 3]
         w_own = got2[chip, 3 if side == 0 else 4]
         p_low = u_all[2 * near_chip]
         p_high = u_all[2 * near_chip + 1]
-        p_far = jnp.where(red, mix, mix + pack * p_low + north_of(pack) * p_high)
+        inside = jnp.where(red, mix, mix + pack * p_low + north_of(pack) * p_high)
         p_near = p_high if side == 0 else p_low
         p_own = low if side == 0 else high
         w_near = jnp.where(there, w_near, 0.0)
         face_own = vertical_ratio * jnp.sqrt(w_near * w_own)
-        face_far = vertical_ratio * jnp.sqrt(w_near * w_far)
         east, north = side_faces(w_near, last_lane)
         fluid = jnp.where(w_near > 0.0, 1.0, 0.0)
         diag = fluid * (
             absorption + (west_of(east) + east + south_of(north) + north) + face_own + face_far
         ) + (1.0 - fluid)
-        applied = diag * p_near - (horizontal(east, north, p_near) + face_own * p_own + face_far * p_far)
-        beyond = jnp.where(there, f_near - applied, 0.0)
+        beyond = inside - (diag * p_near - (horizontal(east, north, p_near) + face_own * p_own))
+        beyond = jnp.where(there, beyond, 0.0)
         if side == 0:
             res[0] = beyond
             face_low = face_own
@@ -321,12 +335,13 @@
             vert = vf[l] * full[l + 1] + vf[l + 1] * full[l + 3]
         applied = d * p - (horizontal(ef[l], nf[l], p) + vert)
         res[l + 1] = fr[l] - applied
+    weights = restriction_matrix()
     for big in range(LEV // 2):
         z = 2 * big
         s = 0.125 * (res[z] + 3.0 * res[z + 1] + 3.0 * res[z + 2] + res[z + 3])
         e = east_of(s)
         s = 0.125 * (west_of(s) + 3.0 * s + 3.0 * e + east_of(e))
-        res[z] = jnp.dot(s, weights[...], precision=lax.Precision.HIGHEST, preferred_element_type=F32)
+        res[z] = jnp.dot(s, weights, precision=lax.Precision.HIGHEST, preferred_element_type=F32)
         out[LEV + big] = jnp.concatenate(
             [res[z, pl.ds(0, 8, stride=2), :], jnp.zeros((8, LAN), F32)], axis=0
         )
@@ -341,23 +356,6 @@
             coarse[big, 8 * j : 8 * j + 8, :] = both[j, LEV + core * 4 + big, 0:8, 0:64]
 
 
-def call(kernel, name, shapes, scratch=(), space=pltpu.VMEM):
-    vm = pl.BlockSpec(memory_space=pltpu.VMEM)
-
-    def run(*args):
-        return pl.pallas_call(
-            kernel,
-            out_shape=[jax.ShapeDtypeStruct(s, F32) for s in shapes],
-            in_specs=[vm] * len(args),
-            out_specs=[vm] * len(shapes),
-            scratch_shapes=[pltpu.VMEM(s, F32) for s in scratch],
-            name=name,
-            interpret=INTERPRET,
-        )(*args)
-
-    return run
-
-
 def restriction_matrix():
     fine = lax.broadcasted_iota(jnp.int32, (LAN, LAN), 0)
     big = lax.broadcasted_iota(jnp.int32, (LAN, LAN), 1)
@@ -367,32 +365,65 @@
     return jnp.where(inner, 0.375, jnp.where(outer, 0.125, 0.0)).astype(F32)
 
 
+def call(kernel, name, shapes, scratch=(), ends=""):
+    vm = pl.BlockSpec(memory_space=pltpu.VMEM)
+    main = pl.BlockSpec(memory_space=pltpu.HBM)
+
+    def run(*args):
+        if not INTERPRET:
+            space = pltpu.HBM if ends == "first" else pltpu.VMEM
+            args = [pltpu.with_memory_space_constraint(a, space) for a in args]
+        plain = ends == "last" or INTERPRET
+        return pl.pallas_call(
+            kernel,
+            out_shape=[jax.ShapeDtypeStruct(s, F32) if plain else pltpu.VMEM(s, F32) for s in shapes],
+            in_specs=[main if ends == "first" else vm] * len(args),
+            out_specs=[vm] * len(shapes),
+            scratch_shapes=scratch,
+            name=name,
+            compiler_params=pltpu.CompilerParams(vmem_limit_bytes=SCOPED),
+            interpret=INTERPRET,
+        )(*args)
+
+    return run
+
+
 def shards(source, conductivity, fluid, pressure):
     cell = (WIN, LAN)
     field = (LEV, WIN, LAN)
-    (mine,) = call(weigh_kernel, "weigh", [(3, 8, 32, LAN)])(source, conductivity, fluid, pressure)
+    block = (HALF, 32, LAN)
+    edge = (3, 4, 8, LAN)
+    vmem = pltpu.VMEM
+    mine, cross, along = call(
+        weigh_kernel,
+        "weigh",
+        [(3,) + block, edge, edge],
+        [vmem(block, F32), vmem(block, F32), vmem(block, jnp.int32), pltpu.SemaphoreType.DMA((4,))],
+        ends="first",
+    )(source, conductivity, fluid, pressure)
+    count = lax.axis_size("xy")
+    swap = [(q, count + q - 1) for q in range(1, count)]
+    swap += [(b, a) for a, b in swap]
+    shift = [(q, q + 1) for q in range(count - 1)] + [(count + q + 1, count + q) for q in range(count - 1)]
+    cross = lax.ppermute(cross, ("zk", "xy"), swap)
+    along = lax.ppermute(along, ("zk", "xy"), shift)
     both = lax.all_gather(mine, "zk", axis=0, tiled=False)
-    (edge,) = call(edge_kernel, "edge", [(3, LEV, 8, LAN)])(both)
-    count = lax.axis_size("xy")
-    pairs = [(q, count + q - 1) for q in range(1, count)]
-    pairs += [(b, a) for a, b in pairs]
-    halo = lax.ppermute(edge, ("zk", "xy"), pairs)
     send2, ef, nf, vf, dg, fr, pr, rc, mm, gr, br, bg = call(
-        first_kernel, "first", [(4, 6) + cell] + [field] * 10 + [(4,) + cell]
-    )(both, halo)
+        first_kernel, "first", [(4, 6) + cell] + [field] * 10 + [(2,) + cell]
+    )(both, cross, along)
     got2 = lax.all_to_all(send2, "zc", 0, 0, tiled=False)
     send3, p1, bb, chain, u_red = call(
-        second_kernel, "second", [(4, 5) + cell, field, field, (3, 8) + cell, (8,) + cell]
+        second_kernel, "second", [(4, 4) + cell, field, field, (3, 8) + cell, (8,) + cell]
     )(got2, ef, nf, vf, fr, pr, rc, mm, gr, br, bg)
     got3 = lax.all_to_all(send3, "zc", 0, 0, tiled=False)
     (done,) = call(
         third_kernel,
         "third",
         [(LEV + LEV // 2, 16, LAN)],
-        [(8,) + cell, (LEV + 4,) + cell, (LEV + 2,) + cell],
-    )(got3, got2, ef, nf, vf, dg, fr, rc, mm, gr, bb, p1, chain, u_red, restriction_matrix())
+        [vmem((8,) + cell, F32), vmem((LEV + 4,) + cell, F32), vmem((LEV + 2,) + cell, F32)],
+    )(got3, got2, ef, nf, vf, dg, fr, rc, mm, gr, bb, p1, chain, u_red)
     ends = lax.all_gather(done, "zk", axis=0, tiled=False)
-    relaxed, coarse = call(last_kernel, "last", [(8, 32, LAN), (4, 16, LAN // 2)])(ends)
+    relaxed, coarse = call(last_kernel, "last", [block, (4, 16, LAN // 2)], ends="last")(ends)
     return relaxed, coarse
 
 

time: 65.5 us -> 46.3 us (0.71)
  waiting for transfers between devices: 14 us -> 0.01 us
  Pallas kernels: 14.5 us -> 3.76 us
  blocking collectives: 21.3 us -> 27.9 us
  local copies, waits for them, and re-layouts: 2.08 us -> 0 us
  starting transfers between devices: 11.4 us -> 13.4 us
    all_to_all x0 -> x2, blocking collectives: none -> 17.1 us  [the longest x1 9.52 us: shards(): got2 = lax.all_to_all(send2, 'zc', 0, 0, tiled=False)]
    pallas_call x6 -> x5, Pallas kernels: 14.5 us -> 3.76 us  [run(): pl.pallas_call(kernel, out_shape=[jax.ShapeDtypeStruct(s, F32) if plain e...]
    all_to_all x2 -> x0, waiting for transfers between devices: 10.5 us -> none  [the longest x1 5.7 us: shards(): got2 = lax.all_to_all(send2, 'zc', 0, 0, tiled=False)]
    ppermute x1 -> x2, starting transfers between devices: 4.01 us -> 13.4 us  [the longest x1 8.81 us: shards(): along = lax.ppermute(along, ('zk', 'xy'), shift)]
    all_to_all x2 -> x0, starting transfers between devices: 7.42 us -> none  [the longest x1 4.02 us: shards(): got2 = lax.all_to_all(send2, 'zc', 0, 0, tiled=False)]
    all_gather x1, blocking collectives: 14.7 us -> 8.45 us  [shards(): ends = lax.all_gather(done, 'zk', axis=0, tiled=False)]
    all_gather x1, blocking collectives: 6.69 us -> 2.39 us  [shards(): both = lax.all_gather(mine, 'zk', axis=0, tiled=False)]
    ppermute x1 -> x2, waiting for transfers between devices: 3.55 us -> 0.01 us  [the longest x1 0.01 us: shards(): cross = lax.ppermute(cross, ('zk', 'xy'), swap)]
  transfers between devices with their start and end apart: 3 -> 2, of which waited for: 3 -> 0; matrix products, arithmetic and copies ran while one was open for 1% -> 0% of each run, Pallas kernels for 0% -> 0%
where the time goes in v3:
time: 46.3 us; the launch traced here: 45.7 us
  blocking collectives  27.9 us (60%)
  starting transfers between devices  13.4 us (29%)
  Pallas kernels  3.76 us (8%)
  between operations  0.67 us (1%)
    all_to_all x1, blocking collectives, shards(): got2 = lax.all_to_all(send2, 'zc', 0, 0, tiled=False)  9.52 us
    ppermute x1, starting transfers between devices, shards(): along = lax.ppermute(along, ('zk', 'xy'), shift)  8.81 us
    all_gather x1, blocking collectives, shards(): ends = lax.all_gather(done, 'zk', axis=0, tiled=False)  8.45 us
    all_to_all x1, blocking collectives, shards(): got3 = lax.all_to_all(send3, 'zc', 0, 0, tiled=False)  7.54 us
    ppermute x1, starting transfers between devices, shards(): cross = lax.ppermute(cross, ('zk', 'xy'), swap)  4.56 us
    pallas_call x5, Pallas kernels, run(): pl.pallas_call(kernel, out_shape=[jax.ShapeDtypeStruct(s, F32) if plain e...  3.76 us
    all_gather x1, blocking collectives, shards(): both = lax.all_gather(mine, 'zk', axis=0, tiled=False)  2.39 us
  transfers between devices with their start and end apart: 2, of which 0 were waited for; matrix products, arithmetic and copies ran while one was open for 0% of the time, Pallas kernels for 0%

profile of v3, /device:TPU:57, one launch (start us, length us, event | category | flops | bytes accessed | tf_op | source)
XLA Modules:
  0.0 45.7 jit_solution(10113555795705600258)
XLA Ops:
  0.6 1.2 %weigh.1 = (f32[3,8,32,128]{3,2,1,0:T(8,128)S(1)}, f32[3,4,8,128]{3,2,1,0:T(8,128)S(1)}, f32[3,4,8,128]{3,2,1,0:T(8,128)S(1)}) custom-call(f32[8,32,128]{2,1,0:T(8,128)} %source.1, f32[8,32,128]{2,1,0:T(8,128)} %cond.1, s32[8,32,128]{2,1,0:T(8,128)} %fluid.1, f32[8,32,128]{2,1,0:T(8,128)} %pressure.1), custom_call_target="tpu_custom_call" | custom-call | tf_op jit(solution)/shard_map/weigh/pallas_call | solution.py:377
  1.8 4.6 %collective-permute-start = (f32[3,4,8,128]{3,2,1,0:T(8,128)S(1)}, f32[3,4,8,128]{3,2,1,0:T(8,128)S(1)}, u32[]{:S(2)}, u32[]{:S(2)}) collective-permute-start(f32[3,4,8,128]{3,2,1,0:T(8,128)S(1)} %get-tuple-element.23), channel_id=1, source_target_pairs={{1,64},{2,65},{3,66},{4,67},{5,68},{6,69},{7,70},{8,71},{9,72},{10... | collective-permute-start | bytes 147464 | tf_op jit(solution)/shard_map/ppermute | solution.py:408
  6.4 8.8 %collective-permute-start.1 = (f32[3,4,8,128]{3,2,1,0:T(8,128)S(1)}, f32[3,4,8,128]{3,2,1,0:T(8,128)S(1)}, u32[]{:S(2)}, u32[]{:S(2)}) collective-permute-start(f32[3,4,8,128]{3,2,1,0:T(8,128)S(1)} %get-tuple-element.24), channel_id=1, source_target_pairs={{0,1},{1,2},{2,3},{3,4},{4,5},{5,6},{6,7},{7,8},{8,9},{9,10},{10,1... | collective-permute-start | bytes 147464 | tf_op jit(solution)/shard_map/ppermute | solution.py:409
  15.2 2.4 %all-gather = f32[6,8,32,128]{3,2,1,0:T(8,128)S(1)} all-gather(f32[3,8,32,128]{3,2,1,0:T(8,128)S(1)} %get-tuple-element.22), channel_id=2, replica_groups=mesh['zc'=4,'zk'=2,'xy'=64] {'zk'}, dimensions={0}, use_global_device_ids=true | all-gather | bytes 1179648 | tf_op jit(solution)/shard_map/all_gather | solution.py:410
  17.6 0.0 collective-permute-done.cross
  17.6 0.0 collective-permute-done.1.along
  17.6 0.6 %first.1 = (f32[4,6,24,128]{3,2,1,0:T(8,128)S(1)}, f32[16,24,128]{2,1,0:T(8,128)S(1)}, f32[16,24,128]{2,1,0:T(8,128)S(1)}, f32[16,24,128]{2,1,0:T(8,128)S(1)}, f...) custom-call(f32[2,3,8,32,128]{4,3,2,1,0:T(8,128)S(1)} %bitcast.2, ...), custom_call_target="tpu_custom_call" | custom-call | tf_op jit(solution)/shard_map/first/pallas_call | solution.py:377
  18.2 9.5 %all_to_all.10.got.got2 = f32[4,6,24,128]{3,2,1,0:T(8,128)S(1)} all-to-all(f32[4,6,24,128]{3,2,1,0:T(8,128)S(1)} %get-tuple-element.25), channel_id=1, replica_groups=mesh['zc'=4,'zk'=2,'xy'=64] {'zc'}, dimensions={0} | all-to-all | bytes 589824 | tf_op jit(solution)/shard_map/all_to_all | solution.py:414
  27.8 0.4 second.1
  28.2 7.5 %all_to_all.11.got3 = f32[4,4,24,128]{3,2,1,0:T(8,128)S(1)} all-to-all(f32[4,4,24,128]{3,2,1,0:T(8,128)S(1)} %get-tuple-element.36), channel_id=1, replica_groups=mesh['zc'=4,'zk'=2,'xy'=64] {'zc'}, dimensions={0} | all-to-all | bytes 393216 | tf_op jit(solution)/shard_map/all_to_all | solution.py:418
  35.7 0.9 %third.1 = f32[24,16,128]{2,1,0:T(8,128)S(1)} custom-call(f32[4,4,24,128]{3,2,1,0:T(8,128)S(1)} %all_to_all.11.got3, f32[4,6,24,128]{3,2,1,0:T(8,128)S(1)} %all_to_all.10.got.got2, f32[16,24,128]{2,1,0:T(8,128)S(1)} %get-tuple-element.26.ef, f32[16,24,128]{2,1,0:T(8,128)S(1)} %get-tuple-element.27.nf, f32[16,24,128]{2,1,0:T(8,128)S(1)} %get-tuple-element.28.vf, ...), custom_call_target="tpu_custom_call" | custom-call | tf_op jit(solution)/shard_map/third/pallas_call | solution.py:377
  36.6 8.5 %all-gather.1 = f32[48,16,128]{2,1,0:T(8,128)S(1)} all-gather(f32[24,16,128]{2,1,0:T(8,128)S(1)} %third.1), channel_id=3, replica_groups=mesh['zc'=4,'zk'=2,'xy'=64] {'zk'}, dimensions={0}, use_global_device_ids=true | all-gather | bytes 589824 | tf_op jit(solution)/shard_map/all_gather | solution.py:425
  45.0 0.7 %last.1 = (f32[8,32,128]{2,1,0:T(8,128)}, f32[4,16,64]{2,1,0:T(8,128)}) custom-call(f32[2,24,16,128]{3,2,1,0:T(8,128)S(1)} %bitcast.3), custom_call_target="tpu_custom_call" | custom-call | tf_op jit(solution)/shard_map/last/pallas_call | solution.py:377
Async XLA Ops:
  1.8 15.8 %collective-permute-start = (f32[3,4,8,128]{3,2,1,0:T(8,128)S(1)}, f32[3,4,8,128]{3,2,1,0:T(8,128)S(1)}, u32[]{:S(2)}, u32[]{:S(2)}) collective-permute-start(f32[3,4,8,128]{3,2,1,0:T(8,128)S(1)} %get-tuple-element.23), channel_id=1, source_target_pairs={{1,64},{2,65},{3,66},{4,67},{5,68},{6,69},{7,70},{8,71},{9,72},{10... | collective-permute-start | bytes 147464 | tf_op jit(solution)/shard_map/ppermute | solution.py:408
  6.4 11.2 %collective-permute-start.1 = (f32[3,4,8,128]{3,2,1,0:T(8,128)S(1)}, f32[3,4,8,128]{3,2,1,0:T(8,128)S(1)}, u32[]{:S(2)}, u32[]{:S(2)}) collective-permute-start(f32[3,4,8,128]{3,2,1,0:T(8,128)S(1)} %get-tuple-element.24), channel_id=1, source_target_pairs={{0,1},{1,2},{2,3},{3,4},{4,5},{5,6},{6,7},{7,8},{8,9},{9,10},{10,1... | collective-permute-start | bytes 147464 | tf_op jit(solution)/shard_map/ppermute | solution.py:409

commit v4 on v3

--- a/solution.py
+++ b/solution.py
@@ -7,6 +7,7 @@
 from jax.sharding import PartitionSpec as P
 
 INTERPRET = False
+AXES = ("zc", "zk", "xy")
 SCOPED = 4 << 20
 vertical_ratio = 100.0
 absorption = 0.05
@@ -56,8 +57,7 @@
     )
 
 
-def weigh_kernel(source, cond, fluid, pressure, out, cross, along, source_v, cond_v, fluid_v, sems):
-    core = lax.axis_index("zk")
+def weigh_kernel(source, cond, fluid, pressure, out, source_v, cond_v, fluid_v, sems):
     copies = [
         pltpu.make_async_copy(cond, cond_v, sems.at[0]),
         pltpu.make_async_copy(fluid, fluid_v, sems.at[1]),
@@ -72,18 +72,20 @@
         real = fluid_v[l].astype(F32)
         out[0, l] = cond_v[l] * real
         out[1, l] = real * source_v[l]
-    row8 = lax.broadcasted_iota(jnp.int32, (8, LAN), 0)
-    for ref, high in ((cross, core), (along, 1 - core)):
-        start = pl.multiple_of(high * 24, 8)
-        keep = (row8 < 4) == (high == 0)
-        for f in range(3):
-            for l in range(4):
-                one = out[f, l, pl.ds(start, 8), :]
-                two = out[f, l + 4, pl.ds(start, 8), :]
-                ref[f, l] = jnp.where(keep, one, pltpu.roll(two, 4, 0))
-
-
-def first_kernel(both, cross, along, send, ef, nf, vf, dg, fr, pr, rc, mm, gr, br, bg):
+
+
+def edge_kernel(both, out):
+    core = lax.axis_index("zk")
+    start = pl.multiple_of(core * 24, 8)
+    keep = (lax.broadcasted_iota(jnp.int32, (8, LAN), 0) < 4) == (core == 0)
+    for f in range(3):
+        for l in range(HALF):
+            low = both[0, f, l, pl.ds(start, 8), :]
+            high = both[1, f, l, pl.ds(start, 8), :]
+            out[f, l] = jnp.where(keep, low, pltpu.roll(high, 4, 0))
+
+
+def first_kernel(both, halo, send, ef, nf, vf, dg, fr, pr, rc, mm, gr, br, bg):
     core = lax.axis_index("zk")
     row, lane, red = iotas()
     last_lane = lane == LAN - 1
@@ -91,13 +93,14 @@
     from_near = (row8 < 4) == (core == 0)
     own_at = pl.multiple_of(core * 16, 8)
     near_at = pl.multiple_of(16 - 8 * core, 8)
+    block = lax.axis_index("xy")
+    inside = jnp.where(core == 0, block > 0, block < lax.axis_size("xy") - 1)
 
     def window(f, l):
         own = both[l // 8, f, l % 8, pl.ds(own_at, 16), :]
         near = both[l // 8, f, l % 8, pl.ds(near_at, 8), :]
-        straight = core == l // 8
-        far = jnp.where(straight, along[f, l % 4], cross[f, l % 4])
-        if l % 8 >= 4:
+        far = jnp.where(inside, halo[1 - core, f, l % 8], 0.0)
+        if l >= HALF:
             far = pltpu.roll(far, 4, 0)
         return jnp.concatenate([own, jnp.where(from_near, near, far)], axis=0)
 
@@ -388,29 +391,37 @@
     return run
 
 
+def side_by_side():
+    chips, cores, count = (lax.axis_size(axis) for axis in AXES)
+
+    def number(chip, core, q):
+        return (chip * cores + core) * count + q
+
+    groups = [[number(c, 0, q), number(c, 1, q - 1)] for c in range(chips) for q in range(1, count)]
+    for c in range(0, chips, 2):
+        groups.append([number(c, 0, 0), number(c + 1, 0, 0)])
+        groups.append([number(c, 1, count - 1), number(c + 1, 1, count - 1)])
+    return groups
+
+
 def shards(source, conductivity, fluid, pressure):
     cell = (WIN, LAN)
     field = (LEV, WIN, LAN)
     block = (HALF, 32, LAN)
-    edge = (3, 4, 8, LAN)
     vmem = pltpu.VMEM
-    mine, cross, along = call(
+    (mine,) = call(
         weigh_kernel,
         "weigh",
-        [(3,) + block, edge, edge],
+        [(3,) + block],
         [vmem(block, F32), vmem(block, F32), vmem(block, jnp.int32), pltpu.SemaphoreType.DMA((4,))],
         ends="first",
     )(source, conductivity, fluid, pressure)
-    count = lax.axis_size("xy")
-    swap = [(q, count + q - 1) for q in range(1, count)]
-    swap += [(b, a) for a, b in swap]
-    shift = [(q, q + 1) for q in range(count - 1)] + [(count + q + 1, count + q) for q in range(count - 1)]
-    cross = lax.ppermute(cross, ("zk", "xy"), swap)
-    along = lax.ppermute(along, ("zk", "xy"), shift)
     both = lax.all_gather(mine, "zk", axis=0, tiled=False)
+    (edge,) = call(edge_kernel, "edge", [(3, HALF, 8, LAN)])(both)
+    halo = lax.all_gather(edge, AXES, axis=0, tiled=False, axis_index_groups=side_by_side())
     send2, ef, nf, vf, dg, fr, pr, rc, mm, gr, br, bg = call(
         first_kernel, "first", [(4, 6) + cell] + [field] * 10 + [(2,) + cell]
-    )(both, cross, along)
+    )(both, halo)
     got2 = lax.all_to_all(send2, "zc", 0, 0, tiled=False)
     send3, p1, bb, chain, u_red = call(
         second_kernel, "second", [(4, 4) + cell, field, field, (3, 8) + cell, (8,) + cell]
@@ -428,6 +439,6 @@
 
 
 def solution(mesh):
-    finer = Mesh(mesh.devices.reshape(4, 2, mesh.shape["xy"]), ("zc", "zk", "xy"))
+    finer = Mesh(mesh.devices.reshape(4, 2, mesh.shape["xy"]), AXES)
     spec = P(("zc", "zk"), "xy", None)
     return jax.shard_map(shards, mesh=finer, in_specs=(spec,) * 4, out_specs=(spec,) * 2, check_vma=False)

time: 46.3 us -> 42.6 us (0.920)
  starting transfers between devices: 13.4 us -> 0 us
  blocking collectives: 27.9 us -> 38 us
    ppermute x2 -> x0, starting transfers between devices: 13.4 us -> none  [the longest x1 8.81 us: shards(): along = lax.ppermute(along, ('zk', 'xy'), shift)]
    all_gather x0 -> x1, blocking collectives: none -> 5.31 us  [shards(): lax.all_gather(edge, AXES, axis=0, tiled=False, axis_index_groups=side_by...]
    all_gather x1, blocking collectives: 8.45 us -> 11.6 us  [shards(): ends = lax.all_gather(done, 'zk', axis=0, tiled=False)]
    all_to_all x1, blocking collectives: 7.54 us -> 8.89 us  [shards(): got3 = lax.all_to_all(send3, 'zc', 0, 0, tiled=False)]
    pallas_call x5 -> x6, Pallas kernels: 3.76 us -> 3.71 us  [run(): pl.pallas_call(kernel, out_shape=[jax.ShapeDtypeStruct(s, F32) if plain e...]
  transfers between devices with their start and end apart: 2 -> 0, of which waited for: 0 -> 0; matrix products, arithmetic and copies ran while one was open for 0% -> 0% of each run, Pallas kernels for 0% -> 0%
where the time goes in v4:
time: 42.6 us; the launch traced here: 42.3 us
  blocking collectives  38 us (89%)
  Pallas kernels  3.71 us (9%)
  between operations  0.65 us (2%)
    all_gather x1, blocking collectives, shards(): ends = lax.all_gather(done, 'zk', axis=0, tiled=False)  11.6 us
    all_to_all x1, blocking collectives, shards(): got2 = lax.all_to_all(send2, 'zc', 0, 0, tiled=False)  9.52 us
    all_to_all x1, blocking collectives, shards(): got3 = lax.all_to_all(send3, 'zc', 0, 0, tiled=False)  8.89 us
    all_gather x1, blocking collectives, shards(): lax.all_gather(edge, AXES, axis=0, tiled=False, axis_index_groups=side_by...  5.31 us
    pallas_call x6, Pallas kernels, run(): pl.pallas_call(kernel, out_shape=[jax.ShapeDtypeStruct(s, F32) if plain e...  3.71 us
    all_gather x1, blocking collectives, shards(): both = lax.all_gather(mine, 'zk', axis=0, tiled=False)  2.67 us

profile of v4, /device:TPU:57, one launch (start us, length us, event | category | flops | bytes accessed | tf_op | source)
XLA Modules:
  0.0 42.3 jit_solution(12715796454298582839)
XLA Ops:
  0.6 1.2 %weigh.1 = f32[3,8,32,128]{3,2,1,0:T(8,128)S(1)} custom-call(f32[8,32,128]{2,1,0:T(8,128)} %source.1, f32[8,32,128]{2,1,0:T(8,128)} %cond.1, s32[8,32,128]{2,1,0:T(8,128)} %fluid.1, f32[8,32,128]{2,1,0:T(8,128)} %pressure.1), custom_call_target="tpu_custom_call" | custom-call | tf_op jit(solution)/shard_map/weigh/pallas_call | solution.py:380
  1.8 2.7 %all-gather = f32[6,8,32,128]{3,2,1,0:T(8,128)S(1)} all-gather(f32[3,8,32,128]{3,2,1,0:T(8,128)S(1)} %weigh.1), channel_id=2, replica_groups=mesh['zc'=4,'zk'=2,'xy'=64] {'zk'}, dimensions={0}, use_global_device_ids=true | all-gather | bytes 1179648 | tf_op jit(solution)/shard_map/all_gather | solution.py:419
  4.5 5.3 %all-gather.1 = f32[6,8,8,128]{3,2,1,0:T(8,128)S(1)} all-gather(f32[3,8,8,128]{3,2,1,0:T(8,128)S(1)} %edge.1), channel_id=3, replica_groups={{1,64},{2,65},{3,66},{4,67},{5,68},{6,69},{7,70},{8,71},{9,72},{10,73},..., dimensions={0}, use_global_device_ids=true | all-gather | bytes 294912 | tf_op jit(solution)/shard_map/all_gather | solution.py:421
  9.8 0.6 %first.1 = (f32[4,6,24,128]{3,2,1,0:T(8,128)S(1)}, f32[16,24,128]{2,1,0:T(8,128)S(1)}, f32[16,24,128]{2,1,0:T(8,128)S(1)}, f32[16,24,128]{2,1,0:T(8,128)S(1)}, f...) custom-call(f32[2,3,8,32,128]{4,3,2,1,0:T(8,128)S(1)} %bitcast.4, ...), custom_call_target="tpu_custom_call" | custom-call | tf_op jit(solution)/shard_map/first/pallas_call | solution.py:380
  10.4 9.5 %all_to_all.10.got.got2 = f32[4,6,24,128]{3,2,1,0:T(8,128)S(1)} all-to-all(f32[4,6,24,128]{3,2,1,0:T(8,128)S(1)} %get-tuple-element.19), channel_id=1, replica_groups=mesh['zc'=4,'zk'=2,'xy'=64] {'zc'}, dimensions={0} | all-to-all | bytes 589824 | tf_op jit(solution)/shard_map/all_to_all | solution.py:425
  19.9 0.4 second.1
  20.4 8.9 %all_to_all.11.got3 = f32[4,4,24,128]{3,2,1,0:T(8,128)S(1)} all-to-all(f32[4,4,24,128]{3,2,1,0:T(8,128)S(1)} %get-tuple-element.30), channel_id=1, replica_groups=mesh['zc'=4,'zk'=2,'xy'=64] {'zc'}, dimensions={0} | all-to-all | bytes 393216 | tf_op jit(solution)/shard_map/all_to_all | solution.py:429
  29.2 0.8 %third.1 = f32[24,16,128]{2,1,0:T(8,128)S(1)} custom-call(f32[4,4,24,128]{3,2,1,0:T(8,128)S(1)} %all_to_all.11.got3, f32[4,6,24,128]{3,2,1,0:T(8,128)S(1)} %all_to_all.10.got.got2, f32[16,24,128]{2,1,0:T(8,128)S(1)} %get-tuple-element.20.ef, f32[16,24,128]{2,1,0:T(8,128)S(1)} %get-tuple-element.21.nf, f32[16,24,128]{2,1,0:T(8,128)S(1)} %get-tuple-element.22.vf, ...), custom_call_target="tpu_custom_call" | custom-call | tf_op jit(solution)/shard_map/third/pallas_call | solution.py:380
  30.1 11.6 %all-gather.2 = f32[48,16,128]{2,1,0:T(8,128)S(1)} all-gather(f32[24,16,128]{2,1,0:T(8,128)S(1)} %third.1), channel_id=4, replica_groups=mesh['zc'=4,'zk'=2,'xy'=64] {'zk'}, dimensions={0}, use_global_device_ids=true | all-gather | bytes 589824 | tf_op jit(solution)/shard_map/all_gather | solution.py:436
  41.7 0.7 %last.1 = (f32[8,32,128]{2,1,0:T(8,128)}, f32[4,16,64]{2,1,0:T(8,128)}) custom-call(f32[2,24,16,128]{3,2,1,0:T(8,128)S(1)} %bitcast.5), custom_call_target="tpu_custom_call" | custom-call | tf_op jit(solution)/shard_map/last/pallas_call | solution.py:380
  (1 shorter events, 0.0 us)

commit v5 on v4

v5 whole, which is shorter than its diff:
```python
import jax
import jax.numpy as jnp
from jax import lax
from jax.experimental import pallas as pl
from jax.experimental.pallas import tpu as pltpu
from jax.sharding import Mesh
from jax.sharding import PartitionSpec as P

INTERPRET = False
AXES = ("zc", "zk", "xy")
SCOPED = 4 << 20
vertical_ratio = 100.0
absorption = 0.05

LEV = 16
HALF = 8
COMMON = 15
SENT = 18
WIN = 24
LAN = 128
F32 = jnp.float32


def east_of(v):
    return pltpu.roll(v, WIN - 1, 0)


def west_of(v):
    return pltpu.roll(v, 1, 0)


def north_of(v):
    return pltpu.roll(v, LAN - 1, 1)


def south_of(v):
    return pltpu.roll(v, 1, 1)


def iotas():
    row = lax.broadcasted_iota(jnp.int32, (WIN, LAN), 0)
    lane = lax.broadcasted_iota(jnp.int32, (WIN, LAN), 1)
    red = ((row + lane) & 1) == 0
    return row, lane, red


def side_faces(w, last_lane):
    east = jnp.sqrt(w * east_of(w))
    north = jnp.where(last_lane, 0.0, jnp.sqrt(w * north_of(w)))
    return east, north


def horizontal(east, north, p):
    return (
        west_of(east * p)
        + east * east_of(p)
        + south_of(north * p)
        + north * north_of(p)
    )


def weigh_kernel(source, cond, fluid, pressure, out, source_v, cond_v, fluid_v, sems):
    copies = [
        pltpu.make_async_copy(cond, cond_v, sems.at[0]),
        pltpu.make_async_copy(fluid, fluid_v, sems.at[1]),
        pltpu.make_async_copy(source, source_v, sems.at[2]),
        pltpu.make_async_copy(pressure, out.at[2], sems.at[3]),
    ]
    for copy in copies:
        copy.start()
    for copy in copies:
        copy.wait()
    for l in range(HALF):
        real = fluid_v[l].astype(F32)
        out[0, l] = cond_v[l] * real
        out[1, l] = real * source_v[l]


def edge_kernel(both, out):
    core = lax.axis_index("zk")
    start = pl.multiple_of(core * 24, 8)
    keep = (lax.broadcasted_iota(jnp.int32, (8, LAN), 0) < 4) == (core == 0)
    for f in range(3):
        for l in range(HALF):
            low = both[0, f, l, pl.ds(start, 8), :]
            high = both[1, f, l, pl.ds(start, 8), :]
            out[f, l] = jnp.where(keep, low, pltpu.roll(high, 4, 0))


def first_kernel(both, halo, send, ef, nf, vf, dg, fr, rc, mm, al, be, ga):
    core = lax.axis_index("zk")
    row, lane, red = iotas()
    last_lane = lane == LAN - 1
    row8 = lax.broadcasted_iota(jnp.int32, (8, LAN), 0)
    from_near = (row8 < 4) == (core == 0)
    own_at = pl.multiple_of(core * 16, 8)
    near_at = pl.multiple_of(16 - 8 * core, 8)
    block = lax.axis_index("xy")
    inside = jnp.where(core == 0, block > 0, block < lax.axis_size("xy") - 1)

    def window(f, l):
        own = both[l // 8, f, l % 8, pl.ds(own_at, 16), :]
        near = both[l // 8, f, l % 8, pl.ds(near_at, 8), :]
        far = jnp.where(inside, halo[1 - core, f, l % 8], 0.0)
        if l >= HALF:
            far = pltpu.roll(far, 4, 0)
        return jnp.concatenate([own, jnp.where(from_near, near, far)], axis=0)

    for l in range(LEV):
        w = window(0, l)
        east, north = side_faces(w, last_lane)
        ef[l] = east
        nf[l] = north
        if l == 0:
            w0 = w
            vf[0] = jnp.zeros_like(w)
        else:
            vf[l] = vertical_ratio * jnp.sqrt(w * w_below)
        w_below = w
        fluid = jnp.where(w > 0.0, 1.0, 0.0)
        dg[l] = fluid * (absorption + (west_of(east) + east + south_of(north) + north)) + (1.0 - fluid)
        fr[l] = window(1, l)
    w15 = w_below
    heat0 = fr[0] + horizontal(ef[0], nf[0], window(2, 0))
    d0 = dg[0] + vf[1]
    dg[0] = d0
    for l in range(1, LEV):
        d = dg[l] + vf[l]
        if l < LEV - 1:
            d = d + vf[l + 1]
        dg[l] = d
        b = fr[l] + horizontal(ef[l], nf[l], window(2, l))
        v = vf[l]
        if l == 1:
            dd, bb, g = d, b, v
        elif l < LEV - 1:
            dd = d - mult * v
            bb = b + mult * bb
            g = mult * g
        if l < LEV - 1:
            rcp = 1.0 / dd
            mult = vf[l + 1] * rcp
            rc[l] = rcp
            mm[l] = mult
            al[l] = bb * rcp
            be[l] = g * rcp
    heat15 = b
    alpha = jnp.where(red, al[LEV - 2], 0.0)
    beta = be[LEV - 2]
    gamma = mm[LEV - 2]
    al[LEV - 2] = alpha
    ga[LEV - 2] = gamma
    for l in range(LEV - 3, 0, -1):
        mult = mm[l]
        alpha = jnp.where(red, al[l] + mult * alpha, 0.0)
        beta = be[l] + mult * beta
        gamma = mult * gamma
        al[l] = alpha
        be[l] = beta
        ga[l] = gamma
    v1 = vf[1]
    v15 = vf[LEV - 1]
    self_low = v1 * be[1]
    self_high = v15 * ga[LEV - 2]
    e_tt, e_bb = ef[0], ef[LEV - 1]
    n_tt, n_bb = nf[0], nf[LEV - 1]
    e_tb = e_bt = n_tb = n_bt = jnp.zeros((WIN, LAN), F32)
    con_low = fr[0]
    con_high = fr[LEV - 1]
    for l in range(1, LEV - 1):
        beta, gamma, alpha = be[l], ga[l], al[l]
        east, north = ef[l], nf[l]
        there_b, there_g = east_of(beta), east_of(gamma)
        mine_b, mine_g = east * beta, east * gamma
        e_tt = e_tt + mine_b * there_b
        e_tb = e_tb + mine_b * there_g
        e_bt = e_bt + mine_g * there_b
        e_bb = e_bb + mine_g * there_g
        there_b, there_g = north_of(beta), north_of(gamma)
        mine_b, mine_g = north * beta, north * gamma
        n_tt = n_tt + mine_b * there_b
        n_tb = n_tb + mine_b * there_g
        n_bt = n_bt + mine_g * there_b
        n_bb = n_bb + mine_g * there_g
        b = fr[l] + horizontal(east, north, alpha)
        con_low = con_low + beta * b
        con_high = con_high + gamma * b
    own_low = v1 * al[1]
    own_high = v15 * al[LEV - 2]
    common = [d0 - self_low, v15 * be[LEV - 2], dg[LEV - 1] - self_high, w0, w15]
    common += [jnp.where(red, heat0 + own_low, con_low), jnp.where(red, heat15 + own_high, con_high)]
    common += [e_tt, e_tb, e_bt, e_bb, n_tt, n_tb, n_bt, n_bb]
    for k, value in enumerate(common):
        for peer in range(4):
            send[peer, k] = value
    upward = [v15, self_high, fr[LEV - 1] + own_high]
    downward = [v1, self_low, fr[0] + own_low]
    chip = lax.axis_index("zc")
    for peer in range(4):
        for k in range(3):
            send[peer, COMMON + k] = jnp.where(chip < peer, upward[k], downward[k])


def chain_factor(diag, link):
    rcp = [None] * 8
    for j in range(4):
        pivot = diag[j] if j == 0 else diag[j] - link[j] * link[j] * rcp[j - 1]
        rcp[j] = 1.0 / pivot
    for j in range(7, 4, -1):
        pivot = diag[j] if j == 7 else diag[j] - link[j + 1] * link[j + 1] * rcp[j + 1]
        rcp[j] = 1.0 / pivot
    rcp[4] = 1.0 / (diag[4] - link[4] * link[4] * rcp[3] - link[5] * link[5] * rcp[5])
    return rcp


def chain_solve(rcp, link, right):
    acc = list(right)
    for j in range(1, 4):
        acc[j] = acc[j] + link[j] * (rcp[j - 1] * acc[j - 1])
    for j in range(6, 4, -1):
        acc[j] = acc[j] + link[j + 1] * (rcp[j + 1] * acc[j + 1])
    out = [None] * 8
    out[4] = (acc[4] + link[4] * (rcp[3] * acc[3]) + link[5] * (rcp[5] * acc[5])) * rcp[4]
    for j in range(3, -1, -1):
        out[j] = (acc[j] + link[j + 1] * out[j + 1]) * rcp[j]
    for j in range(5, 8):
        out[j] = (acc[j] + link[j] * out[j - 1]) * rcp[j]
    return out


def second_kernel(got, ef, nf, vf, dg, fr, rc, mm, al, be, ga, out, ends, heat, full, res):
    chip = lax.axis_index("zc")
    row, lane, red = iotas()
    last_lane = lane == LAN - 1
    diag, link, right = [], [None], []
    for group in range(4):
        up, down = got[group, 0], got[group, 2]
        if group > 0:
            up = up + face
        if group < 3:
            face = vertical_ratio * jnp.sqrt(got[group, 4] * got[group + 1, 3])
            down = down + face
        diag += [up, down]
        link += [got[group, 1]] + ([face] if group < 3 else [])
        right += [got[group, 5], got[group, 6]]
    rcp = chain_factor(diag, link)
    reds = [jnp.where(red, v, 0.0) for v in chain_solve(rcp, link, right)]
    for group in range(4):
        t, b = reds[2 * group], reds[2 * group + 1]
        e_tt, e_tb, e_bt, e_bb, n_tt, n_tb, n_bt, n_bb = (got[group, 7 + k] for k in range(8))
        te, be_, tn, bn = east_of(t), east_of(b), north_of(t), north_of(b)
        right[2 * group] = right[2 * group] + (
            (e_tt * te + e_tb * be_)
            + (n_tt * tn + n_tb * bn)
            + west_of(e_tt * t + e_bt * b)
            + south_of(n_tt * t + n_bt * b)
        )
        right[2 * group + 1] = right[2 * group + 1] + (
            (e_bt * te + e_bb * be_)
            + (n_bt * tn + n_bb * bn)
            + west_of(e_tb * t + e_bb * b)
            + south_of(n_tb * t + n_bb * b)
        )
    blacks = chain_solve(rcp, link, right)
    for j in range(8):
        ends[j] = jnp.where(red, reds[j], blacks[j])
        heat[j] = right[j]
    low = ends[2 * chip]
    high = ends[2 * chip + 1]
    full[2] = low
    full[LEV + 1] = high
    bb = jnp.where(red, 0.0, vf[1] * low)
    for l in range(1, LEV - 1):
        p = jnp.where(red, al[l] + be[l] * low + ga[l] * high, 0.0)
        full[l + 2] = p
        b = fr[l] + horizontal(ef[l], nf[l], p)
        bb = b + (bb if l == 1 else mm[l - 1] * bb)
        res[l] = bb * rc[l]
    cur = high
    for l in range(LEV - 2, 0, -1):
        cur = res[l] + mm[l] * cur
        full[l + 2] = jnp.where(red, full[l + 2], cur)
    for l in range(LEV):
        out[l] = full[l + 2, 0:16, :]

    for side in (0, 1):
        near_chip = jnp.maximum(chip - 1, 0) if side == 0 else jnp.minimum(chip + 1, 3)
        there = chip > 0 if side == 0 else chip < 3
        end = 1 - side
        w_near = jnp.where(there, got[near_chip, 4 - side], 0.0)
        w_own = got[chip, 3 + side]
        p_near = ends[2 * near_chip + end]
        p_other = ends[2 * near_chip + side]
        p_own = low if side == 0 else high
        face_own = vertical_ratio * jnp.sqrt(w_near * w_own)
        face_far = got[near_chip, COMMON]
        east, north = side_faces(w_near, last_lane)
        fluid = jnp.where(w_near > 0.0, 1.0, 0.0)
        d = fluid * (
            absorption + (west_of(east) + east + south_of(north) + north) + face_own + face_far
        ) + (1.0 - fluid)
        known = jnp.where(red, got[near_chip, COMMON + 2] + horizontal(east, north, p_near), heat[2 * near_chip + end])
        inside = got[near_chip, 1] * p_other + got[near_chip, COMMON + 1] * p_near
        beyond = known + inside + face_own * p_own - d * p_near
        beyond = jnp.where(there, beyond, 0.0)
        if side == 0:
            res[0] = beyond
            face_low = face_own
            p_below = p_near
        else:
            res[LEV + 1] = beyond
            face_high = face_own
            p_above = p_near
    for l in range(LEV):
        p = full[l + 2]
        d = dg[l]
        if l == 0:
            d = d + face_low
            vert = face_low * p_below + vf[1] * full[3]
        elif l == LEV - 1:
            d = d + face_high
            vert = vf[l] * full[l + 1] + face_high * p_above
        else:
            vert = vf[l] * full[l + 1] + vf[l + 1] * full[l + 3]
        applied = d * p - (horizontal(ef[l], nf[l], p) + vert)
        res[l + 1] = fr[l] - applied
    weights = restriction_matrix()
    for big in range(LEV // 2):
        z = 2 * big
        s = 0.125 * (res[z] + 3.0 * res[z + 1] + 3.0 * res[z + 2] + res[z + 3])
        e = east_of(s)
        s = 0.125 * (west_of(s) + 3.0 * s + 3.0 * e + east_of(e))
        res[z] = jnp.dot(s, weights, precision=lax.Precision.HIGHEST, preferred_element_type=F32)
        out[LEV + big] = jnp.concatenate(
            [res[z, pl.ds(0, 8, stride=2), :], jnp.zeros((8, LAN), F32)], axis=0
        )


def last_kernel(both, relaxed, coarse):
    core = lax.axis_index("zk")
    for j in range(2):
        for l in range(8):
            relaxed[l, 16 * j : 16 * j + 16, :] = both[j, core * 8 + l]
        for big in range(4):
            coarse[big, 8 * j : 8 * j + 8, :] = both[j, LEV + core * 4 + big, 0:8, 0:64]


def restriction_matrix():
    fine = lax.broadcasted_iota(jnp.int32, (LAN, LAN), 0)
    big = lax.broadcasted_iota(jnp.int32, (LAN, LAN), 1)
    off = fine - 2 * big + 1
    inner = (off == 1) | (off == 2)
    outer = (off == 0) | (off == 3)
    return jnp.where(inner, 0.375, jnp.where(outer, 0.125, 0.0)).astype(F32)


def call(kernel, name, shapes, scratch=(), ends=""):
    vm = pl.BlockSpec(memory_space=pltpu.VMEM)
    main = pl.BlockSpec(memory_space=pltpu.HBM)

    def run(*args):
        if not INTERPRET:
            space = pltpu.HBM if ends == "first" else pltpu.VMEM
            args = [pltpu.with_memory_space_constraint(a, space) for a in args]
        plain = ends == "last" or INTERPRET
        return pl.pallas_call(
            kernel,
            out_shape=[jax.ShapeDtypeStruct(s, F32) if plain else pltpu.VMEM(s, F32) for s in shapes],
            in_specs=[main if ends == "first" else vm] * len(args),
            out_specs=[vm] * len(shapes),
            scratch_shapes=scratch,
            name=name,
            compiler_params=pltpu.CompilerParams(vmem_limit_bytes=SCOPED),
            interpret=INTERPRET,
        )(*args)

    return run


def side_by_side():
    chips, cores, count = (lax.axis_size(axis) for axis in AXES)

    def number(chip, core, q):
        return (chip * cores + core) * count + q

    groups = [[number(c, 0, q), number(c, 1, q - 1)] for c in range(chips) for q in range(1, count)]
    for c in range(0, chips, 2):
        groups.append([number(c, 0, 0), number(c + 1, 0, 0)])
        groups.append([number(c, 1, count - 1), number(c + 1, 1, count - 1)])
    return groups


def shards(source, conductivity, fluid, pressure):
    cell = (WIN, LAN)
    field = (LEV, WIN, LAN)
    block = (HALF, 32, LAN)
    vmem = pltpu.VMEM
    (mine,) = call(
        weigh_kernel,
        "weigh",
        [(3,) + block],
        [vmem(block, F32), vmem(block, F32), vmem(block, jnp.int32), pltpu.SemaphoreType.DMA((4,))],
        ends="first",
    )(source, conductivity, fluid, pressure)
    both = lax.all_gather(mine, "zk", axis=0, tiled=False)
    (edge,) = call(edge_kernel, "edge", [(3, HALF, 8, LAN)])(both)
    halo = lax.all_gather(edge, AXES, axis=0, tiled=False, axis_index_groups=side_by_side())
    send, *fields = call(first_kernel, "first", [(4, SENT) + cell] + [field] * 10)(both, halo)
    got = lax.all_to_all(send, "zc", 0, 0, tiled=False)
    (done,) = call(
        second_kernel,
        "second",
        [(LEV + LEV // 2, 16, LAN)],
        [vmem((8,) + cell, F32)] * 2 + [vmem((LEV + 4,) + cell, F32), vmem((LEV + 2,) + cell, F32)],
    )(got, *fields)
    ends = lax.all_gather(done, "zk", axis=0, tiled=False)
    relaxed, coarse = call(last_kernel, "last", [block, (4, 16, LAN // 2)], ends="last")(ends)
    return relaxed, coarse


def solution(mesh):
    finer = Mesh(mesh.devices.reshape(4, 2, mesh.shape["xy"]), AXES)
    spec = P(("zc", "zk"), "xy", None)
    return jax.shard_map(shards, mesh=finer, in_specs=(spec,) * 4, out_specs=(spec,) * 2, check_vma=False)
```

time: 42.6 us -> 36.9 us (0.87)
  the two profiles are of different devices: /device:TPU:57 before, /device:TPU:1 now
where the time goes in v5:
time: 36.9 us; the launch traced here: 36.7 us
  blocking collectives  32.3 us (88%)
  Pallas kernels  3.76 us (10%)
  between operations  0.65 us (2%)
    all_to_all x1, blocking collectives, shards(): got = lax.all_to_all(send, 'zc', 0, 0, tiled=False)  14.9 us
    all_gather x1, blocking collectives, shards(): both = lax.all_gather(mine, 'zk', axis=0, tiled=False)  8.83 us
    all_gather x1, blocking collectives, shards(): lax.all_gather(edge, AXES, axis=0, tiled=False, axis_index_groups=side_by...  5.02 us
    pallas_call x5, Pallas kernels, run(): pl.pallas_call(kernel, out_shape=[jax.ShapeDtypeStruct(s, F32) if plain e...  3.76 us
    all_gather x1, blocking collectives, shards(): ends = lax.all_gather(done, 'zk', axis=0, tiled=False)  3.48 us

profile of v5, /device:TPU:1, one launch (start us, length us, event | category | flops | bytes accessed | tf_op | source)
XLA Modules:
  0.0 36.7 jit_solution(504450003643432118)
XLA Ops:
  0.6 1.2 %weigh.1 = f32[3,8,32,128]{3,2,1,0:T(8,128)S(1)} custom-call(f32[8,32,128]{2,1,0:T(8,128)} %source.1, f32[8,32,128]{2,1,0:T(8,128)} %cond.1, s32[8,32,128]{2,1,0:T(8,128)} %fluid.1, f32[8,32,128]{2,1,0:T(8,128)} %pressure.1), custom_call_target="tpu_custom_call" | custom-call | tf_op jit(solution)/shard_map/weigh/pallas_call | solution.py:366
  1.8 8.8 %all-gather = f32[6,8,32,128]{3,2,1,0:T(8,128)S(1)} all-gather(f32[3,8,32,128]{3,2,1,0:T(8,128)S(1)} %weigh.1), channel_id=2, replica_groups=mesh['zc'=4,'zk'=2,'xy'=64] {'zk'}, dimensions={0}, use_global_device_ids=true | all-gather | bytes 1179648 | tf_op jit(solution)/shard_map/all_gather | solution.py:405
  10.7 5.0 %all-gather.1 = f32[6,8,8,128]{3,2,1,0:T(8,128)S(1)} all-gather(f32[3,8,8,128]{3,2,1,0:T(8,128)S(1)} %edge.1), channel_id=3, replica_groups={{1,64},{2,65},{3,66},{4,67},{5,68},{6,69},{7,70},{8,71},{9,72},{10,73},..., dimensions={0}, use_global_device_ids=true | all-gather | bytes 294912 | tf_op jit(solution)/shard_map/all_gather | solution.py:407
  15.7 0.9 %first.1 = (f32[4,18,24,128]{3,2,1,0:T(8,128)S(1)}, f32[16,24,128]{2,1,0:T(8,128)S(1)}, f32[16,24,128]{2,1,0:T(8,128)S(1)}, f32[16,24,128]{2,1,0:T(8,128)S(1)}, ...) custom-call(f32[2,3,8,32,128]{4,3,2,1,0:T(8,128)S(1)} %bitcast.4, ...), custom_call_target="tpu_custom_call" | custom-call | tf_op jit(solution)/shard_map/first/pallas_call | solution.py:366
  16.5 14.9 %all_to_all.5.got = f32[4,18,24,128]{3,2,1,0:T(8,128)S(1)} all-to-all(f32[4,18,24,128]{3,2,1,0:T(8,128)S(1)} %get-tuple-element.13), channel_id=1, replica_groups=mesh['zc'=4,'zk'=2,'xy'=64] {'zc'}, dimensions={0} | all-to-all | bytes 1769472 | tf_op jit(solution)/shard_map/all_to_all | solution.py:409
  31.5 1.1 %second.1 = f32[24,16,128]{2,1,0:T(8,128)S(1)} custom-call(f32[4,18,24,128]{3,2,1,0:T(8,128)S(1)} %all_to_all.5.got, f32[16,24,128]{2,1,0:T(8,128)S(1)} %get-tuple-element.14.ef, f32[16,24,128]{2,1,0:T(8,128)S(1)} %get-tuple-element.15.nf, f32[16,24,128]{2,1,0:T(8,128)S(1)} %get-tuple-element.16.vf, f32[16,24,128]{2,1,0:T(8,128)S(1)} %get-tuple-element.17.dg, ...), custom_call_target="tpu_custom_call" | custom-call | tf_op jit(solution)/shard_map/second/pallas_call | solution.py:366
  32.5 3.5 %all-gather.2 = f32[48,16,128]{2,1,0:T(8,128)S(1)} all-gather(f32[24,16,128]{2,1,0:T(8,128)S(1)} %second.1), channel_id=4, replica_groups=mesh['zc'=4,'zk'=2,'xy'=64] {'zk'}, dimensions={0}, use_global_device_ids=true | all-gather | bytes 589824 | tf_op jit(solution)/shard_map/all_gather | solution.py:416
  36.0 0.7 %last.1 = (f32[8,32,128]{2,1,0:T(8,128)}, f32[4,16,64]{2,1,0:T(8,128)}) custom-call(f32[2,24,16,128]{3,2,1,0:T(8,128)S(1)} %bitcast.5), custom_call_target="tpu_custom_call" | custom-call | tf_op jit(solution)/shard_map/last/pallas_call | solution.py:366
  (1 shorter events, 0.0 us)

commit v6 on v5

--- a/solution.py
+++ b/solution.py
@@ -14,8 +14,10 @@
 
 LEV = 16
 HALF = 8
-COMMON = 15
-SENT = 18
+ARRAYS = 16
+OUTER = (0, 1, 2, 3, 4, 5, 6, 7, 8, 9, 10, 11, 11, 12, 12, 7)
+ROLLED = (12, 14, 15)
+SENT = ARRAYS * 16 + 13 * 8
 WIN = 24
 LAN = 128
 F32 = jnp.float32
@@ -85,6 +87,18 @@
             low = both[0, f, l, pl.ds(start, 8), :]
             high = both[1, f, l, pl.ds(start, 8), :]
             out[f, l] = jnp.where(keep, low, pltpu.roll(high, 4, 0))
+
+
+def outer_rows(k):
+    at = ARRAYS * 16 + 8 * OUTER[k]
+    return slice(at, at + 8)
+
+
+def received(got, group, k):
+    outer = got[group, outer_rows(k), :]
+    if k in ROLLED:
+        outer = pltpu.roll(outer, 4, 0)
+    return jnp.concatenate([got[group, 16 * k : 16 * k + 16, :], outer], axis=0)
 
 
 def first_kernel(both, halo, send, ef, nf, vf, dg, fr, rc, mm, al, be, ga):
@@ -190,15 +204,26 @@
     common = [d0 - self_low, v15 * be[LEV - 2], dg[LEV - 1] - self_high, w0, w15]
     common += [jnp.where(red, heat0 + own_low, con_low), jnp.where(red, heat15 + own_high, con_high)]
     common += [e_tt, e_tb, e_bt, e_bb, n_tt, n_tb, n_bt, n_bb]
-    for k, value in enumerate(common):
-        for peer in range(4):
-            send[peer, k] = value
-    upward = [v15, self_high, fr[LEV - 1] + own_high]
-    downward = [v1, self_low, fr[0] + own_low]
     chip = lax.axis_index("zc")
+    row8 = lax.broadcasted_iota(jnp.int32, (8, LAN), 0)
+    upward = fr[LEV - 1] + own_high
+    downward = fr[0] + own_low
+    outer = [value[16:24] for value in common]
+    inner = (row8 < 2) | (row8 > 5)
+    for k in (11, 13):
+        outer[k] = jnp.where(inner, outer[k], pltpu.roll(outer[k + 1], 4, 0))
+    kept = (row8 < 2) | (row8 > 4)
     for peer in range(4):
-        for k in range(3):
-            send[peer, COMMON + k] = jnp.where(chip < peer, upward[k], downward[k])
+        last = jnp.where(chip < peer, upward, downward)
+        for k in range(ARRAYS):
+            value = common[k] if k < ARRAYS - 1 else last
+            send[peer, 16 * k : 16 * k + 16, :] = value[0:16]
+            if k in ROLLED:
+                continue
+            tile = outer[k]
+            if k == 7:
+                tile = jnp.where(kept, tile, pltpu.roll(last[16:24], 4, 0))
+            send[peer, outer_rows(k), :] = tile
 
 
 def chain_factor(diag, link):
@@ -234,20 +259,20 @@
     last_lane = lane == LAN - 1
     diag, link, right = [], [None], []
     for group in range(4):
-        up, down = got[group, 0], got[group, 2]
+        up, down = received(got, group, 0), received(got, group, 2)
         if group > 0:
             up = up + face
         if group < 3:
-            face = vertical_ratio * jnp.sqrt(got[group, 4] * got[group + 1, 3])
+            face = vertical_ratio * jnp.sqrt(received(got, group, 4) * received(got, group + 1, 3))
             down = down + face
         diag += [up, down]
-        link += [got[group, 1]] + ([face] if group < 3 else [])
-        right += [got[group, 5], got[group, 6]]
+        link += [received(got, group, 1)] + ([face] if group < 3 else [])
+        right += [received(got, group, 5), received(got, group, 6)]
     rcp = chain_factor(diag, link)
     reds = [jnp.where(red, v, 0.0) for v in chain_solve(rcp, link, right)]
     for group in range(4):
         t, b = reds[2 * group], reds[2 * group + 1]
-        e_tt, e_tb, e_bt, e_bb, n_tt, n_tb, n_bt, n_bb = (got[group, 7 + k] for k in range(8))
+        e_tt, e_tb, e_bt, e_bb, n_tt, n_tb, n_bt, n_bb = (received(got, group, 7 + k) for k in range(8))
         te, be_, tn, bn = east_of(t), east_of(b), north_of(t), north_of(b)
         right[2 * group] = right[2 * group] + (
             (e_tt * te + e_tb * be_)
@@ -287,21 +312,18 @@
         near_chip = jnp.maximum(chip - 1, 0) if side == 0 else jnp.minimum(chip + 1, 3)
         there = chip > 0 if side == 0 else chip < 3
         end = 1 - side
-        w_near = jnp.where(there, got[near_chip, 4 - side], 0.0)
-        w_own = got[chip, 3 + side]
+        w_near = jnp.where(there, received(got, near_chip, 4 - side), 0.0)
+        w_own = received(got, chip, 3 + side)
         p_near = ends[2 * near_chip + end]
         p_other = ends[2 * near_chip + side]
         p_own = low if side == 0 else high
         face_own = vertical_ratio * jnp.sqrt(w_near * w_own)
-        face_far = got[near_chip, COMMON]
         east, north = side_faces(w_near, last_lane)
-        fluid = jnp.where(w_near > 0.0, 1.0, 0.0)
-        d = fluid * (
-            absorption + (west_of(east) + east + south_of(north) + north) + face_own + face_far
-        ) + (1.0 - fluid)
-        known = jnp.where(red, got[near_chip, COMMON + 2] + horizontal(east, north, p_near), heat[2 * near_chip + end])
-        inside = got[near_chip, 1] * p_other + got[near_chip, COMMON + 1] * p_near
-        beyond = known + inside + face_own * p_own - d * p_near
+        known = jnp.where(
+            red, received(got, near_chip, 15) + horizontal(east, north, p_near), heat[2 * near_chip + end]
+        )
+        d = received(got, near_chip, 2 - 2 * side) + face_own
+        beyond = known + received(got, near_chip, 1) * p_other + face_own * p_own - d * p_near
         beyond = jnp.where(there, beyond, 0.0)
         if side == 0:
             res[0] = beyond
@@ -405,7 +427,7 @@
     both = lax.all_gather(mine, "zk", axis=0, tiled=False)
     (edge,) = call(edge_kernel, "edge", [(3, HALF, 8, LAN)])(both)
     halo = lax.all_gather(edge, AXES, axis=0, tiled=False, axis_index_groups=side_by_side())
-    send, *fields = call(first_kernel, "first", [(4, SENT) + cell] + [field] * 10)(both, halo)
+    send, *fields = call(first_kernel, "first", [(4, SENT, LAN)] + [field] * 10)(both, halo)
     got = lax.all_to_all(send, "zc", 0, 0, tiled=False)
     (done,) = call(
         second_kernel,

time: 36.9 us -> 35.3 us (0.957)
  the two profiles are of different devices: /device:TPU:1 before, /device:TPU:57 now
where the time goes in v6:
time: 35.3 us; the launch traced here: 35 us
  blocking collectives  30.6 us (87%)
  Pallas kernels  3.76 us (11%)
  between operations  0.65 us (2%)
    all_to_all x1, blocking collectives, shards(): got = lax.all_to_all(send, 'zc', 0, 0, tiled=False)  11.9 us
    all_gather x1, blocking collectives, shards(): ends = lax.all_gather(done, 'zk', axis=0, tiled=False)  10.7 us
    all_gather x1, blocking collectives, shards(): lax.all_gather(edge, AXES, axis=0, tiled=False, axis_index_groups=side_by...  5.31 us
    pallas_call x5, Pallas kernels, run(): pl.pallas_call(kernel, out_shape=[jax.ShapeDtypeStruct(s, F32) if plain e...  3.76 us
    all_gather x1, blocking collectives, shards(): both = lax.all_gather(mine, 'zk', axis=0, tiled=False)  2.67 us

profile of v6, /device:TPU:57, one launch (start us, length us, event | category | flops | bytes accessed | tf_op | source)
XLA Modules:
  0.0 35.0 jit_solution(4278749724710884246)
XLA Ops:
  0.6 1.2 %weigh.1 = f32[3,8,32,128]{3,2,1,0:T(8,128)S(1)} custom-call(f32[8,32,128]{2,1,0:T(8,128)} %source.1, f32[8,32,128]{2,1,0:T(8,128)} %cond.1, s32[8,32,128]{2,1,0:T(8,128)} %fluid.1, f32[8,32,128]{2,1,0:T(8,128)} %pressure.1), custom_call_target="tpu_custom_call" | custom-call | tf_op jit(solution)/shard_map/weigh/pallas_call | solution.py:388
  1.8 2.7 %all-gather = f32[6,8,32,128]{3,2,1,0:T(8,128)S(1)} all-gather(f32[3,8,32,128]{3,2,1,0:T(8,128)S(1)} %weigh.1), channel_id=2, replica_groups=mesh['zc'=4,'zk'=2,'xy'=64] {'zk'}, dimensions={0}, use_global_device_ids=true | all-gather | bytes 1179648 | tf_op jit(solution)/shard_map/all_gather | solution.py:427
  4.5 5.3 %all-gather.1 = f32[6,8,8,128]{3,2,1,0:T(8,128)S(1)} all-gather(f32[3,8,8,128]{3,2,1,0:T(8,128)S(1)} %edge.1), channel_id=3, replica_groups={{1,64},{2,65},{3,66},{4,67},{5,68},{6,69},{7,70},{8,71},{9,72},{10,73},..., dimensions={0}, use_global_device_ids=true | all-gather | bytes 294912 | tf_op jit(solution)/shard_map/all_gather | solution.py:429
  9.8 0.9 %first.1 = (f32[4,360,128]{2,1,0:T(8,128)S(1)}, f32[16,24,128]{2,1,0:T(8,128)S(1)}, f32[16,24,128]{2,1,0:T(8,128)S(1)}, f32[16,24,128]{2,1,0:T(8,128)S(1)}, f32[...) custom-call(f32[2,3,8,32,128]{4,3,2,1,0:T(8,128)S(1)} %bitcast.4, ...), custom_call_target="tpu_custom_call" | custom-call | tf_op jit(solution)/shard_map/first/pallas_call | solution.py:388
  10.7 11.9 %all_to_all.5.got = f32[4,360,128]{2,1,0:T(8,128)S(1)} all-to-all(f32[4,360,128]{2,1,0:T(8,128)S(1)} %get-tuple-element.13), channel_id=1, replica_groups=mesh['zc'=4,'zk'=2,'xy'=64] {'zc'}, dimensions={0} | all-to-all | bytes 1474560 | tf_op jit(solution)/shard_map/all_to_all | solution.py:431
  22.6 1.1 %second.1 = f32[24,16,128]{2,1,0:T(8,128)S(1)} custom-call(f32[4,360,128]{2,1,0:T(8,128)S(1)} %all_to_all.5.got, f32[16,24,128]{2,1,0:T(8,128)S(1)} %get-tuple-element.14.ef, f32[16,24,128]{2,1,0:T(8,128)S(1)} %get-tuple-element.15.nf, f32[16,24,128]{2,1,0:T(8,128)S(1)} %get-tuple-element.16.vf, f32[16,24,128]{2,1,0:T(8,128)S(1)} %get-tuple-element.17.dg, ...), custom_call_target="tpu_custom_call" | custom-call | tf_op jit(solution)/shard_map/second/pallas_call | solution.py:388
  23.6 10.7 %all-gather.2 = f32[48,16,128]{2,1,0:T(8,128)S(1)} all-gather(f32[24,16,128]{2,1,0:T(8,128)S(1)} %second.1), channel_id=4, replica_groups=mesh['zc'=4,'zk'=2,'xy'=64] {'zk'}, dimensions={0}, use_global_device_ids=true | all-gather | bytes 589824 | tf_op jit(solution)/shard_map/all_gather | solution.py:438
  34.3 0.7 %last.1 = (f32[8,32,128]{2,1,0:T(8,128)}, f32[4,16,64]{2,1,0:T(8,128)}) custom-call(f32[2,24,16,128]{3,2,1,0:T(8,128)S(1)} %bitcast.5), custom_call_target="tpu_custom_call" | custom-call | tf_op jit(solution)/shard_map/last/pallas_call | solution.py:388
  (1 shorter events, 0.0 us)

commit v7 on v6

--- a/solution.py
+++ b/solution.py
@@ -14,10 +14,13 @@
 
 LEV = 16
 HALF = 8
+PLANES = 20
+PIECES = 4
 ARRAYS = 16
+OWN = ARRAYS * 16 - 8
 OUTER = (0, 1, 2, 3, 4, 5, 6, 7, 8, 9, 10, 11, 11, 12, 12, 7)
 ROLLED = (12, 14, 15)
-SENT = ARRAYS * 16 + 13 * 8
+SENT = OWN + 13 * 8
 WIN = 24
 LAN = 128
 F32 = jnp.float32
@@ -44,6 +47,12 @@
     lane = lax.broadcasted_iota(jnp.int32, (WIN, LAN), 1)
     red = ((row + lane) & 1) == 0
     return row, lane, red
+
+
+def black_mask(rows):
+    row = lax.broadcasted_iota(jnp.int32, (rows, LAN), 0)
+    lane = lax.broadcasted_iota(jnp.int32, (rows, LAN), 1)
+    return ((row + lane) & 1) == 1
 
 
 def side_faces(w, last_lane):
@@ -61,36 +70,39 @@
     )
 
 
-def weigh_kernel(source, cond, fluid, pressure, out, source_v, cond_v, fluid_v, sems):
-    copies = [
-        pltpu.make_async_copy(cond, cond_v, sems.at[0]),
-        pltpu.make_async_copy(fluid, fluid_v, sems.at[1]),
-        pltpu.make_async_copy(source, source_v, sems.at[2]),
-        pltpu.make_async_copy(pressure, out.at[2], sems.at[3]),
-    ]
+def weigh_kernel(source, cond, fluid, pressure, out, source_v, cond_v, fluid_v, pressure_v, sems):
+    parts = [pl.ds(k * HALF // PIECES, HALF // PIECES) for k in range(PIECES)]
+    copies = []
+    for k, part in enumerate(parts):
+        for n, (there, here) in enumerate(
+            ((cond, cond_v), (fluid, fluid_v), (source, source_v), (pressure, pressure_v))
+        ):
+            copies.append(pltpu.make_async_copy(there.at[part], here.at[part], sems.at[k, n]))
     for copy in copies:
         copy.start()
     for copy in copies:
         copy.wait()
+    black = black_mask(32)
     for l in range(HALF):
         real = fluid_v[l].astype(F32)
-        out[0, l] = cond_v[l] * real
-        out[1, l] = real * source_v[l]
+        out[l] = cond_v[l] * real
+        out[HALF + l] = real * source_v[l]
+    for l in range(0, HALF, 2):
+        out[2 * HALF + l // 2] = jnp.where(black, pressure_v[l], pltpu.roll(pressure_v[l + 1], 1, 1))
 
 
 def edge_kernel(both, out):
     core = lax.axis_index("zk")
     start = pl.multiple_of(core * 24, 8)
     keep = (lax.broadcasted_iota(jnp.int32, (8, LAN), 0) < 4) == (core == 0)
-    for f in range(3):
-        for l in range(HALF):
-            low = both[0, f, l, pl.ds(start, 8), :]
-            high = both[1, f, l, pl.ds(start, 8), :]
-            out[f, l] = jnp.where(keep, low, pltpu.roll(high, 4, 0))
+    for k in range(PLANES):
+        low = both[0, k, pl.ds(start, 8), :]
+        high = both[1, k, pl.ds(start, 8), :]
+        out[k] = jnp.where(keep, low, pltpu.roll(high, 4, 0))
 
 
 def outer_rows(k):
-    at = ARRAYS * 16 + 8 * OUTER[k]
+    at = OWN + 8 * OUTER[k]
     return slice(at, at + 8)
 
 
@@ -98,6 +110,9 @@
     outer = got[group, outer_rows(k), :]
     if k in ROLLED:
         outer = pltpu.roll(outer, 4, 0)
+    if k == ARRAYS - 1:
+        folded = got[group, OWN - 8 : OWN, :]
+        return jnp.concatenate([folded, north_of(folded), outer], axis=0)
     return jnp.concatenate([got[group, 16 * k : 16 * k + 16, :], outer], axis=0)
 
 
@@ -113,12 +128,14 @@
     inside = jnp.where(core == 0, block > 0, block < lax.axis_size("xy") - 1)
 
     def window(f, l):
-        own = both[l // 8, f, l % 8, pl.ds(own_at, 16), :]
-        near = both[l // 8, f, l % 8, pl.ds(near_at, 8), :]
-        far = jnp.where(inside, halo[1 - core, f, l % 8], 0.0)
+        k = f * HALF + l % HALF if f < 2 else 2 * HALF + l % HALF // 2
+        own = both[l // HALF, k, pl.ds(own_at, 16), :]
+        near = both[l // HALF, k, pl.ds(near_at, 8), :]
+        far = jnp.where(inside, halo[1 - core, k], 0.0)
         if l >= HALF:
             far = pltpu.roll(far, 4, 0)
-        return jnp.concatenate([own, jnp.where(from_near, near, far)], axis=0)
+        value = jnp.concatenate([own, jnp.where(from_near, near, far)], axis=0)
+        return north_of(value) if f == 2 and l % 2 == 1 else value
 
     for l in range(LEV):
         w = window(0, l)
@@ -216,8 +233,10 @@
     for peer in range(4):
         last = jnp.where(chip < peer, upward, downward)
         for k in range(ARRAYS):
-            value = common[k] if k < ARRAYS - 1 else last
-            send[peer, 16 * k : 16 * k + 16, :] = value[0:16]
+            if k < ARRAYS - 1:
+                send[peer, 16 * k : 16 * k + 16, :] = common[k][0:16]
+            else:
+                send[peer, OWN - 8 : OWN, :] = jnp.where(red[0:8], last[0:8], south_of(last[8:16]))
             if k in ROLLED:
                 continue
             tile = outer[k]
@@ -253,7 +272,7 @@
     return out
 
 
-def second_kernel(got, ef, nf, vf, dg, fr, rc, mm, al, be, ga, out, ends, heat, full, res):
+def second_kernel(got, ef, nf, vf, dg, fr, rc, mm, al, be, ga, keep, give, out, ends, heat, full, res):
     chip = lax.axis_index("zc")
     row, lane, red = iotas()
     last_lane = lane == LAN - 1
@@ -306,7 +325,7 @@
         cur = res[l] + mm[l] * cur
         full[l + 2] = jnp.where(red, full[l + 2], cur)
     for l in range(LEV):
-        out[l] = full[l + 2, 0:16, :]
+        out[l // HALF, l % HALF] = full[l + 2, 0:16, :]
 
     for side in (0, 1):
         near_chip = jnp.maximum(chip - 1, 0) if side == 0 else jnp.minimum(chip + 1, 3)
@@ -353,18 +372,31 @@
         e = east_of(s)
         s = 0.125 * (west_of(s) + 3.0 * s + 3.0 * e + east_of(e))
         res[z] = jnp.dot(s, weights, precision=lax.Precision.HIGHEST, preferred_element_type=F32)
-        out[LEV + big] = jnp.concatenate(
-            [res[z, pl.ds(0, 8, stride=2), :], jnp.zeros((8, LAN), F32)], axis=0
-        )
-
-
-def last_kernel(both, relaxed, coarse):
+        pair = res[z, pl.ds(0, 8, stride=2), :]
+        out[big // 4, HALF + big % 4] = jnp.concatenate([pair, pair], axis=0)
     core = lax.axis_index("zk")
-    for j in range(2):
-        for l in range(8):
-            relaxed[l, 16 * j : 16 * j + 16, :] = both[j, core * 8 + l]
-        for big in range(4):
-            coarse[big, 8 * j : 8 * j + 8, :] = both[j, LEV + core * 4 + big, 0:8, 0:64]
+    keep[...] = out[core]
+    give[...] = out[1 - core]
+
+
+def last_kernel(both, keep, relaxed, coarse, mine, sems):
+    core = lax.axis_index("zk")
+    other = 1 - core
+    copies = []
+    for k in range(PIECES):
+        part = pl.ds(k * HALF // PIECES, HALF // PIECES)
+        for n, (side, here) in enumerate(((core, keep), (other, both.at[other]))):
+            there = relaxed.at[part, pl.ds(pl.multiple_of(side * 16, 8), 16), :]
+            copies.append(pltpu.make_async_copy(here.at[part], there, sems.at[k, n]))
+    for copy in copies:
+        copy.start()
+    for big in range(4):
+        mine[big, pl.ds(pl.multiple_of(core * 8, 8), 8), :] = keep[HALF + big, 0:8, 0:64]
+        mine[big, pl.ds(pl.multiple_of(other * 8, 8), 8), :] = both[other, HALF + big, 0:8, 0:64]
+    copies.append(pltpu.make_async_copy(mine, coarse, sems.at[PIECES, 0]))
+    copies[-1].start()
+    for copy in copies:
+        copy.wait()
 
 
 def restriction_matrix():
@@ -389,7 +421,7 @@
             kernel,
             out_shape=[jax.ShapeDtypeStruct(s, F32) if plain else pltpu.VMEM(s, F32) for s in shapes],
             in_specs=[main if ends == "first" else vm] * len(args),
-            out_specs=[vm] * len(shapes),
+            out_specs=[main if ends == "last" else vm] * len(shapes),
             scratch_shapes=scratch,
             name=name,
             compiler_params=pltpu.CompilerParams(vmem_limit_bytes=SCOPED),
@@ -420,23 +452,33 @@
     (mine,) = call(
         weigh_kernel,
         "weigh",
-        [(3,) + block],
-        [vmem(block, F32), vmem(block, F32), vmem(block, jnp.int32), pltpu.SemaphoreType.DMA((4,))],
+        [(PLANES, 32, LAN)],
+        [vmem(block, t) for t in (F32, F32, jnp.int32, F32)] + [pltpu.SemaphoreType.DMA((PIECES, 4))],
         ends="first",
     )(source, conductivity, fluid, pressure)
     both = lax.all_gather(mine, "zk", axis=0, tiled=False)
-    (edge,) = call(edge_kernel, "edge", [(3, HALF, 8, LAN)])(both)
+    (edge,) = call(edge_kernel, "edge", [(PLANES, 8, LAN)])(both)
     halo = lax.all_gather(edge, AXES, axis=0, tiled=False, axis_index_groups=side_by_side())
     send, *fields = call(first_kernel, "first", [(4, SENT, LAN)] + [field] * 10)(both, halo)
     got = lax.all_to_all(send, "zc", 0, 0, tiled=False)
-    (done,) = call(
+    part = (HALF + HALF // 2, 16, LAN)
+    keep, give = call(
         second_kernel,
         "second",
-        [(LEV + LEV // 2, 16, LAN)],
-        [vmem((8,) + cell, F32)] * 2 + [vmem((LEV + 4,) + cell, F32), vmem((LEV + 2,) + cell, F32)],
+        [part, part],
+        [vmem((2,) + part, F32)]
+        + [vmem((8,) + cell, F32)] * 2
+        + [vmem((LEV + 4,) + cell, F32), vmem((LEV + 2,) + cell, F32)],
     )(got, *fields)
-    ends = lax.all_gather(done, "zk", axis=0, tiled=False)
-    relaxed, coarse = call(last_kernel, "last", [block, (4, 16, LAN // 2)], ends="last")(ends)
+    ends = lax.all_gather(give, "zk", axis=0, tiled=False)
+    coarse = (HALF // 2, 16, LAN // 2)
+    relaxed, coarse = call(
+        last_kernel,
+        "last",
+        [block, coarse],
+        [vmem(coarse, F32), pltpu.SemaphoreType.DMA((PIECES + 1, 2))],
+        ends="last",
+    )(ends, keep)
     return relaxed, coarse
 
 

time: 35.3 us -> 35.3 us (level)
  Pallas kernels: 3.76 us -> 4.34 us
  blocking collectives: 30.6 us -> 30.1 us
    pallas_call x5, Pallas kernels: 3.76 us -> 4.34 us  [run(): pl.pallas_call(kernel, out_shape=[jax.ShapeDtypeStruct(s, F32) if plain e...]
where the time goes in v7:
time: 35.3 us; the launch traced here: 35.1 us
  blocking collectives  30.1 us (85%)
  Pallas kernels  4.34 us (12%)
  between operations  0.65 us (2%)
    all_to_all x1, blocking collectives, shards(): got = lax.all_to_all(send, 'zc', 0, 0, tiled=False)  11.8 us
    all_gather x1, blocking collectives, shards(): ends = lax.all_gather(give, 'zk', axis=0, tiled=False)  10.6 us
    all_gather x1, blocking collectives, shards(): lax.all_gather(edge, AXES, axis=0, tiled=False, axis_index_groups=side_by...  5.13 us
    pallas_call x5, Pallas kernels, run(): pl.pallas_call(kernel, out_shape=[jax.ShapeDtypeStruct(s, F32) if plain e...  4.34 us
    all_gather x1, blocking collectives, shards(): both = lax.all_gather(mine, 'zk', axis=0, tiled=False)  2.58 us

profile of v7, /device:TPU:57, one launch (start us, length us, event | category | flops | bytes accessed | tf_op | source)
XLA Modules:
  0.0 35.1 jit_solution(10355084292075279988)
XLA Ops:
  0.6 1.2 %weigh.1 = f32[20,32,128]{2,1,0:T(8,128)S(1)} custom-call(f32[8,32,128]{2,1,0:T(8,128)} %source.1, f32[8,32,128]{2,1,0:T(8,128)} %cond.1, s32[8,32,128]{2,1,0:T(8,128)} %fluid.1, f32[8,32,128]{2,1,0:T(8,128)} %pressure.1), custom_call_target="tpu_custom_call" | custom-call | tf_op jit(solution)/shard_map/weigh/pallas_call | solution.py:420
  1.9 2.6 %all-gather = f32[40,32,128]{2,1,0:T(8,128)S(1)} all-gather(f32[20,32,128]{2,1,0:T(8,128)S(1)} %weigh.1), channel_id=2, replica_groups=mesh['zc'=4,'zk'=2,'xy'=64] {'zk'}, dimensions={0}, use_global_device_ids=true | all-gather | bytes 983040 | tf_op jit(solution)/shard_map/all_gather | solution.py:459
  4.5 5.1 %all-gather.1 = f32[40,8,128]{2,1,0:T(8,128)S(1)} all-gather(f32[20,8,128]{2,1,0:T(8,128)S(1)} %edge.1), channel_id=3, replica_groups={{1,64},{2,65},{3,66},{4,67},{5,68},{6,69},{7,70},{8,71},{9,72},{10,73},..., dimensions={0}, use_global_device_ids=true | all-gather | bytes 245760 | tf_op jit(solution)/shard_map/all_gather | solution.py:461
  9.6 1.2 %first.1 = (f32[4,352,128]{2,1,0:T(8,128)S(1)}, f32[16,24,128]{2,1,0:T(8,128)S(1)}, f32[16,24,128]{2,1,0:T(8,128)S(1)}, f32[16,24,128]{2,1,0:T(8,128)S(1)}, f32[...) custom-call(f32[2,20,32,128]{3,2,1,0:T(8,128)S(1)} %bitcast.4, ...), custom_call_target="tpu_custom_call" | custom-call | tf_op jit(solution)/shard_map/first/pallas_call | solution.py:420
  10.9 11.8 %all_to_all.5.got = f32[4,352,128]{2,1,0:T(8,128)S(1)} all-to-all(f32[4,352,128]{2,1,0:T(8,128)S(1)} %get-tuple-element.15), channel_id=1, replica_groups=mesh['zc'=4,'zk'=2,'xy'=64] {'zc'}, dimensions={0} | all-to-all | bytes 1441792 | tf_op jit(solution)/shard_map/all_to_all | solution.py:463
  22.7 1.1 %second.1 = (f32[12,16,128]{2,1,0:T(8,128)S(1)}, f32[12,16,128]{2,1,0:T(8,128)S(1)}) custom-call(f32[4,352,128]{2,1,0:T(8,128)S(1)} %all_to_all.5.got, f32[16,24,128]{2,1,0:T(8,128)S(1)} %get-tuple-element.16.ef, f32[16,24,128]{2,1,0:T(8,128)S(1)} %get-tuple-element.17.nf, f32[16,24,128]{2,1,0:T(8,128)S(1)} %get-tuple-element.18.vf, ...), custom_call_target="tpu_custom_call" | custom-call | tf_op jit(solution)/shard_map/second/pallas_call | solution.py:420
  23.8 10.6 %all-gather.2 = f32[24,16,128]{2,1,0:T(8,128)S(1)} all-gather(f32[12,16,128]{2,1,0:T(8,128)S(1)} %get-tuple-element.26), channel_id=4, replica_groups=mesh['zc'=4,'zk'=2,'xy'=64] {'zk'}, dimensions={0}, use_global_device_ids=true | all-gather | bytes 294912 | tf_op jit(solution)/shard_map/all_gather | solution.py:473
  34.3 0.7 %last.1 = (f32[8,32,128]{2,1,0:T(8,128)}, f32[4,16,64]{2,1,0:T(8,128)}) custom-call(f32[2,12,16,128]{3,2,1,0:T(8,128)S(1)} %bitcast.5, f32[12,16,128]{2,1,0:T(8,128)S(1)} %get-tuple-element.27.keep), custom_call_target="tpu_custom_call" | custom-call | tf_op jit(solution)/shard_map/last/pallas_call | solution.py:420
  (1 shorter events, 0.0 us)

commit v8 on v7

--- a/solution.py
+++ b/solution.py
@@ -15,7 +15,6 @@
 LEV = 16
 HALF = 8
 PLANES = 20
-PIECES = 4
 ARRAYS = 16
 OWN = ARRAYS * 16 - 8
 OUTER = (0, 1, 2, 3, 4, 5, 6, 7, 8, 9, 10, 11, 11, 12, 12, 7)
@@ -49,12 +48,6 @@
     return row, lane, red
 
 
-def black_mask(rows):
-    row = lax.broadcasted_iota(jnp.int32, (rows, LAN), 0)
-    lane = lax.broadcasted_iota(jnp.int32, (rows, LAN), 1)
-    return ((row + lane) & 1) == 1
-
-
 def side_faces(w, last_lane):
     east = jnp.sqrt(w * east_of(w))
     north = jnp.where(last_lane, 0.0, jnp.sqrt(w * north_of(w)))
@@ -71,24 +64,25 @@
 
 
 def weigh_kernel(source, cond, fluid, pressure, out, source_v, cond_v, fluid_v, pressure_v, sems):
-    parts = [pl.ds(k * HALF // PIECES, HALF // PIECES) for k in range(PIECES)]
-    copies = []
-    for k, part in enumerate(parts):
-        for n, (there, here) in enumerate(
-            ((cond, cond_v), (fluid, fluid_v), (source, source_v), (pressure, pressure_v))
-        ):
-            copies.append(pltpu.make_async_copy(there.at[part], here.at[part], sems.at[k, n]))
+    copies = [
+        pltpu.make_async_copy(cond, cond_v, sems.at[0]),
+        pltpu.make_async_copy(fluid, fluid_v, sems.at[1]),
+        pltpu.make_async_copy(source, source_v, sems.at[2]),
+        pltpu.make_async_copy(pressure, pressure_v, sems.at[3]),
+    ]
     for copy in copies:
         copy.start()
     for copy in copies:
         copy.wait()
-    black = black_mask(32)
     for l in range(HALF):
         real = fluid_v[l].astype(F32)
         out[l] = cond_v[l] * real
         out[HALF + l] = real * source_v[l]
+    row = lax.broadcasted_iota(jnp.int32, (32, LAN), 0)
+    lane = lax.broadcasted_iota(jnp.int32, (32, LAN), 1)
+    black = ((row + lane) & 1) == 1
     for l in range(0, HALF, 2):
-        out[2 * HALF + l // 2] = jnp.where(black, pressure_v[l], pltpu.roll(pressure_v[l + 1], 1, 1))
+        out[2 * HALF + l // 2] = jnp.where(black, pressure_v[l], south_of(pressure_v[l + 1]))
 
 
 def edge_kernel(both, out):
@@ -127,41 +121,46 @@
     block = lax.axis_index("xy")
     inside = jnp.where(core == 0, block > 0, block < lax.axis_size("xy") - 1)
 
-    def window(f, l):
-        k = f * HALF + l % HALF if f < 2 else 2 * HALF + l % HALF // 2
+    def window(k, l):
         own = both[l // HALF, k, pl.ds(own_at, 16), :]
         near = both[l // HALF, k, pl.ds(near_at, 8), :]
         far = jnp.where(inside, halo[1 - core, k], 0.0)
         if l >= HALF:
             far = pltpu.roll(far, 4, 0)
-        value = jnp.concatenate([own, jnp.where(from_near, near, far)], axis=0)
-        return north_of(value) if f == 2 and l % 2 == 1 else value
-
+        return jnp.concatenate([own, jnp.where(from_near, near, far)], axis=0)
+
+    w = window(0, 0)
+    w0 = w
+    below = None
     for l in range(LEV):
-        w = window(0, l)
         east, north = side_faces(w, last_lane)
         ef[l] = east
         nf[l] = north
+        south = south_of(north)
+        d = absorption + (west_of(east) + east + south + north)
+        fluid = w > 0.0
+        if below is not None:
+            d = d + below
+        v = below
+        if l < LEV - 1:
+            w_next = window((l + 1) % HALF, l + 1)
+            below = vertical_ratio * jnp.sqrt(w_next * w)
+            vf[l + 1] = below
+            d = d + below
+            w = w_next
+        d = jnp.where(fluid, d, 1.0)
+        dg[l] = d
+        f = window(HALF + l % HALF, l)
+        fr[l] = f
+        if l % 2 == 0:
+            old = window(2 * HALF + l % HALF // 2, l)
+            old_up = north_of(old)
+            b = f + ((west_of(east * old) + east * east_of(old)) + (south * south_of(old) + north * old_up))
+        else:
+            b = f + ((west_of(east * old_up) + east * east_of(old_up)) + (south * old + north * north_of(old_up)))
         if l == 0:
-            w0 = w
-            vf[0] = jnp.zeros_like(w)
-        else:
-            vf[l] = vertical_ratio * jnp.sqrt(w * w_below)
-        w_below = w
-        fluid = jnp.where(w > 0.0, 1.0, 0.0)
-        dg[l] = fluid * (absorption + (west_of(east) + east + south_of(north) + north)) + (1.0 - fluid)
-        fr[l] = window(1, l)
-    w15 = w_below
-    heat0 = fr[0] + horizontal(ef[0], nf[0], window(2, 0))
-    d0 = dg[0] + vf[1]
-    dg[0] = d0
-    for l in range(1, LEV):
-        d = dg[l] + vf[l]
-        if l < LEV - 1:
-            d = d + vf[l + 1]
-        dg[l] = d
-        b = fr[l] + horizontal(ef[l], nf[l], window(2, l))
-        v = vf[l]
+            heat0, d0 = b, d
+            continue
         if l == 1:
             dd, bb, g = d, b, v
         elif l < LEV - 1:
@@ -170,36 +169,30 @@
             g = mult * g
         if l < LEV - 1:
             rcp = 1.0 / dd
-            mult = vf[l + 1] * rcp
+            mult = below * rcp
             rc[l] = rcp
             mm[l] = mult
             al[l] = bb * rcp
             be[l] = g * rcp
-    heat15 = b
-    alpha = jnp.where(red, al[LEV - 2], 0.0)
-    beta = be[LEV - 2]
-    gamma = mm[LEV - 2]
-    al[LEV - 2] = alpha
-    ga[LEV - 2] = gamma
-    for l in range(LEV - 3, 0, -1):
-        mult = mm[l]
-        alpha = jnp.where(red, al[l] + mult * alpha, 0.0)
-        beta = be[l] + mult * beta
-        gamma = mult * gamma
-        al[l] = alpha
-        be[l] = beta
-        ga[l] = gamma
-    v1 = vf[1]
-    v15 = vf[LEV - 1]
-    self_low = v1 * be[1]
-    self_high = v15 * ga[LEV - 2]
+    heat15, d15, w15 = b, d, w
     e_tt, e_bb = ef[0], ef[LEV - 1]
     n_tt, n_bb = nf[0], nf[LEV - 1]
     e_tb = e_bt = n_tb = n_bt = jnp.zeros((WIN, LAN), F32)
     con_low = fr[0]
     con_high = fr[LEV - 1]
-    for l in range(1, LEV - 1):
-        beta, gamma, alpha = be[l], ga[l], al[l]
+    for l in range(LEV - 2, 0, -1):
+        mult = mm[l]
+        if l == LEV - 2:
+            alpha, beta, gamma = al[l], be[l], mult
+            high_share = beta
+        else:
+            alpha = al[l] + mult * alpha
+            beta = be[l] + mult * beta
+            gamma = mult * gamma
+        alpha = jnp.where(red, alpha, 0.0)
+        al[l] = alpha
+        be[l] = beta
+        ga[l] = gamma
         east, north = ef[l], nf[l]
         there_b, there_g = east_of(beta), east_of(gamma)
         mine_b, mine_g = east * beta, east * gamma
@@ -207,18 +200,24 @@
         e_tb = e_tb + mine_b * there_g
         e_bt = e_bt + mine_g * there_b
         e_bb = e_bb + mine_g * there_g
+        b = fr[l] + horizontal(east, north, alpha)
+        con_low = con_low + beta * b
+        con_high = con_high + gamma * b
+    for l in range(LEV - 2, 0, -1):
+        alpha, beta, gamma, east, north = al[l], be[l], ga[l], ef[l], nf[l]
         there_b, there_g = north_of(beta), north_of(gamma)
         mine_b, mine_g = north * beta, north * gamma
         n_tt = n_tt + mine_b * there_b
         n_tb = n_tb + mine_b * there_g
         n_bt = n_bt + mine_g * there_b
         n_bb = n_bb + mine_g * there_g
-        b = fr[l] + horizontal(east, north, alpha)
-        con_low = con_low + beta * b
-        con_high = con_high + gamma * b
+    v1 = vf[1]
+    v15 = vf[LEV - 1]
+    self_low = v1 * be[1]
+    self_high = v15 * ga[LEV - 2]
     own_low = v1 * al[1]
     own_high = v15 * al[LEV - 2]
-    common = [d0 - self_low, v15 * be[LEV - 2], dg[LEV - 1] - self_high, w0, w15]
+    common = [d0 - self_low, v15 * be[LEV - 2], d15 - self_high, w0, w15]
     common += [jnp.where(red, heat0 + own_low, con_low), jnp.where(red, heat15 + own_high, con_high)]
     common += [e_tt, e_tb, e_bt, e_bb, n_tt, n_tb, n_bt, n_bb]
     chip = lax.axis_index("zc")
@@ -379,24 +378,16 @@
     give[...] = out[1 - core]
 
 
-def last_kernel(both, keep, relaxed, coarse, mine, sems):
+def last_kernel(both, keep, relaxed, coarse):
     core = lax.axis_index("zk")
     other = 1 - core
-    copies = []
-    for k in range(PIECES):
-        part = pl.ds(k * HALF // PIECES, HALF // PIECES)
-        for n, (side, here) in enumerate(((core, keep), (other, both.at[other]))):
-            there = relaxed.at[part, pl.ds(pl.multiple_of(side * 16, 8), 16), :]
-            copies.append(pltpu.make_async_copy(here.at[part], there, sems.at[k, n]))
-    for copy in copies:
-        copy.start()
-    for big in range(4):
-        mine[big, pl.ds(pl.multiple_of(core * 8, 8), 8), :] = keep[HALF + big, 0:8, 0:64]
-        mine[big, pl.ds(pl.multiple_of(other * 8, 8), 8), :] = both[other, HALF + big, 0:8, 0:64]
-    copies.append(pltpu.make_async_copy(mine, coarse, sems.at[PIECES, 0]))
-    copies[-1].start()
-    for copy in copies:
-        copy.wait()
+    for side, of in ((core, lambda k: keep[k]), (other, lambda k: both[other, k])):
+        at = pl.multiple_of(side * 16, 8)
+        for l in range(HALF):
+            relaxed[l, pl.ds(at, 16), :] = of(l)
+        at = pl.multiple_of(side * 8, 8)
+        for big in range(4):
+            coarse[big, pl.ds(at, 8), :] = of(HALF + big)[0:8, 0:64]
 
 
 def restriction_matrix():
@@ -421,7 +412,7 @@
             kernel,
             out_shape=[jax.ShapeDtypeStruct(s, F32) if plain else pltpu.VMEM(s, F32) for s in shapes],
             in_specs=[main if ends == "first" else vm] * len(args),
-            out_specs=[main if ends == "last" else vm] * len(shapes),
+            out_specs=[vm] * len(shapes),
             scratch_shapes=scratch,
             name=name,
             compiler_params=pltpu.CompilerParams(vmem_limit_bytes=SCOPED),
@@ -453,7 +444,7 @@
         weigh_kernel,
         "weigh",
         [(PLANES, 32, LAN)],
-        [vmem(block, t) for t in (F32, F32, jnp.int32, F32)] + [pltpu.SemaphoreType.DMA((PIECES, 4))],
+        [vmem(block, t) for t in (F32, F32, jnp.int32, F32)] + [pltpu.SemaphoreType.DMA((4,))],
         ends="first",
     )(source, conductivity, fluid, pressure)
     both = lax.all_gather(mine, "zk", axis=0, tiled=False)
@@ -476,7 +467,6 @@
         last_kernel,
         "last",
         [block, coarse],
-        [vmem(coarse, F32), pltpu.SemaphoreType.DMA((PIECES + 1, 2))],
         ends="last",
     )(ends, keep)
     return relaxed, coarse

time: 35.3 us -> 35.1 us (level)
  no operation moved by 1% of the time
where the time goes in v8:
time: 35.1 us; the launch traced here: 34.9 us
  blocking collectives  30.1 us (86%)
  Pallas kernels  4.15 us (12%)
  between operations  0.65 us (2%)
    all_to_all x1, blocking collectives, shards(): got = lax.all_to_all(send, 'zc', 0, 0, tiled=False)  11.8 us
    all_gather x1, blocking collectives, shards(): ends = lax.all_gather(give, 'zk', axis=0, tiled=False)  10.6 us
    all_gather x1, blocking collectives, shards(): lax.all_gather(edge, AXES, axis=0, tiled=False, axis_index_groups=side_by...  5.13 us
    pallas_call x5, Pallas kernels, run(): pl.pallas_call(kernel, out_shape=[jax.ShapeDtypeStruct(s, F32) if plain e...  4.15 us
    all_gather x1, blocking collectives, shards(): both = lax.all_gather(mine, 'zk', axis=0, tiled=False)  2.58 us

profile of v8, /device:TPU:57, one launch (start us, length us, event | category | flops | bytes accessed | tf_op | source)
XLA Modules:
  0.0 34.9 jit_solution(3650020000963191572)
XLA Ops:
  0.6 1.2 %weigh.1 = f32[20,32,128]{2,1,0:T(8,128)S(1)} custom-call(f32[8,32,128]{2,1,0:T(8,128)} %source.1, f32[8,32,128]{2,1,0:T(8,128)} %cond.1, s32[8,32,128]{2,1,0:T(8,128)} %fluid.1, f32[8,32,128]{2,1,0:T(8,128)} %pressure.1), custom_call_target="tpu_custom_call" | custom-call | tf_op jit(solution)/shard_map/weigh/pallas_call | solution.py:411
  1.9 2.6 %all-gather = f32[40,32,128]{2,1,0:T(8,128)S(1)} all-gather(f32[20,32,128]{2,1,0:T(8,128)S(1)} %weigh.1), channel_id=2, replica_groups=mesh['zc'=4,'zk'=2,'xy'=64] {'zk'}, dimensions={0}, use_global_device_ids=true | all-gather | bytes 983040 | tf_op jit(solution)/shard_map/all_gather | solution.py:450
  4.5 5.1 %all-gather.1 = f32[40,8,128]{2,1,0:T(8,128)S(1)} all-gather(f32[20,8,128]{2,1,0:T(8,128)S(1)} %edge.1), channel_id=3, replica_groups={{1,64},{2,65},{3,66},{4,67},{5,68},{6,69},{7,70},{8,71},{9,72},{10,73},..., dimensions={0}, use_global_device_ids=true | all-gather | bytes 245760 | tf_op jit(solution)/shard_map/all_gather | solution.py:452
  9.6 1.1 %first.1 = (f32[4,352,128]{2,1,0:T(8,128)S(1)}, f32[16,24,128]{2,1,0:T(8,128)S(1)}, f32[16,24,128]{2,1,0:T(8,128)S(1)}, f32[16,24,128]{2,1,0:T(8,128)S(1)}, f32[...) custom-call(f32[2,20,32,128]{3,2,1,0:T(8,128)S(1)} %bitcast.4, ...), custom_call_target="tpu_custom_call" | custom-call | tf_op jit(solution)/shard_map/first/pallas_call | solution.py:411
  10.7 11.8 %all_to_all.5.got = f32[4,352,128]{2,1,0:T(8,128)S(1)} all-to-all(f32[4,352,128]{2,1,0:T(8,128)S(1)} %get-tuple-element.15), channel_id=1, replica_groups=mesh['zc'=4,'zk'=2,'xy'=64] {'zc'}, dimensions={0} | all-to-all | bytes 1441792 | tf_op jit(solution)/shard_map/all_to_all | solution.py:454
  22.5 1.1 %second.1 = (f32[12,16,128]{2,1,0:T(8,128)S(1)}, f32[12,16,128]{2,1,0:T(8,128)S(1)}) custom-call(f32[4,352,128]{2,1,0:T(8,128)S(1)} %all_to_all.5.got, f32[16,24,128]{2,1,0:T(8,128)S(1)} %get-tuple-element.16.ef, f32[16,24,128]{2,1,0:T(8,128)S(1)} %get-tuple-element.17.nf, f32[16,24,128]{2,1,0:T(8,128)S(1)} %get-tuple-element.18.vf, ...), custom_call_target="tpu_custom_call" | custom-call | tf_op jit(solution)/shard_map/second/pallas_call | solution.py:411
  23.6 10.6 %all-gather.2 = f32[24,16,128]{2,1,0:T(8,128)S(1)} all-gather(f32[12,16,128]{2,1,0:T(8,128)S(1)} %get-tuple-element.26), channel_id=4, replica_groups=mesh['zc'=4,'zk'=2,'xy'=64] {'zk'}, dimensions={0}, use_global_device_ids=true | all-gather | bytes 294912 | tf_op jit(solution)/shard_map/all_gather | solution.py:464
  34.2 0.7 %last.1 = (f32[8,32,128]{2,1,0:T(8,128)}, f32[4,16,64]{2,1,0:T(8,128)}) custom-call(f32[2,12,16,128]{3,2,1,0:T(8,128)S(1)} %bitcast.5, f32[12,16,128]{2,1,0:T(8,128)S(1)} %get-tuple-element.27.keep), custom_call_target="tpu_custom_call" | custom-call | tf_op jit(solution)/shard_map/last/pallas_call | solution.py:411
  (1 shorter events, 0.0 us)

commit v9 on v6

--- a/solution.py
+++ b/solution.py
@@ -15,9 +15,10 @@
 LEV = 16
 HALF = 8
 ARRAYS = 16
-OUTER = (0, 1, 2, 3, 4, 5, 6, 7, 8, 9, 10, 11, 11, 12, 12, 7)
+OWN = ARRAYS * 16 - 8
+OUTER = (0, 1, 2, 3, 4, 5, None, 6, 7, 8, 9, 10, 10, 11, 11, 6)
 ROLLED = (12, 14, 15)
-SENT = ARRAYS * 16 + 13 * 8
+SENT = OWN + 12 * 8
 WIN = 24
 LAN = 128
 F32 = jnp.float32
@@ -90,14 +91,22 @@
 
 
 def outer_rows(k):
-    at = ARRAYS * 16 + 8 * OUTER[k]
+    at = OWN + 8 * OUTER[k]
     return slice(at, at + 8)
 
 
 def received(got, group, k):
-    outer = got[group, outer_rows(k), :]
+    if k == 6:
+        east = pltpu.roll(got[group, outer_rows(8), :], 6, 0)
+        west = pltpu.roll(got[group, outer_rows(9), :], 3, 0)
+        outer = jnp.where(lax.broadcasted_iota(jnp.int32, (8, LAN), 0) < 3, east, west)
+    else:
+        outer = got[group, outer_rows(k), :]
     if k in ROLLED:
         outer = pltpu.roll(outer, 4, 0)
+    if k == ARRAYS - 1:
+        folded = got[group, OWN - 8 : OWN, :]
+        return jnp.concatenate([folded, pltpu.roll(folded, 7, 0), outer], axis=0)
     return jnp.concatenate([got[group, 16 * k : 16 * k + 16, :], outer], axis=0)
 
 
@@ -213,12 +222,16 @@
     for k in (11, 13):
         outer[k] = jnp.where(inner, outer[k], pltpu.roll(outer[k + 1], 4, 0))
     kept = (row8 < 2) | (row8 > 4)
+    outer[8] = jnp.where(kept, outer[8], pltpu.roll(outer[6], 2, 0))
+    outer[9] = jnp.where(kept, outer[9], pltpu.roll(outer[6], 5, 0))
     for peer in range(4):
         last = jnp.where(chip < peer, upward, downward)
         for k in range(ARRAYS):
-            value = common[k] if k < ARRAYS - 1 else last
-            send[peer, 16 * k : 16 * k + 16, :] = value[0:16]
-            if k in ROLLED:
+            if k < ARRAYS - 1:
+                send[peer, 16 * k : 16 * k + 16, :] = common[k][0:16]
+            else:
+                send[peer, OWN - 8 : OWN, :] = jnp.where(red[0:8], last[0:8], pltpu.roll(last[8:16], 1, 0))
+            if k in ROLLED or k == 6:
                 continue
             tile = outer[k]
             if k == 7:
@@ -253,7 +266,7 @@
     return out
 
 
-def second_kernel(got, ef, nf, vf, dg, fr, rc, mm, al, be, ga, out, ends, heat, full, res):
+def second_kernel(got, ef, nf, vf, dg, fr, rc, mm, al, be, ga, keep, give, out, ends, heat, full, res):
     chip = lax.axis_index("zc")
     row, lane, red = iotas()
     last_lane = lane == LAN - 1
@@ -306,7 +319,7 @@
         cur = res[l] + mm[l] * cur
         full[l + 2] = jnp.where(red, full[l + 2], cur)
     for l in range(LEV):
-        out[l] = full[l + 2, 0:16, :]
+        out[l // HALF, l % HALF] = full[l + 2, 0:16, :]
 
     for side in (0, 1):
         near_chip = jnp.maximum(chip - 1, 0) if side == 0 else jnp.minimum(chip + 1, 3)
@@ -353,18 +366,23 @@
         e = east_of(s)
         s = 0.125 * (west_of(s) + 3.0 * s + 3.0 * e + east_of(e))
         res[z] = jnp.dot(s, weights, precision=lax.Precision.HIGHEST, preferred_element_type=F32)
-        out[LEV + big] = jnp.concatenate(
-            [res[z, pl.ds(0, 8, stride=2), :], jnp.zeros((8, LAN), F32)], axis=0
-        )
-
-
-def last_kernel(both, relaxed, coarse):
+        pair = res[z, pl.ds(0, 8, stride=2), :]
+        out[big // 4, HALF + big % 4] = jnp.concatenate([pair, pair], axis=0)
     core = lax.axis_index("zk")
-    for j in range(2):
-        for l in range(8):
-            relaxed[l, 16 * j : 16 * j + 16, :] = both[j, core * 8 + l]
+    keep[...] = out[core]
+    give[...] = out[1 - core]
+
+
+def last_kernel(both, keep, relaxed, coarse):
+    core = lax.axis_index("zk")
+    other = 1 - core
+    for side, of in ((core, lambda k: keep[k]), (other, lambda k: both[other, k])):
+        at = pl.multiple_of(side * 16, 8)
+        for l in range(HALF):
+            relaxed[l, pl.ds(at, 16), :] = of(l)
+        at = pl.multiple_of(side * 8, 8)
         for big in range(4):
-            coarse[big, 8 * j : 8 * j + 8, :] = both[j, LEV + core * 4 + big, 0:8, 0:64]
+            coarse[big, pl.ds(at, 8), :] = of(HALF + big)[0:8, 0:64]
 
 
 def restriction_matrix():
@@ -429,14 +447,23 @@
     halo = lax.all_gather(edge, AXES, axis=0, tiled=False, axis_index_groups=side_by_side())
     send, *fields = call(first_kernel, "first", [(4, SENT, LAN)] + [field] * 10)(both, halo)
     got = lax.all_to_all(send, "zc", 0, 0, tiled=False)
-    (done,) = call(
+    part = (HALF + HALF // 2, 16, LAN)
+    keep, give = call(
         second_kernel,
         "second",
-        [(LEV + LEV // 2, 16, LAN)],
-        [vmem((8,) + cell, F32)] * 2 + [vmem((LEV + 4,) + cell, F32), vmem((LEV + 2,) + cell, F32)],
+        [part, part],
+        [vmem((2,) + part, F32)]
+        + [vmem((8,) + cell, F32)] * 2
+        + [vmem((LEV + 4,) + cell, F32), vmem((LEV + 2,) + cell, F32)],
     )(got, *fields)
-    ends = lax.all_gather(done, "zk", axis=0, tiled=False)
-    relaxed, coarse = call(last_kernel, "last", [block, (4, 16, LAN // 2)], ends="last")(ends)
+    ends = lax.all_gather(give, "zk", axis=0, tiled=False)
+    coarse = (HALF // 2, 16, LAN // 2)
+    relaxed, coarse = call(
+        last_kernel,
+        "last",
+        [block, coarse],
+        ends="last",
+    )(ends, keep)
     return relaxed, coarse
 
 

time: 35.3 us -> 34.9 us (0.989)
  no operation moved by 1% of the time
where the time goes in v9:
time: 34.9 us; the launch traced here: 34.7 us
  blocking collectives  30.3 us (87%)
  Pallas kernels  3.8 us (11%)
  between operations  0.65 us (2%)
    all_to_all x1, blocking collectives, shards(): got = lax.all_to_all(send, 'zc', 0, 0, tiled=False)  11.7 us
    all_gather x1, blocking collectives, shards(): ends = lax.all_gather(give, 'zk', axis=0, tiled=False)  10.6 us
    all_gather x1, blocking collectives, shards(): lax.all_gather(edge, AXES, axis=0, tiled=False, axis_index_groups=side_by...  5.31 us
    pallas_call x5, Pallas kernels, run(): pl.pallas_call(kernel, out_shape=[jax.ShapeDtypeStruct(s, F32) if plain e...  3.8 us
    all_gather x1, blocking collectives, shards(): both = lax.all_gather(mine, 'zk', axis=0, tiled=False)  2.67 us

profile of v9, /device:TPU:57, one launch (start us, length us, event | category | flops | bytes accessed | tf_op | source)
XLA Modules:
  0.0 34.7 jit_solution(9901214109490082219)
XLA Ops:
  0.6 1.2 %weigh.1 = f32[3,8,32,128]{3,2,1,0:T(8,128)S(1)} custom-call(f32[8,32,128]{2,1,0:T(8,128)} %source.1, f32[8,32,128]{2,1,0:T(8,128)} %cond.1, s32[8,32,128]{2,1,0:T(8,128)} %fluid.1, f32[8,32,128]{2,1,0:T(8,128)} %pressure.1), custom_call_target="tpu_custom_call" | custom-call | tf_op jit(solution)/shard_map/weigh/pallas_call | solution.py:406
  1.8 2.7 %all-gather = f32[6,8,32,128]{3,2,1,0:T(8,128)S(1)} all-gather(f32[3,8,32,128]{3,2,1,0:T(8,128)S(1)} %weigh.1), channel_id=2, replica_groups=mesh['zc'=4,'zk'=2,'xy'=64] {'zk'}, dimensions={0}, use_global_device_ids=true | all-gather | bytes 1179648 | tf_op jit(solution)/shard_map/all_gather | solution.py:445
  4.5 5.3 %all-gather.1 = f32[6,8,8,128]{3,2,1,0:T(8,128)S(1)} all-gather(f32[3,8,8,128]{3,2,1,0:T(8,128)S(1)} %edge.1), channel_id=3, replica_groups={{1,64},{2,65},{3,66},{4,67},{5,68},{6,69},{7,70},{8,71},{9,72},{10,73},..., dimensions={0}, use_global_device_ids=true | all-gather | bytes 294912 | tf_op jit(solution)/shard_map/all_gather | solution.py:447
  9.8 0.9 %first.1 = (f32[4,344,128]{2,1,0:T(8,128)S(1)}, f32[16,24,128]{2,1,0:T(8,128)S(1)}, f32[16,24,128]{2,1,0:T(8,128)S(1)}, f32[16,24,128]{2,1,0:T(8,128)S(1)}, f32[...) custom-call(f32[2,3,8,32,128]{4,3,2,1,0:T(8,128)S(1)} %bitcast.4, ...), custom_call_target="tpu_custom_call" | custom-call | tf_op jit(solution)/shard_map/first/pallas_call | solution.py:406
  10.7 11.7 %all_to_all.5.got = f32[4,344,128]{2,1,0:T(8,128)S(1)} all-to-all(f32[4,344,128]{2,1,0:T(8,128)S(1)} %get-tuple-element.15), channel_id=1, replica_groups=mesh['zc'=4,'zk'=2,'xy'=64] {'zc'}, dimensions={0} | all-to-all | bytes 1409024 | tf_op jit(solution)/shard_map/all_to_all | solution.py:449
  22.4 1.1 %second.1 = (f32[12,16,128]{2,1,0:T(8,128)S(1)}, f32[12,16,128]{2,1,0:T(8,128)S(1)}) custom-call(f32[4,344,128]{2,1,0:T(8,128)S(1)} %all_to_all.5.got, f32[16,24,128]{2,1,0:T(8,128)S(1)} %get-tuple-element.16.ef, f32[16,24,128]{2,1,0:T(8,128)S(1)} %get-tuple-element.17.nf, f32[16,24,128]{2,1,0:T(8,128)S(1)} %get-tuple-element.18.vf, ...), custom_call_target="tpu_custom_call" | custom-call | tf_op jit(solution)/shard_map/second/pallas_call | solution.py:406
  23.5 10.6 %all-gather.2 = f32[24,16,128]{2,1,0:T(8,128)S(1)} all-gather(f32[12,16,128]{2,1,0:T(8,128)S(1)} %get-tuple-element.26), channel_id=4, replica_groups=mesh['zc'=4,'zk'=2,'xy'=64] {'zk'}, dimensions={0}, use_global_device_ids=true | all-gather | bytes 294912 | tf_op jit(solution)/shard_map/all_gather | solution.py:459
  34.0 0.7 %last.1 = (f32[8,32,128]{2,1,0:T(8,128)}, f32[4,16,64]{2,1,0:T(8,128)}) custom-call(f32[2,12,16,128]{3,2,1,0:T(8,128)S(1)} %bitcast.5, f32[12,16,128]{2,1,0:T(8,128)S(1)} %get-tuple-element.27.keep), custom_call_target="tpu_custom_call" | custom-call | tf_op jit(solution)/shard_map/last/pallas_call | solution.py:406
  (1 shorter events, 0.0 us)

commit v10 on v9

--- a/solution.py
+++ b/solution.py
@@ -14,6 +14,7 @@
 
 LEV = 16
 HALF = 8
+PLANES = 20
 ARRAYS = 16
 OWN = ARRAYS * 16 - 8
 OUTER = (0, 1, 2, 3, 4, 5, None, 6, 7, 8, 9, 10, 10, 11, 11, 6)
@@ -62,12 +63,22 @@
     )
 
 
-def weigh_kernel(source, cond, fluid, pressure, out, source_v, cond_v, fluid_v, sems):
+def row_down(tile):
+    row = lax.broadcasted_iota(jnp.int32, (8, LAN), 0)
+    return jnp.where((row & 3) == 0, pltpu.roll(tile, 5, 0), pltpu.roll(tile, 1, 0))
+
+
+def row_up(tile):
+    row = lax.broadcasted_iota(jnp.int32, (8, LAN), 0)
+    return jnp.where((row & 3) == 3, pltpu.roll(tile, 3, 0), pltpu.roll(tile, 7, 0))
+
+
+def weigh_kernel(source, cond, fluid, pressure, out, source_v, cond_v, fluid_v, pressure_v, sems):
     copies = [
         pltpu.make_async_copy(cond, cond_v, sems.at[0]),
         pltpu.make_async_copy(fluid, fluid_v, sems.at[1]),
         pltpu.make_async_copy(source, source_v, sems.at[2]),
-        pltpu.make_async_copy(pressure, out.at[2], sems.at[3]),
+        pltpu.make_async_copy(pressure, pressure_v, sems.at[3]),
     ]
     for copy in copies:
         copy.start()
@@ -75,19 +86,25 @@
         copy.wait()
     for l in range(HALF):
         real = fluid_v[l].astype(F32)
-        out[0, l] = cond_v[l] * real
-        out[1, l] = real * source_v[l]
+        out[l] = cond_v[l] * real
+        out[HALF + l] = real * source_v[l]
+    row = lax.broadcasted_iota(jnp.int32, (8, LAN), 0)
+    lane = lax.broadcasted_iota(jnp.int32, (8, LAN), 1)
+    black = ((row + lane) & 1) == 1
+    for l in range(0, HALF, 2):
+        for t in range(0, 32, 8):
+            tile = slice(t, t + 8)
+            out[2 * HALF + l // 2, tile, :] = jnp.where(black, pressure_v[l, tile, :], row_down(pressure_v[l + 1, tile, :]))
 
 
 def edge_kernel(both, out):
     core = lax.axis_index("zk")
     start = pl.multiple_of(core * 24, 8)
     keep = (lax.broadcasted_iota(jnp.int32, (8, LAN), 0) < 4) == (core == 0)
-    for f in range(3):
-        for l in range(HALF):
-            low = both[0, f, l, pl.ds(start, 8), :]
-            high = both[1, f, l, pl.ds(start, 8), :]
-            out[f, l] = jnp.where(keep, low, pltpu.roll(high, 4, 0))
+    for k in range(PLANES):
+        low = both[0, k, pl.ds(start, 8), :]
+        high = both[1, k, pl.ds(start, 8), :]
+        out[k] = jnp.where(keep, low, pltpu.roll(high, 4, 0))
 
 
 def outer_rows(k):
@@ -122,12 +139,16 @@
     inside = jnp.where(core == 0, block > 0, block < lax.axis_size("xy") - 1)
 
     def window(f, l):
-        own = both[l // 8, f, l % 8, pl.ds(own_at, 16), :]
-        near = both[l // 8, f, l % 8, pl.ds(near_at, 8), :]
-        far = jnp.where(inside, halo[1 - core, f, l % 8], 0.0)
+        k = f * HALF + l % HALF if f < 2 else 2 * HALF + l % HALF // 2
+        own = both[l // HALF, k, pl.ds(own_at, 16), :]
+        near = both[l // HALF, k, pl.ds(near_at, 8), :]
+        far = jnp.where(inside, halo[1 - core, k], 0.0)
         if l >= HALF:
             far = pltpu.roll(far, 4, 0)
-        return jnp.concatenate([own, jnp.where(from_near, near, far)], axis=0)
+        tiles = [own[0:8], own[8:16], jnp.where(from_near, near, far)]
+        if f == 2 and l % 2 == 1:
+            tiles = [row_up(tile) for tile in tiles]
+        return jnp.concatenate(tiles, axis=0)
 
     for l in range(LEV):
         w = window(0, l)
@@ -438,12 +459,12 @@
     (mine,) = call(
         weigh_kernel,
         "weigh",
-        [(3,) + block],
-        [vmem(block, F32), vmem(block, F32), vmem(block, jnp.int32), pltpu.SemaphoreType.DMA((4,))],
+        [(PLANES, 32, LAN)],
+        [vmem(block, t) for t in (F32, F32, jnp.int32, F32)] + [pltpu.SemaphoreType.DMA((4,))],
         ends="first",
     )(source, conductivity, fluid, pressure)
     both = lax.all_gather(mine, "zk", axis=0, tiled=False)
-    (edge,) = call(edge_kernel, "edge", [(3, HALF, 8, LAN)])(both)
+    (edge,) = call(edge_kernel, "edge", [(PLANES, 8, LAN)])(both)
     halo = lax.all_gather(edge, AXES, axis=0, tiled=False, axis_index_groups=side_by_side())
     send, *fields = call(first_kernel, "first", [(4, SENT, LAN)] + [field] * 10)(both, halo)
     got = lax.all_to_all(send, "zc", 0, 0, tiled=False)

time: 34.9 us -> 34.6 us (level)
  no operation moved by 1% of the time
where the time goes in v10:
time: 34.6 us; the launch traced here: 34.5 us
  blocking collectives  30 us (87%)
  Pallas kernels  3.8 us (11%)
  between operations  0.65 us (2%)
    all_to_all x1, blocking collectives, shards(): got = lax.all_to_all(send, 'zc', 0, 0, tiled=False)  11.7 us
    all_gather x1, blocking collectives, shards(): ends = lax.all_gather(give, 'zk', axis=0, tiled=False)  10.6 us
    all_gather x1, blocking collectives, shards(): lax.all_gather(edge, AXES, axis=0, tiled=False, axis_index_groups=side_by...  5.13 us
    pallas_call x5, Pallas kernels, run(): pl.pallas_call(kernel, out_shape=[jax.ShapeDtypeStruct(s, F32) if plain e...  3.8 us
    all_gather x1, blocking collectives, shards(): both = lax.all_gather(mine, 'zk', axis=0, tiled=False)  2.58 us

profile of v10, /device:TPU:57, one launch (start us, length us, event | category | flops | bytes accessed | tf_op | source)
XLA Modules:
  0.0 34.5 jit_solution(17783345247545662864)
XLA Ops:
  0.6 1.2 %weigh.1 = f32[20,32,128]{2,1,0:T(8,128)S(1)} custom-call(f32[8,32,128]{2,1,0:T(8,128)} %source.1, f32[8,32,128]{2,1,0:T(8,128)} %cond.1, s32[8,32,128]{2,1,0:T(8,128)} %fluid.1, f32[8,32,128]{2,1,0:T(8,128)} %pressure.1), custom_call_target="tpu_custom_call" | custom-call | tf_op jit(solution)/shard_map/weigh/pallas_call | solution.py:427
  1.8 2.6 %all-gather = f32[40,32,128]{2,1,0:T(8,128)S(1)} all-gather(f32[20,32,128]{2,1,0:T(8,128)S(1)} %weigh.1), channel_id=2, replica_groups=mesh['zc'=4,'zk'=2,'xy'=64] {'zk'}, dimensions={0}, use_global_device_ids=true | all-gather | bytes 983040 | tf_op jit(solution)/shard_map/all_gather | solution.py:466
  4.4 5.1 %all-gather.1 = f32[40,8,128]{2,1,0:T(8,128)S(1)} all-gather(f32[20,8,128]{2,1,0:T(8,128)S(1)} %edge.1), channel_id=3, replica_groups={{1,64},{2,65},{3,66},{4,67},{5,68},{6,69},{7,70},{8,71},{9,72},{10,73},..., dimensions={0}, use_global_device_ids=true | all-gather | bytes 245760 | tf_op jit(solution)/shard_map/all_gather | solution.py:468
  9.5 0.8 %first.1 = (f32[4,344,128]{2,1,0:T(8,128)S(1)}, f32[16,24,128]{2,1,0:T(8,128)S(1)}, f32[16,24,128]{2,1,0:T(8,128)S(1)}, f32[16,24,128]{2,1,0:T(8,128)S(1)}, f32[...) custom-call(f32[2,20,32,128]{3,2,1,0:T(8,128)S(1)} %bitcast.4, ...), custom_call_target="tpu_custom_call" | custom-call | tf_op jit(solution)/shard_map/first/pallas_call | solution.py:427
  10.4 11.7 %all_to_all.5.got = f32[4,344,128]{2,1,0:T(8,128)S(1)} all-to-all(f32[4,344,128]{2,1,0:T(8,128)S(1)} %get-tuple-element.15), channel_id=1, replica_groups=mesh['zc'=4,'zk'=2,'xy'=64] {'zc'}, dimensions={0} | all-to-all | bytes 1409024 | tf_op jit(solution)/shard_map/all_to_all | solution.py:470
  22.1 1.1 %second.1 = (f32[12,16,128]{2,1,0:T(8,128)S(1)}, f32[12,16,128]{2,1,0:T(8,128)S(1)}) custom-call(f32[4,344,128]{2,1,0:T(8,128)S(1)} %all_to_all.5.got, f32[16,24,128]{2,1,0:T(8,128)S(1)} %get-tuple-element.16.ef, f32[16,24,128]{2,1,0:T(8,128)S(1)} %get-tuple-element.17.nf, f32[16,24,128]{2,1,0:T(8,128)S(1)} %get-tuple-element.18.vf, ...), custom_call_target="tpu_custom_call" | custom-call | tf_op jit(solution)/shard_map/second/pallas_call | solution.py:427
  23.2 10.6 %all-gather.2 = f32[24,16,128]{2,1,0:T(8,128)S(1)} all-gather(f32[12,16,128]{2,1,0:T(8,128)S(1)} %get-tuple-element.26), channel_id=4, replica_groups=mesh['zc'=4,'zk'=2,'xy'=64] {'zk'}, dimensions={0}, use_global_device_ids=true | all-gather | bytes 294912 | tf_op jit(solution)/shard_map/all_gather | solution.py:480
  33.8 0.7 %last.1 = (f32[8,32,128]{2,1,0:T(8,128)}, f32[4,16,64]{2,1,0:T(8,128)}) custom-call(f32[2,12,16,128]{3,2,1,0:T(8,128)S(1)} %bitcast.5, f32[12,16,128]{2,1,0:T(8,128)S(1)} %get-tuple-element.27.keep), custom_call_target="tpu_custom_call" | custom-call | tf_op jit(solution)/shard_map/last/pallas_call | solution.py:427
  (1 shorter events, 0.0 us)

commit v11 on v10

--- a/solution.py
+++ b/solution.py
@@ -380,14 +380,16 @@
             vert = vf[l] * full[l + 1] + vf[l + 1] * full[l + 3]
         applied = d * p - (horizontal(ef[l], nf[l], p) + vert)
         res[l + 1] = fr[l] - applied
-    weights = restriction_matrix()
     for big in range(LEV // 2):
         z = 2 * big
         s = 0.125 * (res[z] + 3.0 * res[z + 1] + 3.0 * res[z + 2] + res[z + 3])
         e = east_of(s)
-        s = 0.125 * (west_of(s) + 3.0 * s + 3.0 * e + east_of(e))
-        res[z] = jnp.dot(s, weights, precision=lax.Precision.HIGHEST, preferred_element_type=F32)
-        pair = res[z, pl.ds(0, 8, stride=2), :]
+        res[big] = 0.125 * (west_of(s) + 3.0 * s + 3.0 * e + east_of(e))
+    flat = res[0:8].reshape(8 * WIN, LAN)
+    flat = jnp.dot(flat, restriction_matrix(), precision=lax.Precision.HIGHEST, preferred_element_type=F32)
+    res[8:16] = flat.reshape(8, WIN, LAN)
+    for big in range(LEV // 2):
+        pair = res[8 + big, pl.ds(0, 8, stride=2), :]
         out[big // 4, HALF + big % 4] = jnp.concatenate([pair, pair], axis=0)
     core = lax.axis_index("zk")
     keep[...] = out[core]

time: 34.6 us -> 34.5 us (level)
  no operation moved by 1% of the time
where the time goes in v11:
time: 34.5 us; the launch traced here: 34.3 us
  blocking collectives  30 us (87%)
  Pallas kernels  3.61 us (10%)
  between operations  0.65 us (2%)
    all_to_all x1, blocking collectives, shards(): got = lax.all_to_all(send, 'zc', 0, 0, tiled=False)  11.7 us
    all_gather x1, blocking collectives, shards(): ends = lax.all_gather(give, 'zk', axis=0, tiled=False)  10.6 us
    all_gather x1, blocking collectives, shards(): lax.all_gather(edge, AXES, axis=0, tiled=False, axis_index_groups=side_by...  5.13 us
    pallas_call x5, Pallas kernels, run(): pl.pallas_call(kernel, out_shape=[jax.ShapeDtypeStruct(s, F32) if plain e...  3.61 us
    all_gather x1, blocking collectives, shards(): both = lax.all_gather(mine, 'zk', axis=0, tiled=False)  2.58 us

profile of v11, /device:TPU:57, one launch (start us, length us, event | category | flops | bytes accessed | tf_op | source)
XLA Modules:
  0.0 34.3 jit_solution(17237706627317260263)
XLA Ops:
  0.6 1.2 %weigh.1 = f32[20,32,128]{2,1,0:T(8,128)S(1)} custom-call(f32[8,32,128]{2,1,0:T(8,128)} %source.1, f32[8,32,128]{2,1,0:T(8,128)} %cond.1, s32[8,32,128]{2,1,0:T(8,128)} %fluid.1, f32[8,32,128]{2,1,0:T(8,128)} %pressure.1), custom_call_target="tpu_custom_call" | custom-call | tf_op jit(solution)/shard_map/weigh/pallas_call | solution.py:429
  1.8 2.6 %all-gather = f32[40,32,128]{2,1,0:T(8,128)S(1)} all-gather(f32[20,32,128]{2,1,0:T(8,128)S(1)} %weigh.1), channel_id=2, replica_groups=mesh['zc'=4,'zk'=2,'xy'=64] {'zk'}, dimensions={0}, use_global_device_ids=true | all-gather | bytes 983040 | tf_op jit(solution)/shard_map/all_gather | solution.py:468
  4.4 5.1 %all-gather.1 = f32[40,8,128]{2,1,0:T(8,128)S(1)} all-gather(f32[20,8,128]{2,1,0:T(8,128)S(1)} %edge.1), channel_id=3, replica_groups={{1,64},{2,65},{3,66},{4,67},{5,68},{6,69},{7,70},{8,71},{9,72},{10,73},..., dimensions={0}, use_global_device_ids=true | all-gather | bytes 245760 | tf_op jit(solution)/shard_map/all_gather | solution.py:470
  9.5 0.8 %first.1 = (f32[4,344,128]{2,1,0:T(8,128)S(1)}, f32[16,24,128]{2,1,0:T(8,128)S(1)}, f32[16,24,128]{2,1,0:T(8,128)S(1)}, f32[16,24,128]{2,1,0:T(8,128)S(1)}, f32[...) custom-call(f32[2,20,32,128]{3,2,1,0:T(8,128)S(1)} %bitcast.4, ...), custom_call_target="tpu_custom_call" | custom-call | tf_op jit(solution)/shard_map/first/pallas_call | solution.py:429
  10.4 11.7 %all_to_all.5.got = f32[4,344,128]{2,1,0:T(8,128)S(1)} all-to-all(f32[4,344,128]{2,1,0:T(8,128)S(1)} %get-tuple-element.15), channel_id=1, replica_groups=mesh['zc'=4,'zk'=2,'xy'=64] {'zc'}, dimensions={0} | all-to-all | bytes 1409024 | tf_op jit(solution)/shard_map/all_to_all | solution.py:472
  22.1 0.9 %second.1 = (f32[12,16,128]{2,1,0:T(8,128)S(1)}, f32[12,16,128]{2,1,0:T(8,128)S(1)}) custom-call(f32[4,344,128]{2,1,0:T(8,128)S(1)} %all_to_all.5.got, f32[16,24,128]{2,1,0:T(8,128)S(1)} %get-tuple-element.16.ef, f32[16,24,128]{2,1,0:T(8,128)S(1)} %get-tuple-element.17.nf, f32[16,24,128]{2,1,0:T(8,128)S(1)} %get-tuple-element.18.vf, ...), custom_call_target="tpu_custom_call" | custom-call | tf_op jit(solution)/shard_map/second/pallas_call | solution.py:429
  23.0 10.6 %all-gather.2 = f32[24,16,128]{2,1,0:T(8,128)S(1)} all-gather(f32[12,16,128]{2,1,0:T(8,128)S(1)} %get-tuple-element.26), channel_id=4, replica_groups=mesh['zc'=4,'zk'=2,'xy'=64] {'zk'}, dimensions={0}, use_global_device_ids=true | all-gather | bytes 294912 | tf_op jit(solution)/shard_map/all_gather | solution.py:482
  33.6 0.7 %last.1 = (f32[8,32,128]{2,1,0:T(8,128)}, f32[4,16,64]{2,1,0:T(8,128)}) custom-call(f32[2,12,16,128]{3,2,1,0:T(8,128)S(1)} %bitcast.5, f32[12,16,128]{2,1,0:T(8,128)S(1)} %get-tuple-element.27.keep), custom_call_target="tpu_custom_call" | custom-call | tf_op jit(solution)/shard_map/last/pallas_call | solution.py:429
  (1 shorter events, 0.0 us)

commit v12 on v11

--- a/solution.py
+++ b/solution.py
@@ -385,11 +385,10 @@
         s = 0.125 * (res[z] + 3.0 * res[z + 1] + 3.0 * res[z + 2] + res[z + 3])
         e = east_of(s)
         res[big] = 0.125 * (west_of(s) + 3.0 * s + 3.0 * e + east_of(e))
-    flat = res[0:8].reshape(8 * WIN, LAN)
+    flat = jnp.concatenate([res[big, pl.ds(0, 8, stride=2), :] for big in range(LEV // 2)], axis=0)
     flat = jnp.dot(flat, restriction_matrix(), precision=lax.Precision.HIGHEST, preferred_element_type=F32)
-    res[8:16] = flat.reshape(8, WIN, LAN)
     for big in range(LEV // 2):
-        pair = res[8 + big, pl.ds(0, 8, stride=2), :]
+        pair = flat[8 * big : 8 * big + 8]
         out[big // 4, HALF + big % 4] = jnp.concatenate([pair, pair], axis=0)
     core = lax.axis_index("zk")
     keep[...] = out[core]

time: 34.5 us -> 34.4 us (level)
  no operation moved by 1% of the time
where the time goes in v12:
time: 34.4 us; the launch traced here: 34.2 us
  blocking collectives  30 us (87%)
  Pallas kernels  3.56 us (10%)
  between operations  0.66 us (2%)
    all_to_all x1, blocking collectives, shards(): got = lax.all_to_all(send, 'zc', 0, 0, tiled=False)  11.7 us
    all_gather x1, blocking collectives, shards(): ends = lax.all_gather(give, 'zk', axis=0, tiled=False)  10.6 us
    all_gather x1, blocking collectives, shards(): lax.all_gather(edge, AXES, axis=0, tiled=False, axis_index_groups=side_by...  5.13 us
    pallas_call x5, Pallas kernels, run(): pl.pallas_call(kernel, out_shape=[jax.ShapeDtypeStruct(s, F32) if plain e...  3.56 us
    all_gather x1, blocking collectives, shards(): both = lax.all_gather(mine, 'zk', axis=0, tiled=False)  2.58 us

profile of v12, /device:TPU:57, one launch (start us, length us, event | category | flops | bytes accessed | tf_op | source)
XLA Modules:
  0.0 34.2 jit_solution(4194863422813097207)
XLA Ops:
  0.6 1.2 %weigh.1 = f32[20,32,128]{2,1,0:T(8,128)S(1)} custom-call(f32[8,32,128]{2,1,0:T(8,128)} %source.1, f32[8,32,128]{2,1,0:T(8,128)} %cond.1, s32[8,32,128]{2,1,0:T(8,128)} %fluid.1, f32[8,32,128]{2,1,0:T(8,128)} %pressure.1), custom_call_target="tpu_custom_call" | custom-call | tf_op jit(solution)/shard_map/weigh/pallas_call | solution.py:428
  1.8 2.6 %all-gather = f32[40,32,128]{2,1,0:T(8,128)S(1)} all-gather(f32[20,32,128]{2,1,0:T(8,128)S(1)} %weigh.1), channel_id=2, replica_groups=mesh['zc'=4,'zk'=2,'xy'=64] {'zk'}, dimensions={0}, use_global_device_ids=true | all-gather | bytes 983040 | tf_op jit(solution)/shard_map/all_gather | solution.py:467
  4.4 5.1 %all-gather.1 = f32[40,8,128]{2,1,0:T(8,128)S(1)} all-gather(f32[20,8,128]{2,1,0:T(8,128)S(1)} %edge.1), channel_id=3, replica_groups={{1,64},{2,65},{3,66},{4,67},{5,68},{6,69},{7,70},{8,71},{9,72},{10,73},..., dimensions={0}, use_global_device_ids=true | all-gather | bytes 245760 | tf_op jit(solution)/shard_map/all_gather | solution.py:469
  9.5 0.8 %first.1 = (f32[4,344,128]{2,1,0:T(8,128)S(1)}, f32[16,24,128]{2,1,0:T(8,128)S(1)}, f32[16,24,128]{2,1,0:T(8,128)S(1)}, f32[16,24,128]{2,1,0:T(8,128)S(1)}, f32[...) custom-call(f32[2,20,32,128]{3,2,1,0:T(8,128)S(1)} %bitcast.4, ...), custom_call_target="tpu_custom_call" | custom-call | tf_op jit(solution)/shard_map/first/pallas_call | solution.py:428
  10.4 11.7 %all_to_all.5.got = f32[4,344,128]{2,1,0:T(8,128)S(1)} all-to-all(f32[4,344,128]{2,1,0:T(8,128)S(1)} %get-tuple-element.15), channel_id=1, replica_groups=mesh['zc'=4,'zk'=2,'xy'=64] {'zc'}, dimensions={0} | all-to-all | bytes 1409024 | tf_op jit(solution)/shard_map/all_to_all | solution.py:471
  22.1 0.8 %second.1 = (f32[12,16,128]{2,1,0:T(8,128)S(1)}, f32[12,16,128]{2,1,0:T(8,128)S(1)}) custom-call(f32[4,344,128]{2,1,0:T(8,128)S(1)} %all_to_all.5.got, f32[16,24,128]{2,1,0:T(8,128)S(1)} %get-tuple-element.16.ef, f32[16,24,128]{2,1,0:T(8,128)S(1)} %get-tuple-element.17.nf, f32[16,24,128]{2,1,0:T(8,128)S(1)} %get-tuple-element.18.vf, ...), custom_call_target="tpu_custom_call" | custom-call | tf_op jit(solution)/shard_map/second/pallas_call | solution.py:428
  23.0 10.6 %all-gather.2 = f32[24,16,128]{2,1,0:T(8,128)S(1)} all-gather(f32[12,16,128]{2,1,0:T(8,128)S(1)} %get-tuple-element.26), channel_id=4, replica_groups=mesh['zc'=4,'zk'=2,'xy'=64] {'zk'}, dimensions={0}, use_global_device_ids=true | all-gather | bytes 294912 | tf_op jit(solution)/shard_map/all_gather | solution.py:481
  33.6 0.7 %last.1 = (f32[8,32,128]{2,1,0:T(8,128)}, f32[4,16,64]{2,1,0:T(8,128)}) custom-call(f32[2,12,16,128]{3,2,1,0:T(8,128)S(1)} %bitcast.5, f32[12,16,128]{2,1,0:T(8,128)S(1)} %get-tuple-element.27.keep), custom_call_target="tpu_custom_call" | custom-call | tf_op jit(solution)/shard_map/last/pallas_call | solution.py:428
  (1 shorter events, 0.0 us)
